TPU v7x, 32 devices: a whole 2x2x4 slice. The times are simulated.
32 devices in a mesh: groups: 2 (over y), seq: 4 (over z), exp: 4 (over x, core).
Axes of the slice: x: 2, y: 2, z: 4, core: 2. Of those that a mesh axis runs over, the one named last changes fastest.
Arguments:
- residual: bfloat16 [2048, 2048], P(('groups', 'seq', 'exp')), parts along dimension 0, may hold values from -6 to 6
- mixer_input: bfloat16 [2, 2048, 4096], P(None, ('groups', 'seq'), 'exp'), parts along dimension 1, may hold values from -6 to 6
- step_raw: bfloat16 [2048, 4096], P(('groups', 'seq'), 'exp'), parts along dimension 0, may hold values from -3 to 1
- state_maps: bfloat16 [2, 16, 2048], P(None, None, ('groups', 'seq')), parts along dimension 2, may hold values from -2 to 2
- decay_rate: float32 [16, 4096], P(None, 'exp'), may hold values from 9.765625e-05 to 0.04
- skip_gain: float32 [4096], P('exp'), may hold values from 0.5 to 1.5
- out_weight: bfloat16 [4096, 2048], P('exp', 'seq'), may hold values from -0.09375 to 0.09375
- norm_gain: float32 [2048], replicated, may hold values from 0.1 to 1.9
- router_weight: bfloat16 [2048, 4], replicated, may hold values from -0.125 to 0.125
- expert_ids: int32 [2048, 2], P(('groups', 'seq', 'exp')), parts along dimension 0, may hold values from 0 to 3, all different within a row; in each aligned block of 64 rows (0 to 63, 64 to 127, ...) at most 42 rows name the same one
- gate_weight: bfloat16 [4, 2048, 7168], P('exp', None, 'seq'), may hold values from -0.125 to 0.125
- up_weight: bfloat16 [4, 2048, 7168], P('exp', None, 'seq'), may hold values from -0.125 to 0.125
- down_weight: bfloat16 [4, 7168, 2048], P('exp', 'seq'), may hold values from -0.0625 to 0.0625
Outputs:
- layer_out: bfloat16 [2048, 2048], P(('groups', 'seq', 'exp')), parts along dimension 0
There are 2 independent parts, one for each index of `groups`. A program takes and returns all parts, laid end to end along the dimension named above; an argument that names none is the same for every part. Nothing has to cross between parts.
Inputs may be any that keep to these rules, and one draw needn't show every extreme that they name: `expert_ids`: each row names two different experts; within each aligned block of 64 rows (the rows of one device) no expert is named by more than 42 rows.
All inputs are finite; a program needn't handle non-finite values.
Results may differ from a plain program's by a relative error of at most 0.0061.
Values may be sent and summed in bfloat16 or wider, within the bound.
No kernel may reach another device: no remote copies, remote signals or barrier semaphores. Data moves between devices by JAX's collectives and lax.ppermute only.
A program may use at most 256 MiB of HBM per device.

v0:
```python
import functools

import jax
import jax.numpy as jnp
from jax import lax
from jax.experimental import pallas as pl
from jax.experimental.pallas import tpu as pltpu
from jax.sharding import PartitionSpec as P

LOG2E = 1.4426950408889634
f32 = jnp.float32
bf16 = jnp.bfloat16
VMEM = pl.BlockSpec(memory_space=pltpu.VMEM)
SMEM = pl.BlockSpec(memory_space=pltpu.SMEM)


def softplus(v):
    return jnp.maximum(v, 0.0) + jnp.log1p(jnp.exp(-jnp.abs(v)))


def ends_kernel(maps_ref, raw_ref, mixer_ref, dec_ref, pack_ref, step_ref, drive_ref):
    rows, channels = raw_ref.shape
    groups = channels // 128
    states = dec_ref.shape[0]
    half = rows // 2

    @pl.loop(0, rows // 16)
    def _(t):
        for g in range(groups):
            lanes = slice(g * 128, (g + 1) * 128)
            at = pl.ds(t * 16, 16)
            step = softplus(raw_ref[at, lanes].astype(f32))
            to = pl.ds(t * 16 * groups + g, 16, stride=groups)
            step_ref[to, :] = step
            drive_ref[to, :] = step * mixer_ref[0, at, lanes].astype(f32)

    def advance(p, carry):
        total, state = list(carry[0]), [list(v) for v in carry[1]]
        for b in range(2):
            pos = b * half + p
            step = step_ref[pl.ds(pos * groups, groups), :]
            drive = drive_ref[pl.ds(pos * groups, groups), :]
            total[b] = total[b] + step
            for n in range(states):
                decay = jnp.exp2(step * dec_ref[n])
                state[b][n] = decay * state[b][n] + drive * maps_ref[n, pos]
        return tuple(total), tuple(tuple(v) for v in state)

    zero = jnp.zeros((groups, 128), f32)
    total, state = lax.fori_loop(
        0, half, advance, ((zero,) * 2, ((zero,) * states,) * 2), unroll=4
    )
    per = 16 // groups
    for b in range(2):
        for n in range(0, states, per):
            values = jnp.concatenate(state[b][n : n + per], axis=0)
            pack_ref[b, pl.ds(n * groups, 16), :] = values.astype(bf16)
        high = total[b].astype(bf16)
        low = (total[b] - high.astype(f32)).astype(bf16)
        pack_ref[b, pl.ds(states * groups, groups), :] = high
        pack_ref[b, pl.ds((states + 1) * groups, groups), :] = low


def scan_kernel(count, place_ref, maps_ref, step_ref, drive_ref, dec_ref, mixer_ref, skip_ref, *rest):
    packs, (out_ref, all_ref, y_ref) = rest[:count], rest[count:]
    rows, channels = out_ref.shape
    groups = channels // 128
    states = dec_ref.shape[0]
    half = rows // 2
    place = place_ref[0]
    for k in range(count):
        all_ref[k] = packs[k][...].astype(f32)

    def fold(b, carry):
        running, first, second = carry
        opening = b < count
        owner = jnp.where(opening, b, 2 * count - 1 - b)
        slot = lax.rem(place - owner + count, count)
        side = jnp.where(opening, 0, 1)
        total = (
            all_ref[slot, side, pl.ds(states * groups, groups), :]
            + all_ref[slot, side, pl.ds((states + 1) * groups, groups), :]
        )
        first = [jnp.where(b == place, r, f) for r, f in zip(running, first)]
        second = [jnp.where(b == 2 * count - 1 - place, r, s) for r, s in zip(running, second)]
        running = [
            jnp.exp2(total * dec_ref[n]) * running[n]
            + all_ref[slot, side, pl.ds(n * groups, groups), :]
            for n in range(states)
        ]
        return running, first, second

    zeros = [all_ref[0, 0, pl.ds(0, groups), :] * 0.0] * states
    _, first, second = lax.fori_loop(0, 2 * count, fold, (zeros, zeros, zeros))

    def advance(p, state):
        state = [list(v) for v in state]
        for b in range(2):
            pos = b * half + p
            at = pl.ds(pos * groups, groups)
            step = step_ref[at, :]
            drive = drive_ref[at, :]
            parts = [None, None]
            for n in range(states):
                decay = jnp.exp2(step * dec_ref[n])
                state[b][n] = decay * state[b][n] + drive * maps_ref[n, pos]
                term = state[b][n] * maps_ref[states + n, pos]
                parts[n % 2] = term if parts[n % 2] is None else parts[n % 2] + term
            y_ref[at, :] = parts[0] + parts[1]
        return tuple(tuple(v) for v in state)

    lax.fori_loop(0, half, advance, (tuple(first), tuple(second)), unroll=4)

    @pl.loop(0, rows // 16)
    def _(t):
        for g in range(groups):
            lanes = slice(g * 128, (g + 1) * 128)
            at = pl.ds(t * 16, 16)
            y = y_ref[pl.ds(t * 16 * groups + g, 16, stride=groups), :]
            x = mixer_ref[0, at, lanes].astype(f32)
            z = mixer_ref[1, at, lanes].astype(f32)
            out_ref[at, lanes] = ((y + skip_ref[:, lanes] * x) * (z * jax.nn.sigmoid(z))).astype(bf16)


def shift(count, k):
    return [(i, (i + k) % count) for i in range(count)]


def mix(mixer_input, step_raw, state_maps, decay_rate, skip_gain):
    rows, channels = step_raw.shape
    groups = channels // 128
    states = decay_rate.shape[0]
    seq_count = lax.axis_size("seq")
    maps = state_maps.reshape(2 * states, rows).astype(f32)
    dec = (-LOG2E * decay_rate).reshape(states, groups, 128)
    shape = jax.ShapeDtypeStruct
    pack, step, drive = pl.pallas_call(
        ends_kernel,
        out_shape=(
            shape((2, (states + 2) * groups, 128), bf16),
            shape((rows * groups, 128), f32),
            shape((rows * groups, 128), f32),
        ),
        in_specs=[SMEM] + [VMEM] * 3,
        out_specs=(VMEM,) * 3,
        compiler_params=pltpu.CompilerParams(vmem_limit_bytes=24 << 20),
        name="ends",
    )(maps, step_raw, mixer_input, dec)
    packs = [pack] + [lax.ppermute(pack, "seq", shift(seq_count, k)) for k in range(1, seq_count)]
    place = lax.axis_index("seq").astype(jnp.int32).reshape(1)
    return pl.pallas_call(
        functools.partial(scan_kernel, seq_count),
        out_shape=shape((rows, channels), bf16),
        in_specs=[SMEM] * 2 + [VMEM] * (5 + seq_count),
        out_specs=VMEM,
        scratch_shapes=[
            pltpu.VMEM((seq_count, 2, (states + 2) * groups, 128), f32),
            pltpu.VMEM((rows * groups, 128), f32),
        ],
        compiler_params=pltpu.CompilerParams(vmem_limit_bytes=32 << 20),
        name="scan",
    )(place, maps, step, drive, dec, mixer_input, skip_gain[None, :], *packs)


def fetch_weight(out_weight):
    seq_count = lax.axis_size("seq")
    rows = out_weight.shape[0] // 2
    group = lax.axis_index("groups")
    mine = lax.dynamic_slice_in_dim(out_weight, group * rows, rows, 0)
    blocks = []
    for k in range(1, seq_count):
        direct = lax.ppermute(mine, "seq", shift(seq_count, k))
        other = lax.ppermute(direct, "groups", [(0, 1), (1, 0)])
        blocks.append((direct, other))
    return blocks


def project(mixed, out_weight, blocks):
    seq_count = lax.axis_size("seq")
    rows = out_weight.shape[0] // 2
    group = lax.axis_index("groups")
    near = lax.dynamic_slice_in_dim(mixed, group * rows, rows, 1)
    far = lax.dynamic_slice_in_dim(mixed, (1 - group) * rows, rows, 1)
    parts = [jnp.dot(mixed, out_weight, preferred_element_type=f32)]
    for direct, other in blocks:
        parts.append(
            jnp.dot(near, direct, preferred_element_type=f32)
            + jnp.dot(far, other, preferred_element_type=f32)
        )
    return parts


def own_order(parts, axis):
    count = len(parts)
    width = parts[0].shape[axis]
    ring = jnp.concatenate(parts[::-1] * 2, axis=axis)
    start = lax.rem(2 * count - 1 - lax.axis_index("seq"), count) * width
    return lax.dynamic_slice_in_dim(ring, start, count * width, axis)


def sum_to_owner(values):
    exp_count = lax.axis_size("exp")
    chips = exp_count // 2
    place = lax.axis_index("exp")
    chip, core = place // 2, place % 2
    rows = values.shape[0] // exp_count
    shaped = values.reshape(chips, 2, rows, values.shape[1])
    away = lax.dynamic_index_in_dim(shaped, 1 - core, 1, False)
    keep = lax.dynamic_index_in_dim(shaped, core, 1, False)
    pair = keep + lax.ppermute(away, "exp", [(i, i ^ 1) for i in range(exp_count)])
    total = lax.dynamic_index_in_dim(pair, chip, 0, False)
    for j in range(1, chips):
        leaving = lax.dynamic_index_in_dim(pair, (chip + j) % chips, 0, False).astype(bf16)
        total = total + lax.ppermute(leaving, "exp", shift(exp_count, 2 * j)).astype(f32)
    return total


def per_device(
    residual,
    mixer_input,
    step_raw,
    state_maps,
    decay_rate,
    skip_gain,
    out_weight,
    norm_gain,
    router_weight,
    expert_ids,
    gate_weight,
    up_weight,
    down_weight,
):
    blocks = fetch_weight(out_weight)
    mixed = mix(mixer_input, step_raw, state_maps, decay_rate, skip_gain)
    projected = own_order(project(mixed, out_weight, blocks), 1)
    summed = sum_to_owner(projected)
    stream_f = (residual.astype(jnp.float32) + summed).astype(jnp.bfloat16).astype(jnp.float32)
    mean_sq = jnp.mean(stream_f * stream_f, axis=-1, keepdims=True)
    normed = (stream_f * lax.rsqrt(mean_sq + 1e-05) * norm_gain[None, :]).astype(jnp.bfloat16)
    tok_rows = residual.shape[0]
    width = residual.shape[1]
    experts = router_weight.shape[1]
    picks = expert_ids.shape[1]
    capacity = max(2, 8 * tok_rows // (3 * experts))
    logits = jnp.dot(normed, router_weight, preferred_element_type=jnp.float32)
    onehot = (expert_ids[:, :, None] == jnp.arange(experts, dtype=jnp.int32)[None, None, :]).astype(
        jnp.float32
    )
    chosen = jnp.sum(onehot * logits[:, None, :], axis=-1)
    weights = jnp.stack(
        [jax.nn.sigmoid(chosen[:, 0] - chosen[:, 1]), jax.nn.sigmoid(chosen[:, 1] - chosen[:, 0])],
        axis=1,
    )
    flat_ids = expert_ids.reshape(-1)
    hot = (flat_ids[:, None] == jnp.arange(experts, dtype=jnp.int32)[None, :]).astype(jnp.int32)
    slot = jnp.sum((jnp.cumsum(hot, axis=0) - hot) * hot, axis=-1)
    target = flat_ids * capacity + slot
    select = (target[None, :] == jnp.arange(experts * capacity, dtype=jnp.int32)[:, None]).astype(
        jnp.bfloat16
    )
    normed_rep = jnp.repeat(normed, picks, axis=0)
    outgoing = jnp.dot(select, normed_rep, preferred_element_type=jnp.float32).astype(jnp.bfloat16)
    outgoing = outgoing.reshape(experts, capacity, width)
    gate_local = gate_weight[0]
    up_local = up_weight[0]
    down_local = down_weight[0]
    seq_count = lax.axis_size("seq")
    copies = jnp.broadcast_to(outgoing[None], (seq_count,) + outgoing.shape).reshape(
        (seq_count * experts,) + outgoing.shape[1:]
    )
    arrived = lax.all_to_all(copies, ("seq", "exp"), split_axis=0, concat_axis=0, tiled=True)
    flat = arrived.reshape(-1, arrived.shape[-1])
    gate = jnp.dot(flat, gate_local, preferred_element_type=jnp.float32)
    upper = jnp.dot(flat, up_local, preferred_element_type=jnp.float32)
    hidden = (jax.nn.silu(gate) * upper).astype(jnp.bfloat16)
    partial_value = (
        jnp.dot(hidden, down_local, preferred_element_type=jnp.float32)
        .reshape(arrived.shape)
        .astype(jnp.bfloat16)
    )
    back = lax.all_to_all(partial_value, ("seq", "exp"), split_axis=0, concat_axis=0, tiled=True)
    returned = jnp.sum(
        back.astype(jnp.float32).reshape((seq_count, experts) + outgoing.shape[1:]), axis=0
    ).astype(jnp.bfloat16)
    gathered = jnp.dot(
        select.T, returned.reshape(experts * capacity, width), preferred_element_type=jnp.float32
    )
    gathered = gathered.reshape(tok_rows, picks, width)
    result = stream_f + jnp.sum(weights[:, :, None] * gathered, axis=1)
    return result.astype(jnp.bfloat16)


def solution(mesh):
    in_specs = (
        P(("groups", "seq", "exp"), None),
        P(None, ("groups", "seq"), "exp"),
        P(("groups", "seq"), "exp"),
        P(None, None, ("groups", "seq")),
        P(None, "exp"),
        P("exp"),
        P("exp", "seq"),
        P(),
        P(),
        P(("groups", "seq", "exp"), None),
        P("exp", None, "seq"),
        P("exp", None, "seq"),
        P("exp", "seq", None),
    )
    out_specs = P(("groups", "seq", "exp"), None)
    return jax.shard_map(
        per_device, mesh=mesh, in_specs=in_specs, out_specs=out_specs, check_vma=False
    )
```

profile of v0, /device:TPU:11, one launch (start us, length us, event | category | flops | bytes accessed | tf_op | source)
XLA Modules:
  0.0 309.1 jit_solution(13967118926662165542)
XLA Ops:
  0.0 1.2 copy-done
  1.2 0.8 constant_dynamic-slice_fusion.1
  2.2 2.3 collective-permute-start.5
  4.5 2.2 collective-permute-start.7
  6.7 0.8 multiply_bitcast_fusion
  7.6 0.7 bitcast_convert_fusion.maps_ref
  8.3 1.2 copy-done.2
  9.5 1.0 copy-done.4
  10.6 5.7 %ends.1 = (bf16[2,144,128]{2,1,0:T(8,128)(2,1)S(1)}, f32[2048,128]{1,0:T(8,128)S(1)}, f32[2048,128]{1,0:T(8,128)S(1)}) custom-call(f32[32,256]{1,0:T(8,128)S(1)} %bitcast_convert_fusion.maps_ref, bf16[256,1024]{1,0:T(8,128)(2,1)S(1)} %copy-done.4, bf16[2,256,1024]{2,1,0:T(8,128)(2,1)S(1)} %copy-done.2, f32[16,8,128]{2,1,0:T(8,128)S(1)} %bitcast.56), custom_call_target="tpu_custom_call" | custom-call | tf_op jit(solution)/shard_map/ends/pallas_call | solution.py:137
  16.3 1.3 collective-permute-start.1
  17.7 36.5 %collective-permute-done.rest_1_ = bf16[2,144,128]{2,1,0:T(8,128)(2,1)S(1)} collective-permute-done((bf16[2,144,128]{2,1,0:T(8,128)(2,1)S(1)}, bf16[2,144,128]{2,1,0:T(8,128)(2,1)S(1)}, u32[]{:S(2)}, u32[]{:S(2)}) %collective-permute-start) | collective-permute-done | bytes 73760 | tf_op jit(solution)/shard_map/ppermute | solution.py:149
  54.2 1.6 collective-permute-done.1.rest_2_
  55.8 2.5 collective-permute-done.2.rest_3_
  58.2 1.2 copy-done.3
  59.5 0.7 copy-done.5
  60.1 7.5 %scan.1 = bf16[256,1024]{1,0:T(8,128)(2,1)S(1)} custom-call(s32[1]{0:T(128)} %bitcast.place_ref, f32[32,256]{1,0:T(8,128)S(1)} %bitcast_convert_fusion.maps_ref, f32[2048,128]{1,0:T(8,128)S(1)} %get-tuple-element.8.step_ref, f32[2048,128]{1,0:T(8,128)S(1)} %get-tuple-element.9.drive_ref, f32[16,8,128]{2,1,0:T(8,128)S(1)} %bitcast.57, ...), custom_call_target="tpu_custom_call" | custom-call | tf_op jit(solution)/shard_map/scan/pallas_call | solution.py:151
  67.7 1.3 collective-permute-start.4
  69.0 1.4 fusion.26
  70.7 1.2 collective-permute-start.8
  71.9 1.3 fusion.24
  73.3 1.3 fusion.22
  74.6 4.1 %collective-permute-done.4 = bf16[512,512]{1,0:T(8,128)(2,1)S(1)} collective-permute-done((bf16[512,512]{1,0:T(8,128)(2,1)}, bf16[512,512]{1,0:T(8,128)(2,1)S(1)}, u32[]{:S(2)}, u32[]{:S(2)}) %collective-permute-start.4) | collective-permute-done | bytes 524320 | tf_op jit(solution)/shard_map/ppermute | solution.py:173
  78.7 0.3 constant_dynamic-update-slice_fusion.7
  79.0 10.9 %collective-permute-done.6 = bf16[512,512]{1,0:T(8,128)(2,1)S(1)} collective-permute-done((bf16[512,512]{1,0:T(8,128)(2,1)}, bf16[512,512]{1,0:T(8,128)(2,1)S(1)}, u32[]{:S(2)}, u32[]{:S(2)}) %collective-permute-start.6) | collective-permute-done | bytes 524320 | tf_op jit(solution)/shard_map/ppermute | solution.py:173
  89.9 0.3 constant_dynamic-update-slice_fusion.6
  90.2 10.9 %collective-permute-done.8 = bf16[512,512]{1,0:T(8,128)(2,1)S(1)} collective-permute-done((bf16[512,512]{1,0:T(8,128)(2,1)}, bf16[512,512]{1,0:T(8,128)(2,1)S(1)}, u32[]{:S(2)}, u32[]{:S(2)}) %collective-permute-start.8) | collective-permute-done | bytes 524320 | tf_op jit(solution)/shard_map/ppermute | solution.py:173
  101.1 0.3 constant_dynamic-update-slice_fusion.5
  101.4 0.4 constant_dynamic-update-slice_fusion.4
  102.4 3.7 %collective-permute-start.9 = (f32[2,64,2048]{2,1,0:T(8,128)S(1)}, f32[2,64,2048]{2,1,0:T(8,128)}, u32[]{:S(2)}, u32[]{:S(2)}) collective-permute-start(f32[2,64,2048]{2,1,0:T(8,128)S(1)} %dynamic-slice_bitcast_fusion), channel_id=1, source_target_pairs={{0,1},{1,0},{2,3},{3,2},{4,5},{5,4},{6,7},{7,6},{8,9},{9,8},{10,11... | collective-permute-start | bytes 3145736 | tf_op jit(solution)/shard_map/ppermute | solution.py:210
  106.7 1.9 collective-permute-done.9
  108.6 1.3 bitcast_add_fusion
  109.9 0.3 collective-permute-start.10
  110.5 7.0 %collective-permute-done.10 = bf16[64,2048]{1,0:T(8,128)(2,1)S(1)} collective-permute-done((bf16[64,2048]{1,0:T(8,128)(2,1)S(1)}, bf16[64,2048]{1,0:T(8,128)(2,1)S(1)}, u32[]{:S(2)}, u32[]{:S(2)}) %collective-permute-start.10) | collective-permute-done | bytes 262176 | tf_op jit(solution)/shard_map/ppermute | solution.py:214
  117.7 0.7 copy-done.7
  118.6 0.3 broadcast_in_dim.9
  119.1 0.3 convolution_convert_fusion
  119.6 0.4 broadcast_in_dim.11
  120.0 75.7 %all_to_all.10 = bf16[16,42,2048]{2,1,0:T(8,128)(2,1)S(1)} all-to-all(bf16[16,42,2048]{2,1,0:T(8,128)(2,1)S(1)} %bitcast.59), channel_id=1, replica_groups=mesh['groups'=2,'seq'=4,'exp'=4] {'seq','exp'}, dimensions={0} | all-to-all | bytes 5505024 | tf_op jit(solution)/shard_map/all_to_all | solution.py:271
  195.7 2.3 reshape.89
  198.0 9.2 %fusion.4 = f32[672,1792]{1,0:T(8,128)S(1)} fusion(bf16[672,2048]{1,0:T(8,128)(2,1)} %reshape.89, bf16[1,2048,1792]{2,1,0:T(8,128)(2,1)} %param.23), kind=kOutput, calls=%fused_computation.4 | convolution fusion | flops 4932501504 | bytes 14909440 | tf_op jit(solution)/shard_map/dot_general | solution.py:273
  207.2 9.7 %multiply_convert_fusion = bf16[672,1792]{1,0:T(8,128)(2,1)} fusion(f32[672,1792]{1,0:T(8,128)S(1)} %fusion.4, bf16[672,2048]{1,0:T(8,128)(2,1)S(1)} %copy-done.6, bf16[1,2048,1792]{2,1,0:T(8,128)(2,1)} %param.24), kind=kOutput, calls=%fused_computation.6 | convolution fusion | flops 4939726848 | bytes 17317888 | tf_op jit(solution)/shard_map/dot_general | solution.py:274
  216.9 2.7 dot_general.52
  219.7 10.3 %fusion.8 = bf16[16,42,2048]{2,1,0:T(8,128)(2,1)} fusion(bf16[16,42,1792]{2,1,0:T(8,128)(2,1)S(1)} %dot_general.52, bf16[1,1792,2048]{2,1,0:T(8,128)(2,1)} %param.25), kind=kOutput, calls=%fused_computation.7 | convolution fusion | flops 4933877760 | bytes 12500992 | tf_op jit(solution)/shard_map/dot_general | solution.py:277
  230.0 5.2 %all-to-all-start.1 = ((bf16[16,42,2048]{2,1,0:T(8,128)(2,1)}), bf16[16,42,2048]{2,1,0:T(8,128)(2,1)}, u32[]{:S(2)}, u32[]{:S(2)}) async-start(bf16[16,42,2048]{2,1,0:T(8,128)(2,1)} %fusion.8), calls=%async_computation.1 | async-start | bytes 6291456 | tf_op jit(solution)/shard_map/all_to_all | solution.py:281
  235.7 69.5 %all-to-all-done.1 = bf16[16,42,2048]{2,1,0:T(8,128)(2,1)} async-done(((bf16[16,42,2048]{2,1,0:T(8,128)(2,1)}), bf16[16,42,2048]{2,1,0:T(8,128)(2,1)}, u32[]{:S(2)}, u32[]{:S(2)}) %all-to-all-start.1) | async-done | bytes 2752544 | tf_op jit(solution)/shard_map/all_to_all | solution.py:281
  305.2 2.6 reduce
  308.0 0.4 fusion.11
  308.4 0.8 fusion.15
  (58 shorter events, 3.2 us)
Async XLA Ops:
  0.0 1.2 copy-start
  2.1 65.6 %collective-permute-start.3 = (bf16[512,512]{1,0:T(8,128)(2,1)}, bf16[512,512]{1,0:T(8,128)(2,1)}, u32[]{:S(2)}, u32[]{:S(2)}) collective-permute-start(bf16[512,512]{1,0:T(8,128)(2,1)} %constant_dynamic-slice_fusion.1), channel_id=1, source_target_pairs={{0,12},{4,0},{8,4},{12,8},{1,13},{5,1},{9,5},{13,9},{2,14},{6,2},{... | collective-permute-start | bytes 1572872 | tf_op jit(solution)/shard_map/ppermute | solution.py:172
  2.2 68.1 %collective-permute-start.5 = (bf16[512,512]{1,0:T(8,128)(2,1)}, bf16[512,512]{1,0:T(8,128)(2,1)}, u32[]{:S(2)}, u32[]{:S(2)}) collective-permute-start(bf16[512,512]{1,0:T(8,128)(2,1)} %constant_dynamic-slice_fusion.1), channel_id=1, source_target_pairs={{0,8},{4,12},{8,0},{12,4},{1,9},{5,13},{9,1},{13,5},{2,10},{6,14},... | collective-permute-start | bytes 1572872 | tf_op jit(solution)/shard_map/ppermute | solution.py:172
  4.5 66.1 %collective-permute-start.7 = (bf16[512,512]{1,0:T(8,128)(2,1)}, bf16[512,512]{1,0:T(8,128)(2,1)}, u32[]{:S(2)}, u32[]{:S(2)}) collective-permute-start(bf16[512,512]{1,0:T(8,128)(2,1)} %constant_dynamic-slice_fusion.1), channel_id=1, source_target_pairs={{0,4},{4,8},{8,12},{12,0},{1,5},{5,9},{9,13},{13,1},{2,6},{6,10},{... | collective-permute-start | bytes 1572872 | tf_op jit(solution)/shard_map/ppermute | solution.py:172
  8.3 1.2 copy-start.2
  9.5 1.0 copy-start.4
  16.3 37.9 %collective-permute-start = (bf16[2,144,128]{2,1,0:T(8,128)(2,1)S(1)}, bf16[2,144,128]{2,1,0:T(8,128)(2,1)S(1)}, u32[]{:S(2)}, u32[]{:S(2)}) collective-permute-start(bf16[2,144,128]{2,1,0:T(8,128)(2,1)S(1)} %get-tuple-element.10.rest_0_), channel_id=1, source_target_pairs={{0,4},{4,8},{8,12},{12,0},{1,5},{5,9},{9,13},{13,1},{2,6},{6,10},{... | collective-permute-start | bytes 221192 | tf_op jit(solution)/shard_map/ppermute | solution.py:149
  16.3 39.4 %collective-permute-start.1 = (bf16[2,144,128]{2,1,0:T(8,128)(2,1)S(1)}, bf16[2,144,128]{2,1,0:T(8,128)(2,1)S(1)}, u32[]{:S(2)}, u32[]{:S(2)}) collective-permute-start(bf16[2,144,128]{2,1,0:T(8,128)(2,1)S(1)} %get-tuple-element.10.rest_0_), channel_id=1, source_target_pairs={{0,8},{4,12},{8,0},{12,4},{1,9},{5,13},{9,1},{13,5},{2,10},{6,14},... | collective-permute-start | bytes 221192 | tf_op jit(solution)/shard_map/ppermute | solution.py:149
  54.2 4.0 %collective-permute-start.2 = (bf16[2,144,128]{2,1,0:T(8,128)(2,1)S(1)}, bf16[2,144,128]{2,1,0:T(8,128)(2,1)S(1)}, u32[]{:S(2)}, u32[]{:S(2)}) collective-permute-start(bf16[2,144,128]{2,1,0:T(8,128)(2,1)S(1)} %get-tuple-element.10.rest_0_), channel_id=1, source_target_pairs={{0,12},{4,0},{8,4},{12,8},{1,13},{5,1},{9,5},{13,9},{2,14},{6,2},{... | collective-permute-start | bytes 221192 | tf_op jit(solution)/shard_map/ppermute | solution.py:149
  58.2 1.2 copy-start.3
  59.5 0.7 copy-start.5
  67.7 11.0 %collective-permute-start.4 = (bf16[512,512]{1,0:T(8,128)(2,1)}, bf16[512,512]{1,0:T(8,128)(2,1)S(1)}, u32[]{:S(2)}, u32[]{:S(2)}) collective-permute-start(bf16[512,512]{1,0:T(8,128)(2,1)} %collective-permute-done.3), channel_id=1, source_target_pairs={{0,16},{16,0},{1,17},{17,1},{2,18},{18,2},{3,19},{19,3},{4,20},{20... | collective-permute-start | bytes 1572872 | tf_op jit(solution)/shard_map/ppermute | solution.py:173
  70.4 19.5 %collective-permute-start.6 = (bf16[512,512]{1,0:T(8,128)(2,1)}, bf16[512,512]{1,0:T(8,128)(2,1)S(1)}, u32[]{:S(2)}, u32[]{:S(2)}) collective-permute-start(bf16[512,512]{1,0:T(8,128)(2,1)} %collective-permute-done.5), channel_id=1, source_target_pairs={{0,16},{16,0},{1,17},{17,1},{2,18},{18,2},{3,19},{19,3},{4,20},{20... | collective-permute-start | bytes 1572872 | tf_op jit(solution)/shard_map/ppermute | solution.py:173
  70.7 30.5 %collective-permute-start.8 = (bf16[512,512]{1,0:T(8,128)(2,1)}, bf16[512,512]{1,0:T(8,128)(2,1)S(1)}, u32[]{:S(2)}, u32[]{:S(2)}) collective-permute-start(bf16[512,512]{1,0:T(8,128)(2,1)} %collective-permute-done.7), channel_id=1, source_target_pairs={{0,16},{16,0},{1,17},{17,1},{2,18},{18,2},{3,19},{19,3},{4,20},{20... | collective-permute-start | bytes 1572872 | tf_op jit(solution)/shard_map/ppermute | solution.py:173
  102.0 4.2 %copy-start.11 = (s32[64,2]{0,1:T(2,128)S(1)}, s32[64,2]{0,1:T(2,128)}, u32[]{:S(2)}) copy-start(s32[64,2]{0,1:T(2,128)} %param.22) | copy-start | bytes 1540
  102.1 15.4 %copy-start.9 = (bf16[64,2048]{1,0:T(8,128)(2,1)S(1)}, bf16[64,2048]{1,0:T(8,128)(2,1)}, u32[]{:S(2)}) copy-start(bf16[64,2048]{1,0:T(8,128)(2,1)} %param.13) | copy-start | bytes 786436
  102.3 16.1 %copy-start.12 = (f32[2048]{0:T(1024)S(1)}, f32[2048]{0:T(1024)}, u32[]{:S(2)}) copy-start(f32[2048]{0:T(1024)} %param.20) | copy-start | bytes 24580
  102.4 6.1 %collective-permute-start.9 = (f32[2,64,2048]{2,1,0:T(8,128)S(1)}, f32[2,64,2048]{2,1,0:T(8,128)}, u32[]{:S(2)}, u32[]{:S(2)}) collective-permute-start(f32[2,64,2048]{2,1,0:T(8,128)S(1)} %dynamic-slice_bitcast_fusion), channel_id=1, source_target_pairs={{0,1},{1,0},{2,3},{3,2},{4,5},{5,4},{6,7},{7,6},{8,9},{9,8},{10,11... | collective-permute-start | bytes 3145736 | tf_op jit(solution)/shard_map/ppermute | solution.py:210
  109.9 7.6 %collective-permute-start.10 = (bf16[64,2048]{1,0:T(8,128)(2,1)S(1)}, bf16[64,2048]{1,0:T(8,128)(2,1)S(1)}, u32[]{:S(2)}, u32[]{:S(2)}) collective-permute-start(bf16[64,2048]{1,0:T(8,128)(2,1)S(1)} %fusion.18), channel_id=1, source_target_pairs={{0,2},{1,3},{2,0},{3,1},{4,6},{5,7},{6,4},{7,5},{8,10},{9,11},{10,... | collective-permute-start | bytes 786440 | tf_op jit(solution)/shard_map/ppermute | solution.py:214
  110.4 7.3 %copy-start.13 = (s32[128]{0:T(128)}, s32[128]{0:T(128)S(1)}, u32[]{:S(2)}) copy-start(s32[128]{0:T(128)S(1)} %select_reduce_fusion) | copy-start | bytes 1540
  117.7 0.7 copy-start.7
  198.0 9.2 %copy-start.6 = (bf16[672,2048]{1,0:T(8,128)(2,1)S(1)}, bf16[672,2048]{1,0:T(8,128)(2,1)}, u32[]{:S(2)}) copy-start(bf16[672,2048]{1,0:T(8,128)(2,1)} %reshape.89) | copy-start | bytes 8257540
  230.0 5.2 %copy-start.14 = (s32[128]{0:T(128)S(1)}, s32[128]{0:T(128)}, u32[]{:S(2)}) copy-start(s32[128]{0:T(128)} %copy-done.13) | copy-start | bytes 1540
  230.0 5.5 %copy-start.10 = (bf16[2048,4]{0,1:T(4,128)(2,1)S(1)}, bf16[2048,4]{0,1:T(4,128)(2,1)}, u32[]{:S(2)}) copy-start(bf16[2048,4]{0,1:T(4,128)(2,1)} %param.21) | copy-start | bytes 49156
  230.0 75.2 %all-to-all-start.1 = ((bf16[16,42,2048]{2,1,0:T(8,128)(2,1)}), bf16[16,42,2048]{2,1,0:T(8,128)(2,1)}, u32[]{:S(2)}, u32[]{:S(2)}) async-start(bf16[16,42,2048]{2,1,0:T(8,128)(2,1)} %fusion.8), calls=%async_computation.1 | async-start | bytes 6291456 | tf_op jit(solution)/shard_map/all_to_all | solution.py:281
  235.2 73.1 %copy-start.8 = (bf16[64,2048]{1,0:T(8,128)(2,1)S(1)}, bf16[64,2048]{1,0:T(8,128)(2,1)}, u32[]{:S(2)}) copy-start(bf16[64,2048]{1,0:T(8,128)(2,1)} %copy-done.7) | copy-start | bytes 786436
  235.2 73.9 %copy-start.1 = (bf16[1024,512]{1,0:T(8,128)(2,1)S(1)}, bf16[1024,512]{1,0:T(8,128)(2,1)}, u32[]{:S(2)}) copy-start(bf16[1024,512]{1,0:T(8,128)(2,1)} %param.19) | copy-start | bytes 3145732
where the time goes:
time: 310 us; the launch traced here: 309 us
  waiting for transfers between devices  145 us (47%)
  blocking collectives  75.7 us (24%)
  matrix products  35.5 us (11%)
  starting transfers between devices  18.2 us (6%)
  local copies, waits for them, and re-layouts  14.2 us (5%)
  Pallas kernels  13.2 us (4%)
  other arithmetic  7.06 us (2%)
    all_to_all x1, blocking collectives, per_device(): lax.all_to_all(copies, ('seq', 'exp'), split_axis=0, concat_axis=0, tiled...  75.7 us
    all_to_all x1, waiting for transfers between devices, per_device(): lax.all_to_all(partial_value, ('seq', 'exp'), split_axis=0, concat_axis=0...  69.5 us
    ppermute x3, waiting for transfers between devices, mix(): lax.ppermute(pack, 'seq', shift(seq_count, k))  40.6 us
    ppermute x3, waiting for transfers between devices, fetch_weight(): other = lax.ppermute(direct, 'groups', [(0, 1), (1, 0)])  25.9 us
    dot_general x1, matrix products, per_device(): jnp.dot(hidden, down_local, preferred_element_type=jnp.float32)  10.3 us
    dot_general x1, matrix products, per_device(): upper = jnp.dot(flat, up_local, preferred_element_type=jnp.float32)  9.7 us
    dot_general x1, matrix products, per_device(): gate = jnp.dot(flat, gate_local, preferred_element_type=jnp.float32)  9.19 us
    pallas_call x1, Pallas kernels, mix(): pl.pallas_call(functools.partial(scan_kernel, seq_count), out_shape=shape...  7.51 us
  transfers between devices with their start and end apart: 12, of which 9 were waited for; matrix products, arithmetic and copies ran while one was open for 2% of the time, Pallas kernels for 4%

commit v1 on v0

--- a/solution.py
+++ b/solution.py
@@ -215,6 +215,80 @@
     return total
 
 
+def pack_tokens(normed, router_weight, expert_ids):
+    rows = normed.shape[0]
+    experts = router_weight.shape[1]
+    logits = jnp.dot(normed, router_weight, preferred_element_type=f32)
+    lane = jnp.arange(experts, dtype=jnp.int32)[None, :]
+    first = expert_ids[:, 0:1] == lane
+    second = expert_ids[:, 1:2] == lane
+    gap = jnp.sum(jnp.where(first, logits, 0.0) - jnp.where(second, logits, 0.0), axis=1, keepdims=True)
+    weight = jnp.where(first, jax.nn.sigmoid(gap), 0.0) + jnp.where(second, jax.nn.sigmoid(-gap), 0.0)
+    routed = first | second
+    earlier = jnp.arange(rows)[:, None] > jnp.arange(rows)[None, :]
+    slot = jnp.dot(earlier.astype(bf16), routed.astype(bf16), preferred_element_type=f32)
+    high = weight.astype(bf16)
+    low = (weight - high.astype(f32)).astype(bf16)
+    slot = jnp.where(routed, slot + 1.0, 0.0).astype(bf16)
+    blank = jnp.zeros((rows, 128 - 3 * experts), bf16)
+    return jnp.concatenate([normed, high, low, slot, blank], axis=1)
+
+
+def expert_part(tokens, capacity, block_rows, experts, gate, up, down):
+    width = tokens.shape[1] - 128
+    count = tokens.shape[0] // block_rows
+    place = lax.axis_index("exp")
+    lane = jnp.arange(128, dtype=jnp.int32)[None, :]
+    slot = jnp.sum(jnp.where(lane == 2 * experts + place, tokens[:, width:].astype(f32), 0.0), axis=1)
+    block = jnp.arange(tokens.shape[0], dtype=jnp.int32) // block_rows
+    target = jnp.where(slot > 0.0, block * capacity + slot.astype(jnp.int32) - 1, -1)
+    chosen = (target[None, :] == jnp.arange(count * capacity, dtype=jnp.int32)[:, None]).astype(bf16)
+    held = jnp.dot(chosen, tokens, preferred_element_type=f32).astype(bf16)
+    mine = (lane == place) | (lane == experts + place)
+    weight = jnp.sum(jnp.where(mine, held[:, width:].astype(f32), 0.0), axis=1, keepdims=True)
+    rows = held[:, :width]
+    gated = jnp.dot(rows, gate, preferred_element_type=f32)
+    upper = jnp.dot(rows, up, preferred_element_type=f32)
+    hidden = (jax.nn.silu(gated) * upper).astype(bf16)
+    partial_value = jnp.dot(hidden, down, preferred_element_type=f32)
+    scaled = (partial_value * weight).astype(bf16)
+    return lax.dot_general(chosen, scaled, (((0,), (0,)), ((), ())), preferred_element_type=f32)
+
+
+def experts_sum(packed, experts, capacity, gate, up, down):
+    seq_count = lax.axis_size("seq")
+    exp_count = lax.axis_size("exp")
+    chips = exp_count // 2
+    rows = packed.shape[0]
+    width = packed.shape[1] - 128
+    partner = [(i, i ^ 1) for i in range(exp_count)]
+    order = [k for pair in zip(range(1, seq_count), range(seq_count - 1, 0, -1)) for k in pair]
+    order = list(dict.fromkeys(order))
+
+    planes = {0: packed}
+    for k in order:
+        planes[k] = lax.ppermute(packed, "seq", shift(seq_count, k))
+
+    total = None
+    for k in order[:-1] + [0] + order[-1:]:
+        row = [planes[k]]
+        for j in range(1, chips):
+            row.append(lax.ppermute(planes[k], "exp", shift(exp_count, 2 * j)))
+        row = jnp.concatenate(row, axis=0)
+        both = jnp.concatenate([row, lax.ppermute(row, "exp", partner)], axis=0)
+        part = expert_part(both, capacity, rows, experts, gate, up, down)
+        held = chips * rows
+        pair = part[:held] + lax.ppermute(part[held:].astype(bf16), "exp", partner).astype(f32)
+        mine = pair[:rows]
+        for j in range(1, chips):
+            leaving = pair[j * rows : (j + 1) * rows].astype(bf16)
+            mine = mine + lax.ppermute(leaving, "exp", shift(exp_count, exp_count - 2 * j)).astype(f32)
+        if k:
+            mine = lax.ppermute(mine.astype(bf16), "seq", shift(seq_count, seq_count - k)).astype(f32)
+        total = mine if total is None else total + mine
+    return total
+
+
 def per_device(
     residual,
     mixer_input,
@@ -238,56 +312,11 @@
     mean_sq = jnp.mean(stream_f * stream_f, axis=-1, keepdims=True)
     normed = (stream_f * lax.rsqrt(mean_sq + 1e-05) * norm_gain[None, :]).astype(jnp.bfloat16)
     tok_rows = residual.shape[0]
-    width = residual.shape[1]
     experts = router_weight.shape[1]
-    picks = expert_ids.shape[1]
     capacity = max(2, 8 * tok_rows // (3 * experts))
-    logits = jnp.dot(normed, router_weight, preferred_element_type=jnp.float32)
-    onehot = (expert_ids[:, :, None] == jnp.arange(experts, dtype=jnp.int32)[None, None, :]).astype(
-        jnp.float32
-    )
-    chosen = jnp.sum(onehot * logits[:, None, :], axis=-1)
-    weights = jnp.stack(
-        [jax.nn.sigmoid(chosen[:, 0] - chosen[:, 1]), jax.nn.sigmoid(chosen[:, 1] - chosen[:, 0])],
-        axis=1,
-    )
-    flat_ids = expert_ids.reshape(-1)
-    hot = (flat_ids[:, None] == jnp.arange(experts, dtype=jnp.int32)[None, :]).astype(jnp.int32)
-    slot = jnp.sum((jnp.cumsum(hot, axis=0) - hot) * hot, axis=-1)
-    target = flat_ids * capacity + slot
-    select = (target[None, :] == jnp.arange(experts * capacity, dtype=jnp.int32)[:, None]).astype(
-        jnp.bfloat16
-    )
-    normed_rep = jnp.repeat(normed, picks, axis=0)
-    outgoing = jnp.dot(select, normed_rep, preferred_element_type=jnp.float32).astype(jnp.bfloat16)
-    outgoing = outgoing.reshape(experts, capacity, width)
-    gate_local = gate_weight[0]
-    up_local = up_weight[0]
-    down_local = down_weight[0]
-    seq_count = lax.axis_size("seq")
-    copies = jnp.broadcast_to(outgoing[None], (seq_count,) + outgoing.shape).reshape(
-        (seq_count * experts,) + outgoing.shape[1:]
-    )
-    arrived = lax.all_to_all(copies, ("seq", "exp"), split_axis=0, concat_axis=0, tiled=True)
-    flat = arrived.reshape(-1, arrived.shape[-1])
-    gate = jnp.dot(flat, gate_local, preferred_element_type=jnp.float32)
-    upper = jnp.dot(flat, up_local, preferred_element_type=jnp.float32)
-    hidden = (jax.nn.silu(gate) * upper).astype(jnp.bfloat16)
-    partial_value = (
-        jnp.dot(hidden, down_local, preferred_element_type=jnp.float32)
-        .reshape(arrived.shape)
-        .astype(jnp.bfloat16)
-    )
-    back = lax.all_to_all(partial_value, ("seq", "exp"), split_axis=0, concat_axis=0, tiled=True)
-    returned = jnp.sum(
-        back.astype(jnp.float32).reshape((seq_count, experts) + outgoing.shape[1:]), axis=0
-    ).astype(jnp.bfloat16)
-    gathered = jnp.dot(
-        select.T, returned.reshape(experts * capacity, width), preferred_element_type=jnp.float32
-    )
-    gathered = gathered.reshape(tok_rows, picks, width)
-    result = stream_f + jnp.sum(weights[:, :, None] * gathered, axis=1)
-    return result.astype(jnp.bfloat16)
+    packed = pack_tokens(normed, router_weight, expert_ids)
+    added = experts_sum(packed, experts, capacity, gate_weight[0], up_weight[0], down_weight[0])
+    return (stream_f + added).astype(jnp.bfloat16)
 
 
 def solution(mesh):

time: 310 us -> 262 us (0.85); the launches traced: 309 us -> 258 us
  blocking collectives: 75.7 us -> 0 us
  matrix products: 35.5 us -> 59.1 us
  waiting for transfers between devices: 145 us -> 126 us
  starting transfers between devices: 18.2 us -> 35.5 us
    all_to_all x1 -> x0, blocking collectives: 75.7 us -> none  [per_device(): lax.all_to_all(copies, ('seq', 'exp'), split_axis=0, concat_axis=0, tiled...]
    all_to_all x1 -> x0, waiting for transfers between devices: 69.5 us -> none  [per_device(): lax.all_to_all(partial_value, ('seq', 'exp'), split_axis=0, concat_axis=0...]
    ppermute x0 -> x22, waiting for transfers between devices: none -> 49.9 us  [the longest x4 16.6 us: experts_sum(): lax.ppermute(leaving, 'exp', shift(exp_count, exp_count - 2 * j))]
    dot_general x6 -> x18, matrix products: 30.1 us -> 53.6 us  [the longest x4 24.1 us: expert_part(): lax.dot_general(chosen, scaled, (((0,), (0,)), ((), ())), preferred_eleme...]
    ppermute x0 -> x22, starting transfers between devices: none -> 22.6 us  [the longest x4 11 us: experts_sum(): both = jnp.concatenate([row, lax.ppermute(row, 'exp', partner)], axis=0)]
    slice x0 -> x8, local copies, waits for them, and re-layouts: none -> 6.45 us  [the longest x4 6.33 us: experts_sum(): part[held:].astype(bf16)]
    all_to_all x1 -> x0, starting transfers between devices: 5.22 us -> none  [per_device(): lax.all_to_all(partial_value, ('seq', 'exp'), split_axis=0, concat_axis=0...]
    add x2 -> x4, other arithmetic: 0.01 us -> 3.78 us  [experts_sum(): part[:held]]
  transfers between devices with their start and end apart: 12 -> 33, of which waited for: 9 -> 19; matrix products, arithmetic and copies ran while one was open for 2% -> 20% of each run, Pallas kernels for 4% -> 5%
where the time goes in v1:
time: 262 us; the launch traced here: 258 us
  waiting for transfers between devices  126 us (48%)
  matrix products  59.1 us (23%)
  starting transfers between devices  35.5 us (14%)
  local copies, waits for them, and re-layouts  13.9 us (5%)
  Pallas kernels  13.2 us (5%)
  other arithmetic  9.55 us (4%)
    ppermute x3, waiting for transfers between devices, mix(): lax.ppermute(pack, 'seq', shift(seq_count, k))  40.8 us
    ppermute x3, waiting for transfers between devices, fetch_weight(): other = lax.ppermute(direct, 'groups', [(0, 1), (1, 0)])  25.9 us
    dot_general x4, matrix products, expert_part(): lax.dot_general(chosen, scaled, (((0,), (0,)), ((), ())), preferred_eleme...  24.1 us
    dot_general x4, matrix products, expert_part(): upper = jnp.dot(rows, up, preferred_element_type=f32)  18.7 us
    ppermute x4, waiting for transfers between devices, experts_sum(): lax.ppermute(leaving, 'exp', shift(exp_count, exp_count - 2 * j))  16.6 us
    ppermute x3, waiting for transfers between devices, experts_sum(): planes[k] = lax.ppermute(packed, 'seq', shift(seq_count, k))  15.4 us
    ppermute x4, starting transfers between devices, experts_sum(): both = jnp.concatenate([row, lax.ppermute(row, 'exp', partner)], axis=0)  11 us
    dot_general x4, matrix products, expert_part(): gated = jnp.dot(rows, gate, preferred_element_type=f32)  9.07 us
  transfers between devices with their start and end apart: 33, of which 19 were waited for; matrix products, arithmetic and copies ran while one was open for 20% of the time, Pallas kernels for 5%

profile of v1, /device:TPU:11, one launch (start us, length us, event | category | flops | bytes accessed | tf_op | source)
XLA Modules:
  0.0 257.8 jit_solution(14509243943428307279)
XLA Ops:
  2.2 2.3 collective-permute-start.5
  4.5 2.2 collective-permute-start.7
  9.4 5.7 %ends.1 = (bf16[2,144,128]{2,1,0:T(8,128)(2,1)S(1)}, f32[2048,128]{1,0:T(8,128)S(1)}, f32[2048,128]{1,0:T(8,128)S(1)}) custom-call(f32[32,256]{1,0:T(8,128)S(1)} %bitcast_convert_fusion.maps_ref, bf16[256,1024]{1,0:T(8,128)(2,1)S(1)} %copy-done.5, bf16[2,256,1024]{2,1,0:T(8,128)(2,1)S(1)} %copy-done.2, f32[16,8,128]{2,1,0:T(8,128)S(1)} %bitcast.110), custom_call_target="tpu_custom_call" | custom-call | tf_op jit(solution)/shard_map/ends/pallas_call | solution.py:137
  16.1 1.3 collective-permute-start.1
  17.4 36.8 %collective-permute-done.rest_1_ = bf16[2,144,128]{2,1,0:T(8,128)(2,1)S(1)} collective-permute-done((bf16[2,144,128]{2,1,0:T(8,128)(2,1)S(1)}, bf16[2,144,128]{2,1,0:T(8,128)(2,1)S(1)}, u32[]{:S(2)}, u32[]{:S(2)}) %collective-permute-start) | collective-permute-done | bytes 73760 | tf_op jit(solution)/shard_map/ppermute | solution.py:149
  54.2 1.6 collective-permute-done.1.rest_2_
  55.8 2.5 collective-permute-done.2.rest_3_
  59.5 7.5 %scan.1 = bf16[256,1024]{1,0:T(8,128)(2,1)S(1)} custom-call(s32[1]{0:T(128)} %bitcast.place_ref, f32[32,256]{1,0:T(8,128)S(1)} %bitcast_convert_fusion.maps_ref, f32[2048,128]{1,0:T(8,128)S(1)} %get-tuple-element.8.step_ref, f32[2048,128]{1,0:T(8,128)S(1)} %copy-done.4, f32[16,8,128]{2,1,0:T(8,128)S(1)} %bitcast.111, bf16[2,256,1024]{2,1,0:T(8,128)(2,1)S(1)} %copy-done.2, ...), custom_call_target="tpu_custom_call" | custom-call | tf_op jit(solution)/shard_map/scan/pallas_call | solution.py:151
  68.3 1.4 fusion.122
  71.2 1.3 fusion.120
  72.6 1.3 fusion.118
  73.9 4.1 %collective-permute-done.4 = bf16[512,512]{1,0:T(8,128)(2,1)S(1)} collective-permute-done((bf16[512,512]{1,0:T(8,128)(2,1)}, bf16[512,512]{1,0:T(8,128)(2,1)S(1)}, u32[]{:S(2)}, u32[]{:S(2)}) %collective-permute-start.4) | collective-permute-done | bytes 524320 | tf_op jit(solution)/shard_map/ppermute | solution.py:173
  78.3 10.9 %collective-permute-done.6 = bf16[512,512]{1,0:T(8,128)(2,1)S(1)} collective-permute-done((bf16[512,512]{1,0:T(8,128)(2,1)}, bf16[512,512]{1,0:T(8,128)(2,1)S(1)}, u32[]{:S(2)}, u32[]{:S(2)}) %collective-permute-start.6) | collective-permute-done | bytes 524320 | tf_op jit(solution)/shard_map/ppermute | solution.py:173
  89.5 10.9 %collective-permute-done.8 = bf16[512,512]{1,0:T(8,128)(2,1)S(1)} collective-permute-done((bf16[512,512]{1,0:T(8,128)(2,1)}, bf16[512,512]{1,0:T(8,128)(2,1)S(1)}, u32[]{:S(2)}, u32[]{:S(2)}) %collective-permute-start.8) | collective-permute-done | bytes 524320 | tf_op jit(solution)/shard_map/ppermute | solution.py:173
  101.7 3.7 %collective-permute-start.9 = (f32[2,64,2048]{2,1,0:T(8,128)S(1)}, f32[2,64,2048]{2,1,0:T(8,128)}, u32[]{:S(2)}, u32[]{:S(2)}) collective-permute-start(f32[2,64,2048]{2,1,0:T(8,128)S(1)} %dynamic-slice_bitcast_fusion), channel_id=1, source_target_pairs={{0,1},{1,0},{2,3},{3,2},{4,5},{5,4},{6,7},{7,6},{8,9},{9,8},{10,11... | collective-permute-start | bytes 3145736 | tf_op jit(solution)/shard_map/ppermute | solution.py:210
  105.4 2.4 collective-permute-done.9
  107.8 1.3 bitcast_add_fusion
  109.8 7.0 %collective-permute-done.10 = bf16[64,2048]{1,0:T(8,128)(2,1)S(1)} collective-permute-done((bf16[64,2048]{1,0:T(8,128)(2,1)S(1)}, bf16[64,2048]{1,0:T(8,128)(2,1)S(1)}, u32[]{:S(2)}, u32[]{:S(2)}) %collective-permute-start.10) | collective-permute-done | bytes 262176 | tf_op jit(solution)/shard_map/ppermute | solution.py:214
  120.0 1.7 collective-permute-start.17
  121.7 4.1 %collective-permute-done.23 = bf16[64,2176]{1,0:T(8,128)(2,1)S(1)} collective-permute-done((bf16[64,2176]{1,0:T(8,128)(2,1)S(1)}, bf16[64,2176]{1,0:T(8,128)(2,1)S(1)}, u32[]{:S(2)}, u32[]{:S(2)}) %collective-permute-start.23) | collective-permute-done | bytes 278560 | tf_op jit(solution)/shard_map/ppermute | solution.py:276
  125.8 2.1 collective-permute-start.24
  128.0 8.9 %collective-permute-done.27 = bf16[64,2176]{1,0:T(8,128)(2,1)S(1)} collective-permute-done((bf16[64,2176]{1,0:T(8,128)(2,1)S(1)}, bf16[64,2176]{1,0:T(8,128)(2,1)S(1)}, u32[]{:S(2)}, u32[]{:S(2)}) %collective-permute-start.27) | collective-permute-done | bytes 278560 | tf_op jit(solution)/shard_map/ppermute | solution.py:270
  138.1 6.5 %collective-permute-done.17 = bf16[64,2176]{1,0:T(8,128)(2,1)S(1)} collective-permute-done((bf16[64,2176]{1,0:T(8,128)(2,1)S(1)}, bf16[64,2176]{1,0:T(8,128)(2,1)S(1)}, u32[]{:S(2)}, u32[]{:S(2)}) %collective-permute-start.17) | collective-permute-done | bytes 278560 | tf_op jit(solution)/shard_map/ppermute | solution.py:270
  146.2 2.1 collective-permute-start.29
  148.3 3.0 %collective-permute-done.18 = bf16[64,2176]{1,0:T(8,128)(2,1)S(1)} collective-permute-done((bf16[64,2176]{1,0:T(8,128)(2,1)S(1)}, bf16[64,2176]{1,0:T(8,128)(2,1)S(1)}, u32[]{:S(2)}, u32[]{:S(2)}) %collective-permute-start.18) | collective-permute-done | bytes 278560 | tf_op jit(solution)/shard_map/ppermute | solution.py:276
  151.4 4.3 %collective-permute-start.19 = (bf16[128,2176]{1,0:T(8,128)(2,1)S(1)}, bf16[128,2176]{1,0:T(8,128)(2,1)S(1)}, u32[]{:S(2)}, u32[]{:S(2)}) collective-permute-start(bf16[128,2176]{1,0:T(8,128)(2,1)S(1)} %pad_maximum_fusion.1), channel_id=1, source_target_pairs={{0,1},{1,0},{2,3},{3,2},{4,5},{5,4},{6,7},{7,6},{8,9},{9,8},{10,11... | collective-permute-start | bytes 1671176 | tf_op jit(solution)/shard_map/ppermute | solution.py:278
  155.7 1.6 collective-permute-done.12
  157.3 2.4 collective-permute-start.13
  162.8 1.5 fusion.22
  164.2 2.5 fusion.20
  166.8 2.5 fusion.16
  169.7 2.6 fusion.18
  173.2 2.4 fusion.57
  175.6 5.0 %fusion.73 = f32[256,2048]{1,0:T(8,128)S(1)} fusion(bf16[168,1792]{1,0:T(8,128)(2,1)} %fusion.57, bf16[1,1792,2048]{2,1,0:T(8,128)(2,1)} %param.25, f32[168]{0:T(256)S(1)} %get-tuple-element.11, s32[256]{0:T(256)S(1)} %get-tuple-element.38), kind=kOutput, calls=%fused_computation.44 | convolution fusion | flops 1410017280 | bytes 10040992 | tf_op jit(solution)/shard_map/dot_general | solution.py:255
  181.8 5.6 %fusion.54 = bf16[168,1792]{1,0:T(8,128)(2,1)} fusion(bf16[1,2048,1792]{2,1,0:T(8,128)(2,1)} %param.24, f32[168,1792]{1,0:T(8,128)} %fusion.20, bf16[168,2176]{1,0:T(8,128)(2,1)S(1)} %copy-done.13), kind=kOutput, calls=%fused_computation.38 | convolution fusion | flops 1234931712 | bytes 9834496 | tf_op jit(solution)/shard_map/dot_general | solution.py:251
  187.5 6.6 %fusion.76 = f32[256,2048]{1,0:T(8,128)} fusion(bf16[168,1792]{1,0:T(8,128)(2,1)} %fusion.54, bf16[1,1792,2048]{2,1,0:T(8,128)(2,1)} %param.25, f32[168]{0:T(256)S(1)} %get-tuple-element.12, s32[256]{0:T(256)S(1)} %get-tuple-element.37), kind=kOutput, calls=%fused_computation.45 | convolution fusion | flops 1410017280 | bytes 10040992 | tf_op jit(solution)/shard_map/dot_general | solution.py:255
  194.1 2.1 slice.210
  196.4 5.6 %fusion.48 = bf16[168,1792]{1,0:T(8,128)(2,1)} fusion(bf16[1,2048,1792]{2,1,0:T(8,128)(2,1)} %param.24, f32[168,1792]{1,0:T(8,128)} %fusion.16, bf16[168,2176]{1,0:T(8,128)(2,1)S(1)} %copy-done.11), kind=kOutput, calls=%fused_computation.36 | convolution fusion | flops 1234931712 | bytes 9834496 | tf_op jit(solution)/shard_map/dot_general | solution.py:251
  202.0 6.3 %fusion.82 = f32[256,2048]{1,0:T(8,128)} fusion(bf16[168,1792]{1,0:T(8,128)(2,1)} %fusion.48, bf16[1,1792,2048]{2,1,0:T(8,128)(2,1)} %param.25, f32[168]{0:T(256)S(1)} %get-tuple-element.14, s32[256]{0:T(256)S(1)} %get-tuple-element.35), kind=kOutput, calls=%fused_computation.47 | convolution fusion | flops 1410017280 | bytes 10040992 | tf_op jit(solution)/shard_map/dot_general | solution.py:255
  208.3 2.1 slice.208
  210.8 5.0 %fusion.51 = bf16[168,1792]{1,0:T(8,128)(2,1)S(1)} fusion(bf16[1,2048,1792]{2,1,0:T(8,128)(2,1)} %param.24, f32[168,1792]{1,0:T(8,128)} %fusion.18, bf16[168,2176]{1,0:T(8,128)(2,1)} %copy-done.15), kind=kOutput, calls=%fused_computation.37 | convolution fusion | flops 1234931712 | bytes 9834496 | tf_op jit(solution)/shard_map/dot_general | solution.py:251
  215.8 6.1 %fusion.79 = f32[256,2048]{1,0:T(8,128)} fusion(bf16[168,1792]{1,0:T(8,128)(2,1)S(1)} %fusion.51, bf16[1,1792,2048]{2,1,0:T(8,128)(2,1)} %param.25, f32[168]{0:T(256)S(1)} %get-tuple-element.13, s32[256]{0:T(256)S(1)} %get-tuple-element.36), kind=kOutput, calls=%fused_computation.46 | convolution fusion | flops 1410017280 | bytes 10040992 | tf_op jit(solution)/shard_map/dot_general | solution.py:255
  230.8 1.4 collective-permute-done.15
  232.3 5.5 %collective-permute-done.21 = bf16[64,2048]{1,0:T(8,128)(2,1)S(1)} collective-permute-done((bf16[64,2048]{1,0:T(8,128)(2,1)S(1)}, bf16[64,2048]{1,0:T(8,128)(2,1)S(1)}, u32[]{:S(2)}, u32[]{:S(2)}) %collective-permute-start.21) | collective-permute-done | bytes 262176 | tf_op jit(solution)/shard_map/ppermute | solution.py:285
  237.9 5.5 %collective-permute-done.31 = bf16[64,2048]{1,0:T(8,128)(2,1)S(1)} collective-permute-done((bf16[64,2048]{1,0:T(8,128)(2,1)S(1)}, bf16[64,2048]{1,0:T(8,128)(2,1)S(1)}, u32[]{:S(2)}, u32[]{:S(2)}) %collective-permute-start.31) | collective-permute-done | bytes 262176 | tf_op jit(solution)/shard_map/ppermute | solution.py:285
  243.5 1.4 collective-permute-start.32
  244.9 4.2 %collective-permute-done.26 = bf16[64,2048]{1,0:T(8,128)(2,1)S(1)} collective-permute-done((bf16[64,2048]{1,0:T(8,128)(2,1)S(1)}, bf16[64,2048]{1,0:T(8,128)(2,1)S(1)}, u32[]{:S(2)}, u32[]{:S(2)}) %collective-permute-start.26) | collective-permute-done | bytes 262176 | tf_op jit(solution)/shard_map/ppermute | solution.py:285
  249.1 7.9 %collective-permute-done.32 = bf16[64,2048]{1,0:T(8,128)(2,1)S(1)} collective-permute-done((bf16[64,2048]{1,0:T(8,128)(2,1)S(1)}, bf16[64,2048]{1,0:T(8,128)(2,1)S(1)}, u32[]{:S(2)}, u32[]{:S(2)}) %collective-permute-start.32) | collective-permute-done | bytes 262176 | tf_op jit(solution)/shard_map/ppermute | solution.py:287
  (149 shorter events, 34.3 us)
Async XLA Ops:
  0.0 8.3 %copy-start.2 = (bf16[2,256,1024]{2,1,0:T(8,128)(2,1)S(1)}, bf16[2,256,1024]{2,1,0:T(8,128)(2,1)}, u32[]{:S(2)}) copy-start(bf16[2,256,1024]{2,1,0:T(8,128)(2,1)} %mixer_ref.3) | copy-start | bytes 3145732
  1.2 57.0 %copy-start.6 = (f32[1024]{0:T(1024)S(1)}, f32[1024]{0:T(1024)}, u32[]{:S(2)}) copy-start(f32[1024]{0:T(1024)} %param.18) | copy-start | bytes 12292
  2.1 64.9 %collective-permute-start.3 = (bf16[512,512]{1,0:T(8,128)(2,1)}, bf16[512,512]{1,0:T(8,128)(2,1)}, u32[]{:S(2)}, u32[]{:S(2)}) collective-permute-start(bf16[512,512]{1,0:T(8,128)(2,1)} %constant_dynamic-slice_fusion.1), channel_id=1, source_target_pairs={{0,12},{4,0},{8,4},{12,8},{1,13},{5,1},{9,5},{13,9},{2,14},{6,2},{... | collective-permute-start | bytes 1572872 | tf_op jit(solution)/shard_map/ppermute | solution.py:172
  2.2 67.5 %collective-permute-start.5 = (bf16[512,512]{1,0:T(8,128)(2,1)}, bf16[512,512]{1,0:T(8,128)(2,1)}, u32[]{:S(2)}, u32[]{:S(2)}) collective-permute-start(bf16[512,512]{1,0:T(8,128)(2,1)} %constant_dynamic-slice_fusion.1), channel_id=1, source_target_pairs={{0,8},{4,12},{8,0},{12,4},{1,9},{5,13},{9,1},{13,5},{2,10},{6,14},... | collective-permute-start | bytes 1572872 | tf_op jit(solution)/shard_map/ppermute | solution.py:172
  4.5 65.5 %collective-permute-start.7 = (bf16[512,512]{1,0:T(8,128)(2,1)}, bf16[512,512]{1,0:T(8,128)(2,1)}, u32[]{:S(2)}, u32[]{:S(2)}) collective-permute-start(bf16[512,512]{1,0:T(8,128)(2,1)} %constant_dynamic-slice_fusion.1), channel_id=1, source_target_pairs={{0,4},{4,8},{8,12},{12,0},{1,5},{5,9},{9,13},{13,1},{2,6},{6,10},{... | collective-permute-start | bytes 1572872 | tf_op jit(solution)/shard_map/ppermute | solution.py:172
  16.1 38.1 %collective-permute-start = (bf16[2,144,128]{2,1,0:T(8,128)(2,1)S(1)}, bf16[2,144,128]{2,1,0:T(8,128)(2,1)S(1)}, u32[]{:S(2)}, u32[]{:S(2)}) collective-permute-start(bf16[2,144,128]{2,1,0:T(8,128)(2,1)S(1)} %get-tuple-element.10.rest_0_), channel_id=1, source_target_pairs={{0,4},{4,8},{8,12},{12,0},{1,5},{5,9},{9,13},{13,1},{2,6},{6,10},{... | collective-permute-start | bytes 221192 | tf_op jit(solution)/shard_map/ppermute | solution.py:149
  16.1 39.7 %collective-permute-start.1 = (bf16[2,144,128]{2,1,0:T(8,128)(2,1)S(1)}, bf16[2,144,128]{2,1,0:T(8,128)(2,1)S(1)}, u32[]{:S(2)}, u32[]{:S(2)}) collective-permute-start(bf16[2,144,128]{2,1,0:T(8,128)(2,1)S(1)} %get-tuple-element.10.rest_0_), channel_id=1, source_target_pairs={{0,8},{4,12},{8,0},{12,4},{1,9},{5,13},{9,1},{13,5},{2,10},{6,14},... | collective-permute-start | bytes 221192 | tf_op jit(solution)/shard_map/ppermute | solution.py:149
  54.2 4.0 %collective-permute-start.2 = (bf16[2,144,128]{2,1,0:T(8,128)(2,1)S(1)}, bf16[2,144,128]{2,1,0:T(8,128)(2,1)S(1)}, u32[]{:S(2)}, u32[]{:S(2)}) collective-permute-start(bf16[2,144,128]{2,1,0:T(8,128)(2,1)S(1)} %get-tuple-element.10.rest_0_), channel_id=1, source_target_pairs={{0,12},{4,0},{8,4},{12,8},{1,13},{5,1},{9,5},{13,9},{2,14},{6,2},{... | collective-permute-start | bytes 221192 | tf_op jit(solution)/shard_map/ppermute | solution.py:149
  67.0 11.0 %collective-permute-start.4 = (bf16[512,512]{1,0:T(8,128)(2,1)}, bf16[512,512]{1,0:T(8,128)(2,1)S(1)}, u32[]{:S(2)}, u32[]{:S(2)}) collective-permute-start(bf16[512,512]{1,0:T(8,128)(2,1)} %collective-permute-done.3), channel_id=1, source_target_pairs={{0,16},{16,0},{1,17},{17,1},{2,18},{18,2},{3,19},{19,3},{4,20},{20... | collective-permute-start | bytes 1572872 | tf_op jit(solution)/shard_map/ppermute | solution.py:173
  69.7 19.5 %collective-permute-start.6 = (bf16[512,512]{1,0:T(8,128)(2,1)}, bf16[512,512]{1,0:T(8,128)(2,1)S(1)}, u32[]{:S(2)}, u32[]{:S(2)}) collective-permute-start(bf16[512,512]{1,0:T(8,128)(2,1)} %collective-permute-done.5), channel_id=1, source_target_pairs={{0,16},{16,0},{1,17},{17,1},{2,18},{18,2},{3,19},{19,3},{4,20},{20... | collective-permute-start | bytes 1572872 | tf_op jit(solution)/shard_map/ppermute | solution.py:173
  70.0 30.5 %collective-permute-start.8 = (bf16[512,512]{1,0:T(8,128)(2,1)}, bf16[512,512]{1,0:T(8,128)(2,1)S(1)}, u32[]{:S(2)}, u32[]{:S(2)}) collective-permute-start(bf16[512,512]{1,0:T(8,128)(2,1)} %collective-permute-done.7), channel_id=1, source_target_pairs={{0,16},{16,0},{1,17},{17,1},{2,18},{18,2},{3,19},{19,3},{4,20},{20... | collective-permute-start | bytes 1572872 | tf_op jit(solution)/shard_map/ppermute | solution.py:173
  101.7 6.1 %collective-permute-start.9 = (f32[2,64,2048]{2,1,0:T(8,128)S(1)}, f32[2,64,2048]{2,1,0:T(8,128)}, u32[]{:S(2)}, u32[]{:S(2)}) collective-permute-start(f32[2,64,2048]{2,1,0:T(8,128)S(1)} %dynamic-slice_bitcast_fusion), channel_id=1, source_target_pairs={{0,1},{1,0},{2,3},{3,2},{4,5},{5,4},{6,7},{7,6},{8,9},{9,8},{10,11... | collective-permute-start | bytes 3145736 | tf_op jit(solution)/shard_map/ppermute | solution.py:210
  105.4 4.1 %copy-start.16 = (s32[64,2]{0,1:T(2,128)S(1)}, s32[64,2]{0,1:T(2,128)}, u32[]{:S(2)}) copy-start(s32[64,2]{0,1:T(2,128)} %param.22) | copy-start | bytes 1540
  109.2 8.8 %copy-start.14 = (f32[2048]{0:T(1024)S(1)}, f32[2048]{0:T(1024)}, u32[]{:S(2)}) copy-start(f32[2048]{0:T(1024)} %param.20) | copy-start | bytes 24580
  109.2 8.9 %copy-start.17 = (bf16[2048,4]{0,1:T(4,128)(2,1)S(1)}, bf16[2048,4]{0,1:T(4,128)(2,1)}, u32[]{:S(2)}) copy-start(bf16[2048,4]{0,1:T(4,128)(2,1)} %param.21) | copy-start | bytes 49156
  109.2 7.6 %collective-permute-start.10 = (bf16[64,2048]{1,0:T(8,128)(2,1)S(1)}, bf16[64,2048]{1,0:T(8,128)(2,1)S(1)}, u32[]{:S(2)}, u32[]{:S(2)}) collective-permute-start(bf16[64,2048]{1,0:T(8,128)(2,1)S(1)} %fusion.114), channel_id=1, source_target_pairs={{0,2},{1,3},{2,0},{3,1},{4,6},{5,7},{6,4},{7,5},{8,10},{9,11},{10,... | collective-permute-start | bytes 786440 | tf_op jit(solution)/shard_map/ppermute | solution.py:214
  118.7 7.1 %collective-permute-start.23 = (bf16[64,2176]{1,0:T(8,128)(2,1)S(1)}, bf16[64,2176]{1,0:T(8,128)(2,1)S(1)}, u32[]{:S(2)}, u32[]{:S(2)}) collective-permute-start(bf16[64,2176]{1,0:T(8,128)(2,1)S(1)} %concatenate.35), channel_id=1, source_target_pairs={{0,2},{1,3},{2,0},{3,1},{4,6},{5,7},{6,4},{7,5},{8,10},{9,11},{10,... | collective-permute-start | bytes 835592 | tf_op jit(solution)/shard_map/ppermute | solution.py:276
  119.1 17.8 %collective-permute-start.27 = (bf16[64,2176]{1,0:T(8,128)(2,1)S(1)}, bf16[64,2176]{1,0:T(8,128)(2,1)S(1)}, u32[]{:S(2)}, u32[]{:S(2)}) collective-permute-start(bf16[64,2176]{1,0:T(8,128)(2,1)S(1)} %concatenate.35), channel_id=1, source_target_pairs={{0,8},{4,12},{8,0},{12,4},{1,9},{5,13},{9,1},{13,5},{2,10},{6,14},... | collective-permute-start | bytes 835592 | tf_op jit(solution)/shard_map/ppermute | solution.py:270
  120.0 24.6 %collective-permute-start.17 = (bf16[64,2176]{1,0:T(8,128)(2,1)S(1)}, bf16[64,2176]{1,0:T(8,128)(2,1)S(1)}, u32[]{:S(2)}, u32[]{:S(2)}) collective-permute-start(bf16[64,2176]{1,0:T(8,128)(2,1)S(1)} %concatenate.35), channel_id=1, source_target_pairs={{0,12},{4,0},{8,4},{12,8},{1,13},{5,1},{9,5},{13,9},{2,14},{6,2},{... | collective-permute-start | bytes 835592 | tf_op jit(solution)/shard_map/ppermute | solution.py:270
  121.7 24.1 %collective-permute-start.11 = (bf16[64,2176]{1,0:T(8,128)(2,1)S(1)}, bf16[64,2176]{1,0:T(8,128)(2,1)S(1)}, u32[]{:S(2)}, u32[]{:S(2)}) collective-permute-start(bf16[64,2176]{1,0:T(8,128)(2,1)S(1)} %concatenate.35), channel_id=1, source_target_pairs={{0,4},{4,8},{8,12},{12,0},{1,5},{5,9},{9,13},{13,1},{2,6},{6,10},{... | collective-permute-start | bytes 835592 | tf_op jit(solution)/shard_map/ppermute | solution.py:270
  125.8 35.6 %collective-permute-start.24 = (bf16[128,2176]{1,0:T(8,128)(2,1)S(1)}, bf16[128,2176]{1,0:T(8,128)(2,1)S(1)}, u32[]{:S(2)}, u32[]{:S(2)}) collective-permute-start(bf16[128,2176]{1,0:T(8,128)(2,1)S(1)} %pad_maximum_fusion.2), channel_id=1, source_target_pairs={{0,1},{1,0},{2,3},{3,2},{4,5},{5,4},{6,7},{7,6},{8,9},{9,8},{10,11... | collective-permute-start | bytes 1671176 | tf_op jit(solution)/shard_map/ppermute | solution.py:278
  136.9 9.3 %collective-permute-start.28 = (bf16[64,2176]{1,0:T(8,128)(2,1)S(1)}, bf16[64,2176]{1,0:T(8,128)(2,1)S(1)}, u32[]{:S(2)}, u32[]{:S(2)}) collective-permute-start(bf16[64,2176]{1,0:T(8,128)(2,1)S(1)} %collective-permute-done.27), channel_id=1, source_target_pairs={{0,2},{1,3},{2,0},{3,1},{4,6},{5,7},{6,4},{7,5},{8,10},{9,11},{10,... | collective-permute-start | bytes 835592 | tf_op jit(solution)/shard_map/ppermute | solution.py:276
  144.6 6.7 %collective-permute-start.18 = (bf16[64,2176]{1,0:T(8,128)(2,1)S(1)}, bf16[64,2176]{1,0:T(8,128)(2,1)S(1)}, u32[]{:S(2)}, u32[]{:S(2)}) collective-permute-start(bf16[64,2176]{1,0:T(8,128)(2,1)S(1)} %collective-permute-done.17), channel_id=1, source_target_pairs={{0,2},{1,3},{2,0},{3,1},{4,6},{5,7},{6,4},{7,5},{8,10},{9,11},{10,... | collective-permute-start | bytes 835592 | tf_op jit(solution)/shard_map/ppermute | solution.py:276
  145.8 11.5 %collective-permute-start.12 = (bf16[64,2176]{1,0:T(8,128)(2,1)S(1)}, bf16[64,2176]{1,0:T(8,128)(2,1)S(1)}, u32[]{:S(2)}, u32[]{:S(2)}) collective-permute-start(bf16[64,2176]{1,0:T(8,128)(2,1)S(1)} %collective-permute-done.11), channel_id=1, source_target_pairs={{0,2},{1,3},{2,0},{3,1},{4,6},{5,7},{6,4},{7,5},{8,10},{9,11},{10,... | collective-permute-start | bytes 835592 | tf_op jit(solution)/shard_map/ppermute | solution.py:276
  146.2 13.6 %collective-permute-start.29 = (bf16[128,2176]{1,0:T(8,128)(2,1)S(1)}, bf16[128,2176]{1,0:T(8,128)(2,1)S(1)}, u32[]{:S(2)}, u32[]{:S(2)}) collective-permute-start(bf16[128,2176]{1,0:T(8,128)(2,1)S(1)} %pad_maximum_fusion.3), channel_id=1, source_target_pairs={{0,1},{1,0},{2,3},{3,2},{4,5},{5,4},{6,7},{7,6},{8,9},{9,8},{10,11... | collective-permute-start | bytes 1671176 | tf_op jit(solution)/shard_map/ppermute | solution.py:278
  151.3 11.4 %slice-start = ((s8[7340032]{0:T(1024)(128)(4,1)}), s8[4194304]{0:T(1024)(128)(4,1)S(1)}, s32[]{:S(2)}) async-start(s8[7340032]{0:T(1024)(128)(4,1)} %bitcast.115), calls=%async_computation | async-start | bytes 8388608
  151.4 8.5 %collective-permute-start.19 = (bf16[128,2176]{1,0:T(8,128)(2,1)S(1)}, bf16[128,2176]{1,0:T(8,128)(2,1)S(1)}, u32[]{:S(2)}, u32[]{:S(2)}) collective-permute-start(bf16[128,2176]{1,0:T(8,128)(2,1)S(1)} %pad_maximum_fusion.1), channel_id=1, source_target_pairs={{0,1},{1,0},{2,3},{3,2},{4,5},{5,4},{6,7},{7,6},{8,9},{9,8},{10,11... | collective-permute-start | bytes 1671176 | tf_op jit(solution)/shard_map/ppermute | solution.py:278
  157.3 4.0 %collective-permute-start.13 = (bf16[128,2176]{1,0:T(8,128)(2,1)S(1)}, bf16[128,2176]{1,0:T(8,128)(2,1)S(1)}, u32[]{:S(2)}, u32[]{:S(2)}) collective-permute-start(bf16[128,2176]{1,0:T(8,128)(2,1)S(1)} %pad_maximum_fusion), channel_id=1, source_target_pairs={{0,1},{1,0},{2,3},{3,2},{4,5},{5,4},{6,7},{7,6},{8,9},{9,8},{10,11... | collective-permute-start | bytes 1671176 | tf_op jit(solution)/shard_map/ppermute | solution.py:278
  162.3 9.9 %copy-start.10 = (bf16[168,2176]{1,0:T(8,128)(2,1)}, bf16[168,2176]{1,0:T(8,128)(2,1)S(1)}, u32[]{:S(2)}) copy-start(bf16[168,2176]{1,0:T(8,128)(2,1)S(1)} %convolution_convert_fusion) | copy-start | bytes 2193412
  162.7 9.5 %copy-start.12 = (bf16[168,2176]{1,0:T(8,128)(2,1)}, bf16[168,2176]{1,0:T(8,128)(2,1)S(1)}, u32[]{:S(2)}) copy-start(bf16[168,2176]{1,0:T(8,128)(2,1)S(1)} %convolution_convert_fusion.2) | copy-start | bytes 2193412
  169.3 3.1 %slice-start.2 = ((s8[7340032]{0:T(1024)(128)(4,1)}), s8[4194304]{0:T(1024)(128)(4,1)S(1)}, s32[]{:S(2)}) async-start(s8[7340032]{0:T(1024)(128)(4,1)} %bitcast.117), calls=%async_computation.2 | async-start | bytes 8388608
  169.7 3.5 %slice-start.3 = ((s8[7340032]{0:T(1024)(128)(4,1)}), s8[3145728]{0:T(1024)(128)(4,1)S(1)}, s32[]{:S(2)}) async-start(s8[7340032]{0:T(1024)(128)(4,1)} %bitcast.117), calls=%async_computation.3 | async-start | bytes 6291456
  175.5 6.3 %copy-start.13 = (bf16[168,2176]{1,0:T(8,128)(2,1)S(1)}, bf16[168,2176]{1,0:T(8,128)(2,1)}, u32[]{:S(2)}) copy-start(bf16[168,2176]{1,0:T(8,128)(2,1)} %copy-done.12) | copy-start | bytes 2193412
  181.4 42.0 %collective-permute-start.14 = (bf16[128,2048]{1,0:T(8,128)(2,1)}, bf16[128,2048]{1,0:T(8,128)(2,1)}, u32[]{:S(2)}, u32[]{:S(2)}) collective-permute-start(bf16[128,2048]{1,0:T(8,128)(2,1)} %slice.211), channel_id=1, source_target_pairs={{0,1},{1,0},{2,3},{3,2},{4,5},{5,4},{6,7},{7,6},{8,9},{9,8},{10,11... | collective-permute-start | bytes 1572872 | tf_op jit(solution)/shard_map/ppermute | solution.py:281
  187.5 8.9 %copy-start.11 = (bf16[168,2176]{1,0:T(8,128)(2,1)S(1)}, bf16[168,2176]{1,0:T(8,128)(2,1)}, u32[]{:S(2)}) copy-start(bf16[168,2176]{1,0:T(8,128)(2,1)} %copy-done.10) | copy-start | bytes 2193412
  196.2 29.8 %collective-permute-start.20 = (bf16[128,2048]{1,0:T(8,128)(2,1)}, bf16[128,2048]{1,0:T(8,128)(2,1)}, u32[]{:S(2)}, u32[]{:S(2)}) collective-permute-start(bf16[128,2048]{1,0:T(8,128)(2,1)} %slice.210), channel_id=1, source_target_pairs={{0,1},{1,0},{2,3},{3,2},{4,5},{5,4},{6,7},{7,6},{8,9},{9,8},{10,11... | collective-permute-start | bytes 1572872 | tf_op jit(solution)/shard_map/ppermute | solution.py:281
  210.4 17.3 %collective-permute-start.30 = (bf16[128,2048]{1,0:T(8,128)(2,1)}, bf16[128,2048]{1,0:T(8,128)(2,1)}, u32[]{:S(2)}, u32[]{:S(2)}) collective-permute-start(bf16[128,2048]{1,0:T(8,128)(2,1)} %slice.208), channel_id=1, source_target_pairs={{0,1},{1,0},{2,3},{3,2},{4,5},{5,4},{6,7},{7,6},{8,9},{9,8},{10,11... | collective-permute-start | bytes 1572872 | tf_op jit(solution)/shard_map/ppermute | solution.py:281
  223.2 6.8 %collective-permute-start.25 = (bf16[128,2048]{1,0:T(8,128)(2,1)S(1)}, bf16[128,2048]{1,0:T(8,128)(2,1)S(1)}, u32[]{:S(2)}, u32[]{:S(2)}) collective-permute-start(bf16[128,2048]{1,0:T(8,128)(2,1)S(1)} %slice.209), channel_id=1, source_target_pairs={{0,1},{1,0},{2,3},{3,2},{4,5},{5,4},{6,7},{7,6},{8,9},{9,8},{10,11... | collective-permute-start | bytes 1572872 | tf_op jit(solution)/shard_map/ppermute | solution.py:281
  224.7 3.0 %copy-start.8 = (f32[256,2048]{1,0:T(8,128)S(1)}, f32[256,2048]{1,0:T(8,128)}, u32[]{:S(2)}) copy-start(f32[256,2048]{1,0:T(8,128)} %fusion.82) | copy-start | bytes 6291460
  224.7 7.5 %collective-permute-start.15 = (bf16[64,2048]{1,0:T(8,128)(2,1)S(1)}, bf16[64,2048]{1,0:T(8,128)(2,1)S(1)}, u32[]{:S(2)}, u32[]{:S(2)}) collective-permute-start(bf16[64,2048]{1,0:T(8,128)(2,1)S(1)} %slice.215), channel_id=1, source_target_pairs={{0,2},{1,3},{2,0},{3,1},{4,6},{5,7},{6,4},{7,5},{8,10},{9,11},{10,... | collective-permute-start | bytes 786440 | tf_op jit(solution)/shard_map/ppermute | solution.py:285
  227.2 2.8 %copy-start.9 = (f32[256,2048]{1,0:T(8,128)S(1)}, f32[256,2048]{1,0:T(8,128)}, u32[]{:S(2)}) copy-start(f32[256,2048]{1,0:T(8,128)} %fusion.79) | copy-start | bytes 6291460
  227.2 10.6 %collective-permute-start.21 = (bf16[64,2048]{1,0:T(8,128)(2,1)S(1)}, bf16[64,2048]{1,0:T(8,128)(2,1)S(1)}, u32[]{:S(2)}, u32[]{:S(2)}) collective-permute-start(bf16[64,2048]{1,0:T(8,128)(2,1)S(1)} %slice.214), channel_id=1, source_target_pairs={{0,2},{1,3},{2,0},{3,1},{4,6},{5,7},{6,4},{7,5},{8,10},{9,11},{10,... | collective-permute-start | bytes 786440 | tf_op jit(solution)/shard_map/ppermute | solution.py:285
  229.0 14.4 %collective-permute-start.31 = (bf16[64,2048]{1,0:T(8,128)(2,1)S(1)}, bf16[64,2048]{1,0:T(8,128)(2,1)S(1)}, u32[]{:S(2)}, u32[]{:S(2)}) collective-permute-start(bf16[64,2048]{1,0:T(8,128)(2,1)S(1)} %slice.212), channel_id=1, source_target_pairs={{0,2},{1,3},{2,0},{3,1},{4,6},{5,7},{6,4},{7,5},{8,10},{9,11},{10,... | collective-permute-start | bytes 786440 | tf_op jit(solution)/shard_map/ppermute | solution.py:285
  230.2 18.9 %collective-permute-start.26 = (bf16[64,2048]{1,0:T(8,128)(2,1)S(1)}, bf16[64,2048]{1,0:T(8,128)(2,1)S(1)}, u32[]{:S(2)}, u32[]{:S(2)}) collective-permute-start(bf16[64,2048]{1,0:T(8,128)(2,1)S(1)} %slice.213), channel_id=1, source_target_pairs={{0,2},{1,3},{2,0},{3,1},{4,6},{5,7},{6,4},{7,5},{8,10},{9,11},{10,... | collective-permute-start | bytes 786440 | tf_op jit(solution)/shard_map/ppermute | solution.py:285
  232.3 16.8 %collective-permute-start.16 = (bf16[64,2048]{1,0:T(8,128)(2,1)S(1)}, bf16[64,2048]{1,0:T(8,128)(2,1)S(1)}, u32[]{:S(2)}, u32[]{:S(2)}) collective-permute-start(bf16[64,2048]{1,0:T(8,128)(2,1)S(1)} %fusion.111), channel_id=1, source_target_pairs={{0,12},{4,0},{8,4},{12,8},{1,13},{5,1},{9,5},{13,9},{2,14},{6,2},{... | collective-permute-start | bytes 786440 | tf_op jit(solution)/shard_map/ppermute | solution.py:287
  237.8 20.0 %copy-start.1 = (bf16[1024,512]{1,0:T(8,128)(2,1)S(1)}, bf16[1024,512]{1,0:T(8,128)(2,1)}, u32[]{:S(2)}) copy-start(bf16[1024,512]{1,0:T(8,128)(2,1)} %param.19) | copy-start | bytes 3145732
  237.9 11.2 %collective-permute-start.22 = (bf16[64,2048]{1,0:T(8,128)(2,1)S(1)}, bf16[64,2048]{1,0:T(8,128)(2,1)S(1)}, u32[]{:S(2)}, u32[]{:S(2)}) collective-permute-start(bf16[64,2048]{1,0:T(8,128)(2,1)S(1)} %fusion.110), channel_id=1, source_target_pairs={{0,4},{4,8},{8,12},{12,0},{1,5},{5,9},{9,13},{13,1},{2,6},{6,10},{... | collective-permute-start | bytes 786440 | tf_op jit(solution)/shard_map/ppermute | solution.py:287
  243.5 13.4 %collective-permute-start.32 = (bf16[64,2048]{1,0:T(8,128)(2,1)S(1)}, bf16[64,2048]{1,0:T(8,128)(2,1)S(1)}, u32[]{:S(2)}, u32[]{:S(2)}) collective-permute-start(bf16[64,2048]{1,0:T(8,128)(2,1)S(1)} %fusion.107), channel_id=1, source_target_pairs={{0,8},{4,12},{8,0},{12,4},{1,9},{5,13},{9,1},{13,5},{2,10},{6,14},... | collective-permute-start | bytes 786440 | tf_op jit(solution)/shard_map/ppermute | solution.py:287
  (7 other events, 12.6 us)

commit v2 on v1

v2 whole, which is shorter than its diff:
```python
import functools

import jax
import jax.numpy as jnp
from jax import lax
from jax.experimental import pallas as pl
from jax.experimental.pallas import tpu as pltpu
from jax.sharding import PartitionSpec as P

LOG2E = 1.4426950408889634
f32 = jnp.float32
bf16 = jnp.bfloat16
VMEM_EXPERT = 16
VMEM = pl.BlockSpec(memory_space=pltpu.VMEM)
SMEM = pl.BlockSpec(memory_space=pltpu.SMEM)


def softplus(v):
    return jnp.maximum(v, 0.0) + jnp.log1p(jnp.exp(-jnp.abs(v)))


def load_decay(rate_ref, dec_ref):
    states, groups = dec_ref.shape[0] * 128 // rate_ref.shape[1], rate_ref.shape[1] // 128
    for g in range(groups):
        lanes = slice(g * 128, (g + 1) * 128)
        dec_ref[pl.ds(g, states, stride=groups), :] = -LOG2E * rate_ref[:, lanes]


def ends_kernel(maps_ref, raw_ref, mixer_ref, rate_ref, pack_ref, step_ref, drive_ref, dec_ref):
    rows, channels = raw_ref.shape
    groups = channels // 128
    states = rate_ref.shape[0]
    half = rows // 2
    load_decay(rate_ref, dec_ref)
    dec = [dec_ref[pl.ds(n * groups, groups), :] for n in range(states)]

    @pl.loop(0, rows // 16)
    def _(t):
        for g in range(groups):
            lanes = slice(g * 128, (g + 1) * 128)
            at = pl.ds(t * 16, 16)
            step = softplus(raw_ref[at, lanes].astype(f32))
            to = pl.ds(t * 16 * groups + g, 16, stride=groups)
            step_ref[to, :] = step
            drive_ref[to, :] = step * mixer_ref[0, at, lanes].astype(f32)

    def advance(p, carry):
        total, state = list(carry[0]), [list(v) for v in carry[1]]
        for b in range(2):
            pos = b * half + p
            step = step_ref[pl.ds(pos * groups, groups), :]
            drive = drive_ref[pl.ds(pos * groups, groups), :]
            total[b] = total[b] + step
            for n in range(states):
                decay = jnp.exp2(step * dec[n])
                state[b][n] = decay * state[b][n] + drive * maps_ref[n, pos]
        return tuple(total), tuple(tuple(v) for v in state)

    zero = jnp.zeros((groups, 128), f32)
    total, state = lax.fori_loop(
        0, half, advance, ((zero,) * 2, ((zero,) * states,) * 2), unroll=4
    )
    per = 16 // groups
    for b in range(2):
        for n in range(0, states, per):
            values = jnp.concatenate(state[b][n : n + per], axis=0)
            pack_ref[b, pl.ds(n * groups, 16), :] = values.astype(bf16)
        high = total[b].astype(bf16)
        low = (total[b] - high.astype(f32)).astype(bf16)
        pack_ref[b, pl.ds(states * groups, groups), :] = high
        pack_ref[b, pl.ds((states + 1) * groups, groups), :] = low


def scan_kernel(count, maps_ref, step_ref, drive_ref, rate_ref, mixer_ref, skip_ref, *rest):
    packs, (out_ref, all_ref, y_ref, dec_ref) = rest[:count], rest[count:]
    rows, channels = out_ref.shape
    groups = channels // 128
    states = rate_ref.shape[0]
    load_decay(rate_ref, dec_ref)
    dec = [dec_ref[pl.ds(n * groups, groups), :] for n in range(states)]
    half = rows // 2
    place = lax.axis_index("seq")
    for k in range(count):
        all_ref[k] = packs[k][...].astype(f32)

    def fold(b, carry):
        running, first, second = carry
        opening = b < count
        owner = jnp.where(opening, b, 2 * count - 1 - b)
        slot = lax.rem(place - owner + count, count)
        side = jnp.where(opening, 0, 1)
        total = (
            all_ref[slot, side, pl.ds(states * groups, groups), :]
            + all_ref[slot, side, pl.ds((states + 1) * groups, groups), :]
        )
        first = [jnp.where(b == place, r, f) for r, f in zip(running, first)]
        second = [jnp.where(b == 2 * count - 1 - place, r, s) for r, s in zip(running, second)]
        running = [
            jnp.exp2(total * dec[n]) * running[n]
            + all_ref[slot, side, pl.ds(n * groups, groups), :]
            for n in range(states)
        ]
        return running, first, second

    zeros = [all_ref[0, 0, pl.ds(0, groups), :] * 0.0] * states
    _, first, second = lax.fori_loop(0, 2 * count, fold, (zeros, zeros, zeros))

    def advance(p, state):
        state = [list(v) for v in state]
        for b in range(2):
            pos = b * half + p
            at = pl.ds(pos * groups, groups)
            step = step_ref[at, :]
            drive = drive_ref[at, :]
            parts = [None, None]
            for n in range(states):
                decay = jnp.exp2(step * dec[n])
                state[b][n] = decay * state[b][n] + drive * maps_ref[n, pos]
                term = state[b][n] * maps_ref[states + n, pos]
                parts[n % 2] = term if parts[n % 2] is None else parts[n % 2] + term
            y_ref[at, :] = parts[0] + parts[1]
        return tuple(tuple(v) for v in state)

    lax.fori_loop(0, half, advance, (tuple(first), tuple(second)), unroll=4)

    @pl.loop(0, rows // 16)
    def _(t):
        for g in range(groups):
            lanes = slice(g * 128, (g + 1) * 128)
            at = pl.ds(t * 16, 16)
            y = y_ref[pl.ds(t * 16 * groups + g, 16, stride=groups), :]
            x = mixer_ref[0, at, lanes].astype(f32)
            z = mixer_ref[1, at, lanes].astype(f32)
            out_ref[at, lanes] = ((y + skip_ref[:, lanes] * x) * (z * jax.nn.sigmoid(z))).astype(bf16)


def shift(count, k):
    return [(i, (i + k) % count) for i in range(count)]


def after(values, ready):
    return lax.optimization_barrier((values, ready))[0]


def far_order(count):
    order = [k for pair in zip(range(1, count), range(count - 1, 0, -1)) for k in pair]
    return list(dict.fromkeys(order))


def mix(mixer_input, step_raw, state_maps, decay_rate, skip_gain, out_weight):
    rows, channels = step_raw.shape
    groups = channels // 128
    states = decay_rate.shape[0]
    seq_count = lax.axis_size("seq")
    order = far_order(seq_count)
    swap = [(0, 1), (1, 0)]
    half = out_weight.shape[0] // 2
    mine = lax.dynamic_slice_in_dim(out_weight, lax.axis_index("groups") * half, half, 0)
    direct = {order[0]: lax.ppermute(mine, "seq", shift(seq_count, order[0]))}

    maps = state_maps.reshape(2 * states, rows).astype(f32)
    shape = jax.ShapeDtypeStruct
    pack, step, drive = pl.pallas_call(
        ends_kernel,
        out_shape=(
            shape((2, (states + 2) * groups, 128), bf16),
            shape((rows * groups, 128), f32),
            shape((rows * groups, 128), f32),
        ),
        in_specs=[SMEM] + [VMEM] * 3,
        out_specs=(VMEM,) * 3,
        scratch_shapes=[pltpu.VMEM((states * groups, 128), f32)],
        compiler_params=pltpu.CompilerParams(vmem_limit_bytes=8 << 20),
        name="ends",
    )(maps, step_raw, mixer_input, decay_rate)
    packs = {0: pack}
    for k in order:
        packs[k] = lax.ppermute(pack, "seq", shift(seq_count, k))
    packs = [packs[k] for k in range(seq_count)]
    rest = after(mine, packs)
    for k in order[1:]:
        direct[k] = lax.ppermute(rest, "seq", shift(seq_count, k))
    other = {k: lax.ppermute(direct[k], "groups", swap) for k in order}

    mixed = pl.pallas_call(
        functools.partial(scan_kernel, seq_count),
        out_shape=shape((rows, channels), bf16),
        in_specs=[SMEM] + [VMEM] * (5 + seq_count),
        out_specs=VMEM,
        scratch_shapes=[
            pltpu.VMEM((seq_count, 2, (states + 2) * groups, 128), f32),
            pltpu.VMEM((rows * groups, 128), f32),
            pltpu.VMEM((states * groups, 128), f32),
        ],
        compiler_params=pltpu.CompilerParams(vmem_limit_bytes=12 << 20),
        name="scan",
    )(maps, step, drive, decay_rate, mixer_input, skip_gain[None, :], *packs)
    return mixed, [(k, direct[k], other[k]) for k in order]


def project_kernel(kinds, mixed_ref, *refs):
    keep_ref, away_ref = refs[-2:]
    core = lax.rem(lax.axis_index("exp"), 2)
    group = lax.axis_index("groups")
    chips = lax.axis_size("exp") // 2
    rows = mixed_ref.shape[0] // (2 * chips)
    half = mixed_ref.shape[1] // 2
    spans = (
        slice(None),
        pl.ds(pl.multiple_of(group * half, 128), half),
        pl.ds(pl.multiple_of((1 - group) * half, 128), half),
    )
    for to_ref, side in ((keep_ref, core), (away_ref, 1 - core)):
        parts = [
            jnp.concatenate(
                [mixed_ref[pl.ds(pl.multiple_of((2 * x + side) * rows, rows), rows), span] for x in range(chips)],
                axis=0,
            )
            for span in spans
        ]
        at = 0
        used = 0
        for split in kinds:
            width = refs[used].shape[1]
            if split:
                value = jnp.dot(parts[1], refs[used][...], preferred_element_type=f32)
                value += jnp.dot(parts[2], refs[used + 1][...], preferred_element_type=f32)
            else:
                value = jnp.dot(parts[0], refs[used][...], preferred_element_type=f32)
            to_ref[:, at : at + width] = value
            at += width
            used += 2 if split else 1


def project(mixed, pieces):
    kinds = tuple(len(piece) == 2 for piece in pieces)
    arrays = [array for piece in pieces for array in piece]
    width = sum(piece[0].shape[1] for piece in pieces)
    out = jax.ShapeDtypeStruct((mixed.shape[0] // 2, width), f32)
    return pl.pallas_call(
        functools.partial(project_kernel, kinds),
        out_shape=(out, out),
        in_specs=[VMEM] * (1 + len(arrays)),
        out_specs=(VMEM, VMEM),
        compiler_params=pltpu.CompilerParams(vmem_limit_bytes=12 << 20),
        cost_estimate=pl.CostEstimate(
            flops=2 * mixed.size * width, bytes_accessed=2 * mixed.shape[1] * width, transcendentals=0
        ),
        name="project",
    )(mixed, *arrays)


def leave_kernel(keep_ref, theirs_ref, *out_refs):
    chips = len(out_refs) + 1
    chip = lax.axis_index("exp") // 2
    rows = keep_ref.shape[0] // chips
    for j in range(1, chips):
        at = pl.ds(pl.multiple_of(lax.rem(chip + j, chips) * rows, rows), rows)
        out_refs[j - 1][...] = (keep_ref[at, :] + theirs_ref[at, :]).astype(bf16)


def sum_to_owner(keep, away):
    exp_count = lax.axis_size("exp")
    chips = exp_count // 2
    theirs = lax.ppermute(away, "exp", [(i, i ^ 1) for i in range(exp_count)])
    terms = [keep, theirs]
    out = jax.ShapeDtypeStruct((keep.shape[0] // chips, keep.shape[1]), bf16)
    leaving = pl.pallas_call(
        leave_kernel,
        out_shape=(out,) * (chips - 1),
        in_specs=[VMEM] * 2,
        out_specs=(VMEM,) * (chips - 1),
        compiler_params=pltpu.CompilerParams(vmem_limit_bytes=8 << 20),
        name="leave",
    )(keep, theirs)
    for j in range(1, chips):
        terms.append(lax.ppermute(leaving[j - 1], "exp", shift(exp_count, 2 * j)))
    return terms


def route_kernel(sets, experts, *refs):
    count = sum(len(ks) for ks, _ in sets)
    terms_total = sum(terms for _, terms in sets)
    terms, (residual_ref, gain_ref, router_ref, ids_ref) = refs[:terms_total], refs[terms_total : terms_total + 4]
    stream_ref, packed_ref, sum_ref = refs[terms_total + 4 :]
    rows, width = residual_ref.shape
    part = width // count
    place = lax.axis_index("seq")
    mine = pl.ds(pl.multiple_of(lax.axis_index("exp") // 2 * rows, rows), rows)
    used = 0
    for ks, number in sets:
        for i, k in enumerate(ks):
            lanes = slice(i * part, (i + 1) * part)
            value = terms[used][mine, lanes] + terms[used + 1][mine, lanes]
            for extra in range(2, number):
                value = value + terms[used + extra][:, lanes].astype(f32)
            at = pl.multiple_of(lax.rem(place - k + count, count) * part, 128)
            sum_ref[:, pl.ds(at, part)] = value
        used += number
    stream = (residual_ref[...].astype(f32) + sum_ref[...]).astype(bf16)
    stream_ref[...] = stream
    stream = stream.astype(f32)
    mean_sq = jnp.mean(stream * stream, axis=1, keepdims=True)
    normed = (stream * lax.rsqrt(mean_sq + 1e-05) * gain_ref[...]).astype(bf16)
    packed_ref[:, :width] = normed
    logits = jnp.dot(normed, router_ref[...], preferred_element_type=f32)
    row, column = (lax.broadcasted_iota(jnp.int32, (rows, rows), d) for d in range(2))
    same = jnp.where(row == column, 1.0, 0.0).astype(bf16)
    name = lax.broadcasted_iota(jnp.int32, (128, rows), 0)

    def picked(choice):
        hot = jnp.where(ids_ref[choice : choice + 1, :] == name, 1.0, 0.0).astype(bf16)
        return lax.dot_general(same, hot, (((1,), (1,)), ((), ())), preferred_element_type=f32) > 0.5

    first, second = picked(0), picked(1)
    gap = jnp.sum(jnp.where(first, logits, 0.0), axis=1, keepdims=True) - jnp.sum(
        jnp.where(second, logits, 0.0), axis=1, keepdims=True
    )
    weight = jnp.where(first, jax.nn.sigmoid(gap), 0.0) + jnp.where(second, jax.nn.sigmoid(-gap), 0.0)
    routed = jnp.where(first, 1.0, 0.0) + jnp.where(second, 1.0, 0.0)
    earlier = jnp.where(row > column, 1.0, 0.0)
    slot = jnp.dot(earlier.astype(bf16), routed.astype(bf16), preferred_element_type=f32)
    slot = jnp.where(routed > 0.0, slot + 1.0, 0.0)
    high = weight.astype(bf16).astype(f32)
    lanes = high + pltpu.roll(weight - high, experts, 1) + pltpu.roll(slot, 2 * experts, 1)
    packed_ref[:, width:] = lanes.astype(bf16)


def route(sets, residual, norm_gain, router, experts, expert_ids):
    rows, width = residual.shape
    shape = jax.ShapeDtypeStruct
    terms = [term for _, group in sets for term in group]
    kinds = tuple((tuple(ks), len(group)) for ks, group in sets)
    return pl.pallas_call(
        functools.partial(route_kernel, kinds, experts),
        out_shape=(shape((rows, width), bf16), shape((rows, width + 128), bf16)),
        in_specs=[VMEM] * (len(terms) + 4),
        out_specs=(VMEM, VMEM),
        scratch_shapes=[pltpu.VMEM((rows, width), f32)],
        compiler_params=pltpu.CompilerParams(vmem_limit_bytes=8 << 20),
        name="route",
    )(*terms, residual, norm_gain[None, :], router, expert_ids.T)


def expert_kernel(capacity, block_rows, experts, tile, own_ref, mate_ref, gate_ref, up_ref, down_ref, *rest):
    keep_ref, send_ref, acc_ref = rest
    rows, width = keep_ref.shape
    slots = acc_ref.shape[0]
    lane = lax.broadcasted_iota(jnp.int32, (1, 128), 1)
    place = lax.axis_index("exp")
    picked = lane == 2 * experts + place
    wanted = jnp.broadcast_to(jnp.where(picked, 1.0, 0.0), (8, 128)).astype(bf16)
    held = None
    for side, ref in enumerate((own_ref, mate_ref)):
        slot = lax.dot_general(
            wanted, ref[:, width:], (((1,), (1,)), ((), ())), preferred_element_type=f32
        )[0:1, :].astype(jnp.int32)
        block = lax.broadcasted_iota(jnp.int32, (1, rows), 1) // block_rows + side * (rows // block_rows)
        target = jnp.where(slot > 0, block * capacity + slot - 1, -1)
        chosen = jnp.where(lax.broadcasted_iota(jnp.int32, (slots, rows), 0) == target, 1.0, 0.0)
        value = jnp.dot(chosen.astype(bf16), ref[...], preferred_element_type=f32)
        held = value if held is None else held + value
    mine = (lane == place) | (lane == experts + place)
    weight = jnp.sum(jnp.where(mine, held[:, width:], 0.0), axis=1, keepdims=True)
    held = held[:, :width].astype(bf16)

    for t in range(gate_ref.shape[2] // tile):
        at = slice(t * tile, (t + 1) * tile)
        gated = jnp.dot(held, gate_ref[0, :, at], preferred_element_type=f32)
        upper = jnp.dot(held, up_ref[0, :, at], preferred_element_type=f32)
        hidden = (gated * jax.nn.sigmoid(gated) * upper).astype(bf16)
        value = jnp.dot(hidden, down_ref[0, at, :], preferred_element_type=f32)
        if t == 0:
            acc_ref[...] = value
        else:
            acc_ref[...] += value

    scaled = (acc_ref[...] * weight).astype(bf16)
    for side, ref in enumerate((own_ref, mate_ref)):
        slot = jnp.sum(jnp.where(picked, ref[:, width:].astype(f32), 0.0), axis=1, keepdims=True)
        block = lax.broadcasted_iota(jnp.int32, (rows, 1), 0) // block_rows + side * (rows // block_rows)
        target = jnp.where(slot > 0.0, block * capacity + slot.astype(jnp.int32) - 1, -1)
        chosen = jnp.where(lax.broadcasted_iota(jnp.int32, (rows, slots), 1) == target, 1.0, 0.0)
        back = jnp.dot(chosen.astype(bf16), scaled, preferred_element_type=f32)
        if side == 0:
            keep_ref[...] = back
        else:
            send_ref[...] = back.astype(bf16)


def hold_kernel(from_ref, to_ref):
    pltpu.sync_copy(from_ref, to_ref)


def hold(weight, ready):
    return pl.pallas_call(
        hold_kernel,
        out_shape=jax.ShapeDtypeStruct(weight.shape, weight.dtype),
        in_specs=[pl.BlockSpec(memory_space=pl.ANY)],
        out_specs=VMEM,
        compiler_params=pltpu.CompilerParams(vmem_limit_bytes=16 << 20),
        cost_estimate=pl.CostEstimate(flops=0, bytes_accessed=2 * weight.size, transcendentals=0),
        name="hold",
    )(after(weight, ready))


def expert_part(own, mate, capacity, block_rows, experts, gate, up, down):
    rows, width = own.shape[0], own.shape[1] - 128
    hidden = gate.shape[2]
    tile = 256 if hidden % 256 == 0 else hidden
    slots = -(-2 * rows // block_rows * capacity // 16) * 16
    shape = jax.ShapeDtypeStruct
    return pl.pallas_call(
        functools.partial(expert_kernel, capacity, block_rows, experts, tile),
        out_shape=(shape((rows, width), f32), shape((rows, width), bf16)),
        in_specs=[VMEM] * 5,
        out_specs=(VMEM, VMEM),
        scratch_shapes=[pltpu.VMEM((slots, width), f32)],
        compiler_params=pltpu.CompilerParams(vmem_limit_bytes=VMEM_EXPERT << 20),
        cost_estimate=pl.CostEstimate(
            flops=6 * slots * width * hidden,
            bytes_accessed=6 * width * hidden,
            transcendentals=slots * hidden,
        ),
        name="expert",
    )(own, mate, gate, up, down)


def experts_sum(packed, experts, capacity, gate, up, down):
    seq_count = lax.axis_size("seq")
    exp_count = lax.axis_size("exp")
    chips = exp_count // 2
    rows = packed.shape[0]
    partner = [(i, i ^ 1) for i in range(exp_count)]
    order = far_order(seq_count)

    planes = {0: packed}
    for k in order:
        planes[k] = lax.ppermute(packed, "seq", shift(seq_count, k))

    total = None
    for k in [0] + order:
        row = [planes[k]]
        for j in range(1, chips):
            row.append(lax.ppermute(planes[k], "exp", shift(exp_count, 2 * j)))
        row = jnp.concatenate(row, axis=0)
        mate = lax.ppermute(row, "exp", partner)
        keep, send = expert_part(row, mate, capacity, rows, experts, gate, up, down)
        pair = keep + lax.ppermute(send, "exp", partner).astype(f32)
        mine = pair[:rows]
        for j in range(1, chips):
            leaving = pair[j * rows : (j + 1) * rows].astype(bf16)
            mine = mine + lax.ppermute(leaving, "exp", shift(exp_count, exp_count - 2 * j)).astype(f32)
        if k:
            mine = lax.ppermute(mine.astype(bf16), "seq", shift(seq_count, seq_count - k)).astype(f32)
        total = mine if total is None else total + mine
    return total


def per_device(
    residual,
    mixer_input,
    step_raw,
    state_maps,
    decay_rate,
    skip_gain,
    out_weight,
    norm_gain,
    router_weight,
    expert_ids,
    gate_weight,
    up_weight,
    down_weight,
):
    experts = router_weight.shape[1]
    router = jnp.pad(router_weight, ((0, 0), (0, 128 - experts)))
    skip_gain, router, expert_ids = lax.optimization_barrier((skip_gain, router, expert_ids))
    mixed, blocks = mix(mixer_input, step_raw, state_maps, decay_rate, skip_gain, out_weight)
    weights = (gate_weight, up_weight, down_weight)
    held = [hold(weight, mixed) for weight in weights]
    order = [0] + [block[0] for block in blocks]
    pieces = [(out_weight,)] + [block[1:] for block in blocks]
    sets = []
    for part in (slice(0, -1), slice(-1, None)):
        keep, away = project(mixed, pieces[part])
        sets.append((order[part], sum_to_owner(keep, away)))
    stream, packed = route(sets, residual, norm_gain, router, experts, expert_ids)
    capacity = max(2, 8 * residual.shape[0] // (3 * experts))
    added = experts_sum(packed, experts, capacity, *held)
    return (stream.astype(f32) + added).astype(bf16)


def solution(mesh):
    in_specs = (
        P(("groups", "seq", "exp"), None),
        P(None, ("groups", "seq"), "exp"),
        P(("groups", "seq"), "exp"),
        P(None, None, ("groups", "seq")),
        P(None, "exp"),
        P("exp"),
        P("exp", "seq"),
        P(),
        P(),
        P(("groups", "seq", "exp"), None),
        P("exp", None, "seq"),
        P("exp", None, "seq"),
        P("exp", "seq", None),
    )
    out_specs = P(("groups", "seq", "exp"), None)

    return jax.shard_map(per_device, mesh=mesh, in_specs=in_specs, out_specs=out_specs, check_vma=False)
```

time: 262 us -> 202 us (0.77)
  the two profiles are of different devices: /device:TPU:11 before, /device:TPU:0 now
where the time goes in v2:
time: 202 us; the launch traced here: 201 us
  waiting for transfers between devices  93.3 us (46%)
  Pallas kernels  45.2 us (22%)
  starting transfers between devices  40.4 us (20%)
  local copies, waits for them, and re-layouts  19.8 us (10%)
  other arithmetic  2.2 us (1%)
    pallas_call x4, Pallas kernels, expert_part(): pl.pallas_call(functools.partial(expert_kernel, capacity, block_rows, exp...  25.6 us
    ppermute x4, waiting for transfers between devices, experts_sum(): lax.ppermute(leaving, 'exp', shift(exp_count, exp_count - 2 * j))  18.8 us
    unnamed x45, local copies, waits for them, and re-layouts  16.5 us
    ppermute x3, waiting for transfers between devices, mix(): other = {k: lax.ppermute(direct[k], 'groups', swap) for k in order}  13.5 us
    ppermute x3, waiting for transfers between devices, experts_sum(): lax.ppermute(mine.astype(bf16), 'seq', shift(seq_count, seq_count - k))  12.9 us
    ppermute x2, waiting for transfers between devices, mix(): direct[k] = lax.ppermute(rest, 'seq', shift(seq_count, k))  12.8 us
    ppermute x4, waiting for transfers between devices, experts_sum(): row.append(lax.ppermute(planes[k], 'exp', shift(exp_count, 2 * j)))  11.1 us
    ppermute x1, waiting for transfers between devices, mix(): direct = {order[0]: lax.ppermute(mine, 'seq', shift(seq_count, order[0]))}  11 us
  transfers between devices with their start and end apart: 35, of which 16 were waited for; matrix products, arithmetic and copies ran while one was open for 3% of the time, Pallas kernels for 19%

profile of v2, /device:TPU:0, one launch (start us, length us, event | category | flops | bytes accessed | tf_op | source)
XLA Modules:
  0.0 201.3 jit_solution(7387502564942715607)
XLA Ops:
  0.7 1.2 copy-done
  3.8 5.7 %ends.1 = (bf16[2,144,128]{2,1,0:T(8,128)(2,1)S(1)}, f32[2048,128]{1,0:T(8,128)S(1)}, f32[2048,128]{1,0:T(8,128)S(1)}) custom-call(f32[32,256]{1,0:T(8,128)S(1)} %bitcast_convert_fusion.maps_ref, bf16[256,1024]{1,0:T(8,128)(2,1)S(1)} %copy-done.7, bf16[2,256,1024]{2,1,0:T(8,128)(2,1)S(1)} %copy-done, f32[16,1024]{1,0:T(8,128)S(1)} %copy-done.8), custom_call_target="tpu_custom_call" | custom-call | tf_op jit(solution)/shard_map/ends/pallas_call | solution.py:163
  11.5 3.1 %collective-permute-start = (bf16[2,144,128]{2,1,0:T(8,128)(2,1)S(1)}, bf16[2,144,128]{2,1,0:T(8,128)(2,1)S(1)}, u32[]{:S(2)}, u32[]{:S(2)}) collective-permute-start(bf16[2,144,128]{2,1,0:T(8,128)(2,1)S(1)} %get-tuple-element.32.rest_0_), channel_id=1, source_target_pairs={{0,4},{4,8},{8,12},{12,0},{1,5},{5,9},{9,13},{13,1},{2,6},{6,10},{... | collective-permute-start | bytes 221192 | tf_op jit(solution)/shard_map/ppermute | solution.py:178
  14.6 2.6 %collective-permute-start.1 = (bf16[2,144,128]{2,1,0:T(8,128)(2,1)S(1)}, bf16[2,144,128]{2,1,0:T(8,128)(2,1)S(1)}, u32[]{:S(2)}, u32[]{:S(2)}) collective-permute-start(bf16[2,144,128]{2,1,0:T(8,128)(2,1)S(1)} %get-tuple-element.32.rest_0_), channel_id=1, source_target_pairs={{0,8},{4,12},{8,0},{12,4},{1,9},{5,13},{9,1},{13,5},{2,10},{6,14},... | collective-permute-start | bytes 221192 | tf_op jit(solution)/shard_map/ppermute | solution.py:178
  17.2 1.3 collective-permute-start.2
  18.5 1.9 constant_dynamic-slice_fusion
  22.4 4.0 %collective-permute-start.5 = (bf16[512,512]{1,0:T(8,128)(2,1)}, bf16[512,512]{1,0:T(8,128)(2,1)}, u32[]{:S(2)}, u32[]{:S(2)}) collective-permute-start(bf16[512,512]{1,0:T(8,128)(2,1)} %constant_dynamic-slice_fusion), channel_id=1, source_target_pairs={{0,12},{4,0},{8,4},{12,8},{1,13},{5,1},{9,5},{13,9},{2,14},{6,2},{... | collective-permute-start | bytes 1572872 | tf_op jit(solution)/shard_map/ppermute | solution.py:182
  26.4 11.0 %collective-permute-done.3.refs_1_ = bf16[512,512]{1,0:T(8,128)(2,1)} collective-permute-done((bf16[512,512]{1,0:T(8,128)(2,1)}, bf16[512,512]{1,0:T(8,128)(2,1)}, u32[]{:S(2)}, u32[]{:S(2)}) %collective-permute-start.3) | collective-permute-done | bytes 524320 | tf_op jit(solution)/shard_map/ppermute | solution.py:159
  37.4 1.5 collective-permute-start.4
  38.9 7.7 %collective-permute-done.5.refs_3_ = bf16[512,512]{1,0:T(8,128)(2,1)} collective-permute-done((bf16[512,512]{1,0:T(8,128)(2,1)}, bf16[512,512]{1,0:T(8,128)(2,1)}, u32[]{:S(2)}, u32[]{:S(2)}) %collective-permute-start.5) | collective-permute-done | bytes 524320 | tf_op jit(solution)/shard_map/ppermute | solution.py:182
  46.6 1.5 collective-permute-start.6
  48.1 1.1 collective-permute-start.9
  49.2 1.8 copy.14
  51.0 1.1 pad.4.refs_8_
  52.1 1.2 copy-done.1
  53.4 1.2 copy-done.4
  54.6 1.2 copy-done.6
  57.3 7.5 %scan.1.mixed_ref = bf16[256,1024]{1,0:T(8,128)(2,1)S(1)} custom-call(f32[32,256]{1,0:T(8,128)S(1)} %bitcast_convert_fusion.maps_ref, f32[2048,128]{1,0:T(8,128)S(1)} %copy-done.4, f32[2048,128]{1,0:T(8,128)S(1)} %copy-done.6, f32[16,1024]{1,0:T(8,128)S(1)} %copy-done.9, bf16[2,256,1024]{2,1,0:T(8,128)(2,1)S(1)} %copy-done.1, f32[1,1024]{1,0:T(1,128)S(1)} %bitcast.13, ...), custom_call_target="tpu_custom_call" | custom-call | tf_op jit(solution)/shard_map/scan/pallas_call | solution.py:185
  64.9 1.4 copy-done.2
  66.2 2.7 %project.2 = (f32[128,1536]{1,0:T(8,128)S(1)}, f32[128,1536]{1,0:T(8,128)S(1)}) custom-call(bf16[256,1024]{1,0:T(8,128)(2,1)S(1)} %scan.1.mixed_ref, bf16[1024,512]{1,0:T(8,128)(2,1)S(1)} %copy-done.2, bf16[512,512]{1,0:T(8,128)(2,1)} %collective-permute-done.3.refs_1_, bf16[512,512]{1,0:T(8,128)(2,1)} %collective-permute-done.4.refs_2_, ...), custom_call_target="tpu_custom_call" | custom-call | flops 805306368 | bytes 3145728 | tf_op jit(solution)/shard_map/project/pallas_call | solution.py:240
  69.0 5.1 %collective-permute-done.9.refs_0_ = bf16[512,512]{1,0:T(8,128)(2,1)} collective-permute-done((bf16[512,512]{1,0:T(8,128)(2,1)}, bf16[512,512]{1,0:T(8,128)(2,1)}, u32[]{:S(2)}, u32[]{:S(2)}) %collective-permute-start.9) | collective-permute-done | bytes 524320 | tf_op jit(solution)/shard_map/ppermute | solution.py:182
  74.6 13.5 %collective-permute-done.10.refs_1_ = bf16[512,512]{1,0:T(8,128)(2,1)S(1)} collective-permute-done((bf16[512,512]{1,0:T(8,128)(2,1)}, bf16[512,512]{1,0:T(8,128)(2,1)S(1)}, u32[]{:S(2)}, u32[]{:S(2)}) %collective-permute-start.10) | collective-permute-done | bytes 524320 | tf_op jit(solution)/shard_map/ppermute | solution.py:183
  88.2 1.5 project.3
  89.8 1.6 collective-permute-start.8
  91.4 1.4 collective-permute-start.12
  97.3 1.2 collective-permute-done.12.refs_5_
  99.4 3.8 %collective-permute-start.23 = (bf16[64,2176]{1,0:T(8,128)(2,1)S(1)}, bf16[64,2176]{1,0:T(8,128)(2,1)S(1)}, u32[]{:S(2)}, u32[]{:S(2)}) collective-permute-start(bf16[64,2176]{1,0:T(8,128)(2,1)S(1)} %get-tuple-element.41), channel_id=1, source_target_pairs={{0,12},{4,0},{8,4},{12,8},{1,13},{5,1},{9,5},{13,9},{2,14},{6,2},{... | collective-permute-start | bytes 835592 | tf_op jit(solution)/shard_map/ppermute | solution.py:439
  103.2 1.5 collective-permute-start.13
  104.7 6.1 %collective-permute-done.13 = bf16[64,2176]{1,0:T(8,128)(2,1)S(1)} collective-permute-done((bf16[64,2176]{1,0:T(8,128)(2,1)S(1)}, bf16[64,2176]{1,0:T(8,128)(2,1)S(1)}, u32[]{:S(2)}, u32[]{:S(2)}) %collective-permute-start.13) | collective-permute-done | bytes 278560 | tf_op jit(solution)/shard_map/ppermute | solution.py:445
  110.9 1.6 collective-permute-start.18
  112.5 3.5 %collective-permute-done.23 = bf16[64,2176]{1,0:T(8,128)(2,1)S(1)} collective-permute-done((bf16[64,2176]{1,0:T(8,128)(2,1)S(1)}, bf16[64,2176]{1,0:T(8,128)(2,1)S(1)}, u32[]{:S(2)}, u32[]{:S(2)}) %collective-permute-start.23) | collective-permute-done | bytes 278560 | tf_op jit(solution)/shard_map/ppermute | solution.py:439
  116.0 1.5 collective-permute-start.24
  117.5 7.2 %collective-permute-done.29 = bf16[64,2176]{1,0:T(8,128)(2,1)S(1)} collective-permute-done((bf16[64,2176]{1,0:T(8,128)(2,1)S(1)}, bf16[64,2176]{1,0:T(8,128)(2,1)S(1)}, u32[]{:S(2)}, u32[]{:S(2)}) %collective-permute-start.29) | collective-permute-done | bytes 278560 | tf_op jit(solution)/shard_map/ppermute | solution.py:439
  124.7 1.5 collective-permute-start.30
  127.0 5.0 %collective-permute-done.30 = bf16[64,2176]{1,0:T(8,128)(2,1)S(1)} collective-permute-done((bf16[64,2176]{1,0:T(8,128)(2,1)S(1)}, bf16[64,2176]{1,0:T(8,128)(2,1)S(1)}, u32[]{:S(2)}, u32[]{:S(2)}) %collective-permute-start.30) | collective-permute-done | bytes 278560 | tf_op jit(solution)/shard_map/ppermute | solution.py:445
  132.0 6.3 %expert.4 = (f32[128,2048]{1,0:T(8,128)S(1)}, bf16[128,2048]{1,0:T(8,128)(2,1)S(1)}) custom-call(bf16[128,2176]{1,0:T(8,128)(2,1)S(1)} %constant_dynamic-update-slice_fusion.own_ref, bf16[128,2176]{1,0:T(8,128)(2,1)S(1)} %collective-permute-done.14.mate_ref, bf16[1,2048,1792]{2,1,0:T(8,128)(2,1)S(1)} %hold.3.gate_ref, ...), custom_call_target="tpu_custom_call" | custom-call | flops 3875536896 | bytes 22020096 | tf_op jit(solution)/shard_map/expert/pallas_call | solution.py:413
  139.0 6.3 %expert.5 = (f32[128,2048]{1,0:T(8,128)S(1)}, bf16[128,2048]{1,0:T(8,128)(2,1)S(1)}) custom-call(bf16[128,2176]{1,0:T(8,128)(2,1)S(1)} %constant_dynamic-update-slice_fusion.2.own_ref, bf16[128,2176]{1,0:T(8,128)(2,1)S(1)} %collective-permute-done.19.mate_ref, bf16[1,2048,1792]{2,1,0:T(8,128)(2,1)S(1)} %hold.3.gate_ref, ...), custom_call_target="tpu_custom_call" | custom-call | flops 3875536896 | bytes 22020096 | tf_op jit(solution)/shard_map/expert/pallas_call | solution.py:413
  145.4 6.6 %expert.6 = (f32[128,2048]{1,0:T(8,128)S(1)}, bf16[128,2048]{1,0:T(8,128)(2,1)S(1)}) custom-call(bf16[128,2176]{1,0:T(8,128)(2,1)S(1)} %constant_dynamic-update-slice_fusion.4.own_ref, bf16[128,2176]{1,0:T(8,128)(2,1)S(1)} %collective-permute-done.25.mate_ref, bf16[1,2048,1792]{2,1,0:T(8,128)(2,1)S(1)} %hold.3.gate_ref, ...), custom_call_target="tpu_custom_call" | custom-call | flops 3875536896 | bytes 22020096 | tf_op jit(solution)/shard_map/expert/pallas_call | solution.py:413
  152.5 6.3 %expert.7 = (f32[128,2048]{1,0:T(8,128)S(1)}, bf16[128,2048]{1,0:T(8,128)(2,1)S(1)}) custom-call(bf16[128,2176]{1,0:T(8,128)(2,1)S(1)} %constant_dynamic-update-slice_fusion.6.own_ref, bf16[128,2176]{1,0:T(8,128)(2,1)S(1)} %collective-permute-done.31.mate_ref, bf16[1,2048,1792]{2,1,0:T(8,128)(2,1)S(1)} %hold.3.gate_ref, ...), custom_call_target="tpu_custom_call" | custom-call | flops 3875536896 | bytes 22020096 | tf_op jit(solution)/shard_map/expert/pallas_call | solution.py:413
  159.1 1.6 collective-permute-start.16
  161.6 1.6 collective-permute-start.27
  163.9 10.1 %collective-permute-done.21 = bf16[64,2048]{1,0:T(8,128)(2,1)S(1)} collective-permute-done((bf16[64,2048]{1,0:T(8,128)(2,1)S(1)}, bf16[64,2048]{1,0:T(8,128)(2,1)S(1)}, u32[]{:S(2)}, u32[]{:S(2)}) %collective-permute-start.21) | collective-permute-done | bytes 262176 | tf_op jit(solution)/shard_map/ppermute | solution.py:453
  174.0 1.4 collective-permute-start.22
  175.4 4.2 %collective-permute-done.27 = bf16[64,2048]{1,0:T(8,128)(2,1)S(1)} collective-permute-done((bf16[64,2048]{1,0:T(8,128)(2,1)S(1)}, bf16[64,2048]{1,0:T(8,128)(2,1)S(1)}, u32[]{:S(2)}, u32[]{:S(2)}) %collective-permute-start.27) | collective-permute-done | bytes 262176 | tf_op jit(solution)/shard_map/ppermute | solution.py:453
  180.2 4.5 %collective-permute-done.33 = bf16[64,2048]{1,0:T(8,128)(2,1)S(1)} collective-permute-done((bf16[64,2048]{1,0:T(8,128)(2,1)S(1)}, bf16[64,2048]{1,0:T(8,128)(2,1)S(1)}, u32[]{:S(2)}, u32[]{:S(2)}) %collective-permute-start.33) | collective-permute-done | bytes 262176 | tf_op jit(solution)/shard_map/ppermute | solution.py:453
  184.8 2.7 %collective-permute-start.34 = (bf16[64,2048]{1,0:T(8,128)(2,1)S(1)}, bf16[64,2048]{1,0:T(8,128)(2,1)S(1)}, u32[]{:S(2)}, u32[]{:S(2)}) collective-permute-start(bf16[64,2048]{1,0:T(8,128)(2,1)S(1)} %fusion), channel_id=1, source_target_pairs={{0,8},{4,12},{8,0},{12,4},{1,9},{5,13},{9,1},{13,5},{2,10},{6,14},... | collective-permute-start | bytes 786440 | tf_op jit(solution)/shard_map/ppermute | solution.py:455
  187.5 2.9 %collective-permute-done.28 = bf16[64,2048]{1,0:T(8,128)(2,1)S(1)} collective-permute-done((bf16[64,2048]{1,0:T(8,128)(2,1)S(1)}, bf16[64,2048]{1,0:T(8,128)(2,1)S(1)}, u32[]{:S(2)}, u32[]{:S(2)}) %collective-permute-start.28) | collective-permute-done | bytes 262176 | tf_op jit(solution)/shard_map/ppermute | solution.py:455
  190.4 9.9 %collective-permute-done.34 = bf16[64,2048]{1,0:T(8,128)(2,1)S(1)} collective-permute-done((bf16[64,2048]{1,0:T(8,128)(2,1)S(1)}, bf16[64,2048]{1,0:T(8,128)(2,1)S(1)}, u32[]{:S(2)}, u32[]{:S(2)}) %collective-permute-start.34) | collective-permute-done | bytes 262176 | tf_op jit(solution)/shard_map/ppermute | solution.py:455
  (103 shorter events, 19.8 us)
Async XLA Ops:
  0.7 1.2 copy-start
  11.5 81.3 %slice-start = ((s8[7340032]{0:T(1024)(128)(4,1)}), s8[3145728]{0:T(1024)(128)(4,1)S(1)}, s32[]{:S(2)}) async-start(s8[7340032]{0:T(1024)(128)(4,1)} %bitcast.6), calls=%async_computation | async-start | bytes 6291456
  11.5 9.5 %collective-permute-start = (bf16[2,144,128]{2,1,0:T(8,128)(2,1)S(1)}, bf16[2,144,128]{2,1,0:T(8,128)(2,1)S(1)}, u32[]{:S(2)}, u32[]{:S(2)}) collective-permute-start(bf16[2,144,128]{2,1,0:T(8,128)(2,1)S(1)} %get-tuple-element.32.rest_0_), channel_id=1, source_target_pairs={{0,4},{4,8},{8,12},{12,0},{1,5},{5,9},{9,13},{13,1},{2,6},{6,10},{... | collective-permute-start | bytes 221192 | tf_op jit(solution)/shard_map/ppermute | solution.py:178
  14.6 7.5 %collective-permute-start.1 = (bf16[2,144,128]{2,1,0:T(8,128)(2,1)S(1)}, bf16[2,144,128]{2,1,0:T(8,128)(2,1)S(1)}, u32[]{:S(2)}, u32[]{:S(2)}) collective-permute-start(bf16[2,144,128]{2,1,0:T(8,128)(2,1)S(1)} %get-tuple-element.32.rest_0_), channel_id=1, source_target_pairs={{0,8},{4,12},{8,0},{12,4},{1,9},{5,13},{9,1},{13,5},{2,10},{6,14},... | collective-permute-start | bytes 221192 | tf_op jit(solution)/shard_map/ppermute | solution.py:178
  17.2 5.2 %collective-permute-start.2 = (bf16[2,144,128]{2,1,0:T(8,128)(2,1)S(1)}, bf16[2,144,128]{2,1,0:T(8,128)(2,1)S(1)}, u32[]{:S(2)}, u32[]{:S(2)}) collective-permute-start(bf16[2,144,128]{2,1,0:T(8,128)(2,1)S(1)} %get-tuple-element.32.rest_0_), channel_id=1, source_target_pairs={{0,12},{4,0},{8,4},{12,8},{1,13},{5,1},{9,5},{13,9},{2,14},{6,2},{... | collective-permute-start | bytes 221192 | tf_op jit(solution)/shard_map/ppermute | solution.py:178
  20.4 17.0 %collective-permute-start.3 = (bf16[512,512]{1,0:T(8,128)(2,1)}, bf16[512,512]{1,0:T(8,128)(2,1)}, u32[]{:S(2)}, u32[]{:S(2)}) collective-permute-start(bf16[512,512]{1,0:T(8,128)(2,1)} %constant_dynamic-slice_fusion), channel_id=1, source_target_pairs={{0,4},{4,8},{8,12},{12,0},{1,5},{5,9},{9,13},{13,1},{2,6},{6,10},{... | collective-permute-start | bytes 1572872 | tf_op jit(solution)/shard_map/ppermute | solution.py:159
  22.4 24.2 %collective-permute-start.5 = (bf16[512,512]{1,0:T(8,128)(2,1)}, bf16[512,512]{1,0:T(8,128)(2,1)}, u32[]{:S(2)}, u32[]{:S(2)}) collective-permute-start(bf16[512,512]{1,0:T(8,128)(2,1)} %constant_dynamic-slice_fusion), channel_id=1, source_target_pairs={{0,12},{4,0},{8,4},{12,8},{1,13},{5,1},{9,5},{13,9},{2,14},{6,2},{... | collective-permute-start | bytes 1572872 | tf_op jit(solution)/shard_map/ppermute | solution.py:182
  37.4 27.5 %collective-permute-start.4 = (bf16[512,512]{1,0:T(8,128)(2,1)}, bf16[512,512]{1,0:T(8,128)(2,1)}, u32[]{:S(2)}, u32[]{:S(2)}) collective-permute-start(bf16[512,512]{1,0:T(8,128)(2,1)} %collective-permute-done.3.refs_1_), channel_id=1, source_target_pairs={{0,16},{16,0},{1,17},{17,1},{2,18},{18,2},{3,19},{19,3},{4,20},{20... | collective-permute-start | bytes 1572872 | tf_op jit(solution)/shard_map/ppermute | solution.py:183
  46.6 18.3 %collective-permute-start.6 = (bf16[512,512]{1,0:T(8,128)(2,1)}, bf16[512,512]{1,0:T(8,128)(2,1)}, u32[]{:S(2)}, u32[]{:S(2)}) collective-permute-start(bf16[512,512]{1,0:T(8,128)(2,1)} %collective-permute-done.5.refs_3_), channel_id=1, source_target_pairs={{0,16},{16,0},{1,17},{17,1},{2,18},{18,2},{3,19},{19,3},{4,20},{20... | collective-permute-start | bytes 1572872 | tf_op jit(solution)/shard_map/ppermute | solution.py:183
  48.1 26.0 %collective-permute-start.9 = (bf16[512,512]{1,0:T(8,128)(2,1)}, bf16[512,512]{1,0:T(8,128)(2,1)}, u32[]{:S(2)}, u32[]{:S(2)}) collective-permute-start(bf16[512,512]{1,0:T(8,128)(2,1)} %constant_dynamic-slice_fusion), channel_id=1, source_target_pairs={{0,8},{4,12},{8,0},{12,4},{1,9},{5,13},{9,1},{13,5},{2,10},{6,14},... | collective-permute-start | bytes 1572872 | tf_op jit(solution)/shard_map/ppermute | solution.py:182
  52.1 1.2 copy-start.1
  53.4 1.2 copy-start.4
  64.8 28.0 %slice-start.1 = ((s8[7340032]{0:T(1024)(128)(4,1)}), s8[4194304]{0:T(1024)(128)(4,1)S(1)}, s32[]{:S(2)}) async-start(s8[7340032]{0:T(1024)(128)(4,1)} %bitcast.6), calls=%async_computation.1 | async-start | bytes 8388608
  64.9 1.4 copy-start.2
  68.9 20.8 %collective-permute-start.7 = (f32[128,1536]{1,0:T(8,128)S(1)}, f32[128,1536]{1,0:T(8,128)S(1)}, u32[]{:S(2)}, u32[]{:S(2)}) collective-permute-start(f32[128,1536]{1,0:T(8,128)S(1)} %get-tuple-element.35), channel_id=1, source_target_pairs={{0,1},{1,0},{2,3},{3,2},{4,5},{5,4},{6,7},{7,6},{8,9},{9,8},{10,11... | collective-permute-start | bytes 2359304 | tf_op jit(solution)/shard_map/ppermute | solution.py:265
  74.1 14.1 %collective-permute-start.10 = (bf16[512,512]{1,0:T(8,128)(2,1)}, bf16[512,512]{1,0:T(8,128)(2,1)S(1)}, u32[]{:S(2)}, u32[]{:S(2)}) collective-permute-start(bf16[512,512]{1,0:T(8,128)(2,1)} %collective-permute-done.9.refs_0_), channel_id=1, source_target_pairs={{0,16},{16,0},{1,17},{17,1},{2,18},{18,2},{3,19},{19,3},{4,20},{20... | collective-permute-start | bytes 1572872 | tf_op jit(solution)/shard_map/ppermute | solution.py:183
  89.6 1.7 collective-permute-start.11
  89.8 8.7 %collective-permute-start.8 = (bf16[64,1536]{1,0:T(8,128)(2,1)S(1)}, bf16[64,1536]{1,0:T(8,128)(2,1)S(1)}, u32[]{:S(2)}, u32[]{:S(2)}) collective-permute-start(bf16[64,1536]{1,0:T(8,128)(2,1)S(1)} %leave.2), channel_id=1, source_target_pairs={{0,2},{1,3},{2,0},{3,1},{4,6},{5,7},{6,4},{7,5},{8,10},{9,11},{10,... | collective-permute-start | bytes 589832 | tf_op jit(solution)/shard_map/ppermute | solution.py:277
  91.4 2.2 %slice-start.2 = ((s8[7340032]{0:T(1024)(128)(4,1)}), s8[4194304]{0:T(1024)(128)(4,1)S(1)}, s32[]{:S(2)}) async-start(s8[7340032]{0:T(1024)(128)(4,1)} %bitcast.8), calls=%async_computation.2 | async-start | bytes 8388608
  91.4 3.2 %slice-start.3 = ((s8[7340032]{0:T(1024)(128)(4,1)}), s8[3145728]{0:T(1024)(128)(4,1)S(1)}, s32[]{:S(2)}) async-start(s8[7340032]{0:T(1024)(128)(4,1)} %bitcast.8), calls=%async_computation.3 | async-start | bytes 6291456
  91.4 7.1 %collective-permute-start.12 = (bf16[64,512]{1,0:T(8,128)(2,1)S(1)}, bf16[64,512]{1,0:T(8,128)(2,1)S(1)}, u32[]{:S(2)}, u32[]{:S(2)}) collective-permute-start(bf16[64,512]{1,0:T(8,128)(2,1)S(1)} %leave.3), channel_id=1, source_target_pairs={{0,2},{1,3},{2,0},{3,1},{4,6},{5,7},{6,4},{7,5},{8,10},{9,11},{10,... | collective-permute-start | bytes 196616 | tf_op jit(solution)/shard_map/ppermute | solution.py:277
  92.8 3.1 %slice-start.4 = ((s8[7340032]{0:T(1024)(128)(4,1)}), s8[4194304]{0:T(1024)(128)(4,1)S(1)}, s32[]{:S(2)}) async-start(s8[7340032]{0:T(1024)(128)(4,1)} %bitcast.10), calls=%async_computation.4 | async-start | bytes 8388608
  94.5 2.3 %slice-start.5 = ((s8[7340032]{0:T(1024)(128)(4,1)}), s8[3145728]{0:T(1024)(128)(4,1)S(1)}, s32[]{:S(2)}) async-start(s8[7340032]{0:T(1024)(128)(4,1)} %bitcast.10), calls=%async_computation.5 | async-start | bytes 6291456
  96.8 1.7 copy-start.10
  96.8 1.7 copy-start.11
  96.8 1.8 copy-start.13
  99.3 11.6 %collective-permute-start.17 = (bf16[64,2176]{1,0:T(8,128)(2,1)S(1)}, bf16[64,2176]{1,0:T(8,128)(2,1)S(1)}, u32[]{:S(2)}, u32[]{:S(2)}) collective-permute-start(bf16[64,2176]{1,0:T(8,128)(2,1)S(1)} %get-tuple-element.41), channel_id=1, source_target_pairs={{0,4},{4,8},{8,12},{12,0},{1,5},{5,9},{9,13},{13,1},{2,6},{6,10},{... | collective-permute-start | bytes 835592 | tf_op jit(solution)/shard_map/ppermute | solution.py:439
  99.4 16.6 %collective-permute-start.23 = (bf16[64,2176]{1,0:T(8,128)(2,1)S(1)}, bf16[64,2176]{1,0:T(8,128)(2,1)S(1)}, u32[]{:S(2)}, u32[]{:S(2)}) collective-permute-start(bf16[64,2176]{1,0:T(8,128)(2,1)S(1)} %get-tuple-element.41), channel_id=1, source_target_pairs={{0,12},{4,0},{8,4},{12,8},{1,13},{5,1},{9,5},{13,9},{2,14},{6,2},{... | collective-permute-start | bytes 835592 | tf_op jit(solution)/shard_map/ppermute | solution.py:439
  103.2 21.5 %collective-permute-start.29 = (bf16[64,2176]{1,0:T(8,128)(2,1)S(1)}, bf16[64,2176]{1,0:T(8,128)(2,1)S(1)}, u32[]{:S(2)}, u32[]{:S(2)}) collective-permute-start(bf16[64,2176]{1,0:T(8,128)(2,1)S(1)} %get-tuple-element.41), channel_id=1, source_target_pairs={{0,8},{4,12},{8,0},{12,4},{1,9},{5,13},{9,1},{13,5},{2,10},{6,14},... | collective-permute-start | bytes 835592 | tf_op jit(solution)/shard_map/ppermute | solution.py:439
  103.2 7.6 %collective-permute-start.13 = (bf16[64,2176]{1,0:T(8,128)(2,1)S(1)}, bf16[64,2176]{1,0:T(8,128)(2,1)S(1)}, u32[]{:S(2)}, u32[]{:S(2)}) collective-permute-start(bf16[64,2176]{1,0:T(8,128)(2,1)S(1)} %get-tuple-element.41), channel_id=1, source_target_pairs={{0,2},{1,3},{2,0},{3,1},{4,6},{5,7},{6,4},{7,5},{8,10},{9,11},{10,... | collective-permute-start | bytes 835592 | tf_op jit(solution)/shard_map/ppermute | solution.py:445
  110.9 21.2 %collective-permute-start.14 = (bf16[128,2176]{1,0:T(8,128)(2,1)S(1)}, bf16[128,2176]{1,0:T(8,128)(2,1)S(1)}, u32[]{:S(2)}, u32[]{:S(2)}) collective-permute-start(bf16[128,2176]{1,0:T(8,128)(2,1)S(1)} %constant_dynamic-update-slice_fusion.own_ref), channel_id=1, source_target_pairs={{0,1},{1,0},{2,3},{3,2},{4,5},{5,4},{6,7},{7,6},{8,9},{9,8},{10,11... | collective-permute-start | bytes 1671176 | tf_op jit(solution)/shard_map/ppermute | solution.py:447
  110.9 15.3 %collective-permute-start.18 = (bf16[64,2176]{1,0:T(8,128)(2,1)S(1)}, bf16[64,2176]{1,0:T(8,128)(2,1)S(1)}, u32[]{:S(2)}, u32[]{:S(2)}) collective-permute-start(bf16[64,2176]{1,0:T(8,128)(2,1)S(1)} %collective-permute-done.17), channel_id=1, source_target_pairs={{0,2},{1,3},{2,0},{3,1},{4,6},{5,7},{6,4},{7,5},{8,10},{9,11},{10,... | collective-permute-start | bytes 835592 | tf_op jit(solution)/shard_map/ppermute | solution.py:445
  116.0 10.4 %collective-permute-start.24 = (bf16[64,2176]{1,0:T(8,128)(2,1)S(1)}, bf16[64,2176]{1,0:T(8,128)(2,1)S(1)}, u32[]{:S(2)}, u32[]{:S(2)}) collective-permute-start(bf16[64,2176]{1,0:T(8,128)(2,1)S(1)} %collective-permute-done.23), channel_id=1, source_target_pairs={{0,2},{1,3},{2,0},{3,1},{4,6},{5,7},{6,4},{7,5},{8,10},{9,11},{10,... | collective-permute-start | bytes 835592 | tf_op jit(solution)/shard_map/ppermute | solution.py:445
  124.7 7.2 %collective-permute-start.30 = (bf16[64,2176]{1,0:T(8,128)(2,1)S(1)}, bf16[64,2176]{1,0:T(8,128)(2,1)S(1)}, u32[]{:S(2)}, u32[]{:S(2)}) collective-permute-start(bf16[64,2176]{1,0:T(8,128)(2,1)S(1)} %collective-permute-done.29), channel_id=1, source_target_pairs={{0,2},{1,3},{2,0},{3,1},{4,6},{5,7},{6,4},{7,5},{8,10},{9,11},{10,... | collective-permute-start | bytes 835592 | tf_op jit(solution)/shard_map/ppermute | solution.py:445
  126.3 12.7 %collective-permute-start.19 = (bf16[128,2176]{1,0:T(8,128)(2,1)S(1)}, bf16[128,2176]{1,0:T(8,128)(2,1)S(1)}, u32[]{:S(2)}, u32[]{:S(2)}) collective-permute-start(bf16[128,2176]{1,0:T(8,128)(2,1)S(1)} %constant_dynamic-update-slice_fusion.2.own_ref), channel_id=1, source_target_pairs={{0,1},{1,0},{2,3},{3,2},{4,5},{5,4},{6,7},{7,6},{8,9},{9,8},{10,11... | collective-permute-start | bytes 1671176 | tf_op jit(solution)/shard_map/ppermute | solution.py:447
  126.4 19.0 %collective-permute-start.25 = (bf16[128,2176]{1,0:T(8,128)(2,1)S(1)}, bf16[128,2176]{1,0:T(8,128)(2,1)S(1)}, u32[]{:S(2)}, u32[]{:S(2)}) collective-permute-start(bf16[128,2176]{1,0:T(8,128)(2,1)S(1)} %constant_dynamic-update-slice_fusion.4.own_ref), channel_id=1, source_target_pairs={{0,1},{1,0},{2,3},{3,2},{4,5},{5,4},{6,7},{7,6},{8,9},{9,8},{10,11... | collective-permute-start | bytes 1671176 | tf_op jit(solution)/shard_map/ppermute | solution.py:447
  132.0 20.6 %collective-permute-start.31 = (bf16[128,2176]{1,0:T(8,128)(2,1)S(1)}, bf16[128,2176]{1,0:T(8,128)(2,1)S(1)}, u32[]{:S(2)}, u32[]{:S(2)}) collective-permute-start(bf16[128,2176]{1,0:T(8,128)(2,1)S(1)} %constant_dynamic-update-slice_fusion.6.own_ref), channel_id=1, source_target_pairs={{0,1},{1,0},{2,3},{3,2},{4,5},{5,4},{6,7},{7,6},{8,9},{9,8},{10,11... | collective-permute-start | bytes 1671176 | tf_op jit(solution)/shard_map/ppermute | solution.py:447
  138.4 20.6 %collective-permute-start.15 = (bf16[128,2048]{1,0:T(8,128)(2,1)S(1)}, bf16[128,2048]{1,0:T(8,128)(2,1)S(1)}, u32[]{:S(2)}, u32[]{:S(2)}) collective-permute-start(bf16[128,2048]{1,0:T(8,128)(2,1)S(1)} %get-tuple-element.46), channel_id=1, source_target_pairs={{0,1},{1,0},{2,3},{3,2},{4,5},{5,4},{6,7},{7,6},{8,9},{9,8},{10,11... | collective-permute-start | bytes 1572872 | tf_op jit(solution)/shard_map/ppermute | solution.py:449
  145.3 15.4 %collective-permute-start.20 = (bf16[128,2048]{1,0:T(8,128)(2,1)S(1)}, bf16[128,2048]{1,0:T(8,128)(2,1)S(1)}, u32[]{:S(2)}, u32[]{:S(2)}) collective-permute-start(bf16[128,2048]{1,0:T(8,128)(2,1)S(1)} %get-tuple-element.48), channel_id=1, source_target_pairs={{0,1},{1,0},{2,3},{3,2},{4,5},{5,4},{6,7},{7,6},{8,9},{9,8},{10,11... | collective-permute-start | bytes 1572872 | tf_op jit(solution)/shard_map/ppermute | solution.py:449
  151.9 9.5 %collective-permute-start.26 = (bf16[128,2048]{1,0:T(8,128)(2,1)S(1)}, bf16[128,2048]{1,0:T(8,128)(2,1)S(1)}, u32[]{:S(2)}, u32[]{:S(2)}) collective-permute-start(bf16[128,2048]{1,0:T(8,128)(2,1)S(1)} %get-tuple-element.50), channel_id=1, source_target_pairs={{0,1},{1,0},{2,3},{3,2},{4,5},{5,4},{6,7},{7,6},{8,9},{9,8},{10,11... | collective-permute-start | bytes 1572872 | tf_op jit(solution)/shard_map/ppermute | solution.py:449
  158.9 4.3 %collective-permute-start.32 = (bf16[128,2048]{1,0:T(8,128)(2,1)S(1)}, bf16[128,2048]{1,0:T(8,128)(2,1)S(1)}, u32[]{:S(2)}, u32[]{:S(2)}) collective-permute-start(bf16[128,2048]{1,0:T(8,128)(2,1)S(1)} %get-tuple-element.52), channel_id=1, source_target_pairs={{0,1},{1,0},{2,3},{3,2},{4,5},{5,4},{6,7},{7,6},{8,9},{9,8},{10,11... | collective-permute-start | bytes 1572872 | tf_op jit(solution)/shard_map/ppermute | solution.py:449
  159.1 28.4 %collective-permute-start.16 = (bf16[64,2048]{1,0:T(8,128)(2,1)S(1)}, bf16[64,2048]{1,0:T(8,128)(2,1)S(1)}, u32[]{:S(2)}, u32[]{:S(2)}) collective-permute-start(bf16[64,2048]{1,0:T(8,128)(2,1)S(1)} %slice.71), channel_id=1, source_target_pairs={{0,2},{1,3},{2,0},{3,1},{4,6},{5,7},{6,4},{7,5},{8,10},{9,11},{10,... | collective-permute-start | bytes 786440 | tf_op jit(solution)/shard_map/ppermute | solution.py:453
  160.8 13.1 %collective-permute-start.21 = (bf16[64,2048]{1,0:T(8,128)(2,1)S(1)}, bf16[64,2048]{1,0:T(8,128)(2,1)S(1)}, u32[]{:S(2)}, u32[]{:S(2)}) collective-permute-start(bf16[64,2048]{1,0:T(8,128)(2,1)S(1)} %slice.70), channel_id=1, source_target_pairs={{0,2},{1,3},{2,0},{3,1},{4,6},{5,7},{6,4},{7,5},{8,10},{9,11},{10,... | collective-permute-start | bytes 786440 | tf_op jit(solution)/shard_map/ppermute | solution.py:453
  161.6 18.0 %collective-permute-start.27 = (bf16[64,2048]{1,0:T(8,128)(2,1)S(1)}, bf16[64,2048]{1,0:T(8,128)(2,1)S(1)}, u32[]{:S(2)}, u32[]{:S(2)}) collective-permute-start(bf16[64,2048]{1,0:T(8,128)(2,1)S(1)} %slice.69), channel_id=1, source_target_pairs={{0,2},{1,3},{2,0},{3,1},{4,6},{5,7},{6,4},{7,5},{8,10},{9,11},{10,... | collective-permute-start | bytes 786440 | tf_op jit(solution)/shard_map/ppermute | solution.py:453
  163.3 21.4 %collective-permute-start.33 = (bf16[64,2048]{1,0:T(8,128)(2,1)S(1)}, bf16[64,2048]{1,0:T(8,128)(2,1)S(1)}, u32[]{:S(2)}, u32[]{:S(2)}) collective-permute-start(bf16[64,2048]{1,0:T(8,128)(2,1)S(1)} %slice.68), channel_id=1, source_target_pairs={{0,2},{1,3},{2,0},{3,1},{4,6},{5,7},{6,4},{7,5},{8,10},{9,11},{10,... | collective-permute-start | bytes 786440 | tf_op jit(solution)/shard_map/ppermute | solution.py:453
  174.0 13.5 %collective-permute-start.22 = (bf16[64,2048]{1,0:T(8,128)(2,1)S(1)}, bf16[64,2048]{1,0:T(8,128)(2,1)S(1)}, u32[]{:S(2)}, u32[]{:S(2)}) collective-permute-start(bf16[64,2048]{1,0:T(8,128)(2,1)S(1)} %fusion.2), channel_id=1, source_target_pairs={{0,12},{4,0},{8,4},{12,8},{1,13},{5,1},{9,5},{13,9},{2,14},{6,2},{... | collective-permute-start | bytes 786440 | tf_op jit(solution)/shard_map/ppermute | solution.py:455
  179.6 10.8 %collective-permute-start.28 = (bf16[64,2048]{1,0:T(8,128)(2,1)S(1)}, bf16[64,2048]{1,0:T(8,128)(2,1)S(1)}, u32[]{:S(2)}, u32[]{:S(2)}) collective-permute-start(bf16[64,2048]{1,0:T(8,128)(2,1)S(1)} %fusion.1), channel_id=1, source_target_pairs={{0,4},{4,8},{8,12},{12,0},{1,5},{5,9},{9,13},{13,1},{2,6},{6,10},{... | collective-permute-start | bytes 786440 | tf_op jit(solution)/shard_map/ppermute | solution.py:455
  184.8 15.6 %collective-permute-start.34 = (bf16[64,2048]{1,0:T(8,128)(2,1)S(1)}, bf16[64,2048]{1,0:T(8,128)(2,1)S(1)}, u32[]{:S(2)}, u32[]{:S(2)}) collective-permute-start(bf16[64,2048]{1,0:T(8,128)(2,1)S(1)} %fusion), channel_id=1, source_target_pairs={{0,8},{4,12},{8,0},{12,4},{1,9},{5,13},{9,1},{13,5},{2,10},{6,14},... | collective-permute-start | bytes 786440 | tf_op jit(solution)/shard_map/ppermute | solution.py:455
  (7 other events, 6.6 us)

commit v3 on v2

--- a/solution.py
+++ b/solution.py
@@ -142,9 +142,12 @@
     return lax.optimization_barrier((values, ready))[0]
 
 
-def far_order(count):
-    order = [k for pair in zip(range(1, count), range(count - 1, 0, -1)) for k in pair]
-    return list(dict.fromkeys(order))
+def ring_order(count):
+    return list(range(1, count // 2 + 1)) + list(range(count - 1, count // 2, -1))
+
+
+def carrier(count, k):
+    return (k - 1, 1) if k <= count // 2 else ((k + 1) % count, count - 1)
 
 
 def mix(mixer_input, step_raw, state_maps, decay_rate, skip_gain, out_weight):
@@ -152,11 +155,13 @@
     groups = channels // 128
     states = decay_rate.shape[0]
     seq_count = lax.axis_size("seq")
-    order = far_order(seq_count)
+    order = ring_order(seq_count)
     swap = [(0, 1), (1, 0)]
     half = out_weight.shape[0] // 2
-    mine = lax.dynamic_slice_in_dim(out_weight, lax.axis_index("groups") * half, half, 0)
-    direct = {order[0]: lax.ppermute(mine, "seq", shift(seq_count, order[0]))}
+    group = lax.axis_index("groups")
+    mine = lax.dynamic_slice_in_dim(out_weight, group * half, half, 0)
+    extra = lax.dynamic_slice_in_dim(out_weight, (1 - group) * half, half // 2, 0)
+    direct = {1: lax.ppermute(mine, "seq", shift(seq_count, 1))}
 
     maps = state_maps.reshape(2 * states, rows).astype(f32)
     shape = jax.ShapeDtypeStruct
@@ -174,13 +179,22 @@
         name="ends",
     )(maps, step_raw, mixer_input, decay_rate)
     packs = {0: pack}
-    for k in order:
+    for k in range(1, seq_count):
         packs[k] = lax.ppermute(pack, "seq", shift(seq_count, k))
     packs = [packs[k] for k in range(seq_count)]
-    rest = after(mine, packs)
+
+    direct[0], direct[1], extra = after((mine, direct[1], extra), packs)
     for k in order[1:]:
-        direct[k] = lax.ppermute(rest, "seq", shift(seq_count, k))
-    other = {k: lax.ppermute(direct[k], "groups", swap) for k in order}
+        source, step_size = carrier(seq_count, k)
+        direct[k] = lax.ppermute(direct[source], "seq", shift(seq_count, step_size))
+    last = order[-1]
+    direct_more = lax.ppermute(extra, "seq", shift(seq_count, last))
+    blocks = []
+    for k in order[:-1]:
+        other = lax.ppermute(direct[k], "groups", swap)
+        blocks.append((k, ((1, 0, direct[k]), (2, 0, other))))
+    other = lax.ppermute(direct[last][half // 2 :], "groups", swap)
+    blocks.append((last, ((1, 0, direct[last]), (2, 0, direct_more), (2, half // 2, other))))
 
     mixed = pl.pallas_call(
         functools.partial(scan_kernel, seq_count),
@@ -195,7 +209,7 @@
         compiler_params=pltpu.CompilerParams(vmem_limit_bytes=12 << 20),
         name="scan",
     )(maps, step, drive, decay_rate, mixer_input, skip_gain[None, :], *packs)
-    return mixed, [(k, direct[k], other[k]) for k in order]
+    return mixed, blocks
 
 
 def project_kernel(kinds, mixed_ref, *refs):
@@ -220,22 +234,24 @@
         ]
         at = 0
         used = 0
-        for split in kinds:
+        for piece in kinds:
             width = refs[used].shape[1]
-            if split:
-                value = jnp.dot(parts[1], refs[used][...], preferred_element_type=f32)
-                value += jnp.dot(parts[2], refs[used + 1][...], preferred_element_type=f32)
-            else:
-                value = jnp.dot(parts[0], refs[used][...], preferred_element_type=f32)
+            value = None
+            for which, start in piece:
+                depth = refs[used].shape[0]
+                term = jnp.dot(
+                    parts[which][:, start : start + depth], refs[used][...], preferred_element_type=f32
+                )
+                value = term if value is None else value + term
+                used += 1
             to_ref[:, at : at + width] = value
             at += width
-            used += 2 if split else 1
 
 
 def project(mixed, pieces):
-    kinds = tuple(len(piece) == 2 for piece in pieces)
-    arrays = [array for piece in pieces for array in piece]
-    width = sum(piece[0].shape[1] for piece in pieces)
+    kinds = tuple(tuple(part[:2] for part in piece) for piece in pieces)
+    arrays = [part[2] for piece in pieces for part in piece]
+    width = sum(piece[0][2].shape[1] for piece in pieces)
     out = jax.ShapeDtypeStruct((mixed.shape[0] // 2, width), f32)
     return pl.pallas_call(
         functools.partial(project_kernel, kinds),
@@ -303,7 +319,11 @@
     mean_sq = jnp.mean(stream * stream, axis=1, keepdims=True)
     normed = (stream * lax.rsqrt(mean_sq + 1e-05) * gain_ref[...]).astype(bf16)
     packed_ref[:, :width] = normed
-    logits = jnp.dot(normed, router_ref[...], preferred_element_type=f32)
+    lane = lax.broadcasted_iota(jnp.int32, (rows, 128), 1)
+    logits = jnp.zeros((rows, 128), f32)
+    for e in range(experts):
+        product = normed.astype(f32) * router_ref[e : e + 1, :].astype(f32)
+        logits = jnp.where(lane == e, jnp.sum(product, axis=1, keepdims=True), logits)
     row, column = (lax.broadcasted_iota(jnp.int32, (rows, rows), d) for d in range(2))
     same = jnp.where(row == column, 1.0, 0.0).astype(bf16)
     name = lax.broadcasted_iota(jnp.int32, (128, rows), 0)
@@ -326,8 +346,9 @@
     packed_ref[:, width:] = lanes.astype(bf16)
 
 
-def route(sets, residual, norm_gain, router, experts, expert_ids):
+def route(sets, residual, norm_gain, router_weight, expert_ids):
     rows, width = residual.shape
+    experts = router_weight.shape[1]
     shape = jax.ShapeDtypeStruct
     terms = [term for _, group in sets for term in group]
     kinds = tuple((tuple(ks), len(group)) for ks, group in sets)
@@ -339,7 +360,7 @@
         scratch_shapes=[pltpu.VMEM((rows, width), f32)],
         compiler_params=pltpu.CompilerParams(vmem_limit_bytes=8 << 20),
         name="route",
-    )(*terms, residual, norm_gain[None, :], router, expert_ids.T)
+    )(*terms, residual, norm_gain[None, :], router_weight.T, expert_ids.T)
 
 
 def expert_kernel(capacity, block_rows, experts, tile, own_ref, mate_ref, gate_ref, up_ref, down_ref, *rest):
@@ -432,11 +453,12 @@
     chips = exp_count // 2
     rows = packed.shape[0]
     partner = [(i, i ^ 1) for i in range(exp_count)]
-    order = far_order(seq_count)
+    order = ring_order(seq_count)
 
     planes = {0: packed}
     for k in order:
-        planes[k] = lax.ppermute(packed, "seq", shift(seq_count, k))
+        source, step_size = carrier(seq_count, k)
+        planes[k] = lax.ppermute(planes[source], "seq", shift(seq_count, step_size))
 
     total = None
     for k in [0] + order:
@@ -473,18 +495,16 @@
     down_weight,
 ):
     experts = router_weight.shape[1]
-    router = jnp.pad(router_weight, ((0, 0), (0, 128 - experts)))
-    skip_gain, router, expert_ids = lax.optimization_barrier((skip_gain, router, expert_ids))
     mixed, blocks = mix(mixer_input, step_raw, state_maps, decay_rate, skip_gain, out_weight)
     weights = (gate_weight, up_weight, down_weight)
     held = [hold(weight, mixed) for weight in weights]
     order = [0] + [block[0] for block in blocks]
-    pieces = [(out_weight,)] + [block[1:] for block in blocks]
+    pieces = [((0, 0, out_weight),)] + [block[1] for block in blocks]
     sets = []
     for part in (slice(0, -1), slice(-1, None)):
         keep, away = project(mixed, pieces[part])
         sets.append((order[part], sum_to_owner(keep, away)))
-    stream, packed = route(sets, residual, norm_gain, router, experts, expert_ids)
+    stream, packed = route(sets, residual, norm_gain, router_weight, expert_ids)
     capacity = max(2, 8 * residual.shape[0] // (3 * experts))
     added = experts_sum(packed, experts, capacity, *held)
     return (stream.astype(f32) + added).astype(bf16)

time: 202 us -> 180 us (0.89)
  waiting for transfers between devices: 93.3 us -> 80.2 us
  starting transfers between devices: 40.4 us -> 35 us
    ppermute x9 -> x10, waiting for transfers between devices: 48 us -> 20.5 us  [the longest x2 11.2 us: mix(): direct[k] = lax.ppermute(direct[source], 'seq', shift(seq_count, step_size))]
    ppermute x4, waiting for transfers between devices: 11.1 us -> 23.9 us  [experts_sum(): row.append(lax.ppermute(planes[k], 'exp', shift(exp_count, 2 * j)))]
    ppermute x3, starting transfers between devices: 4.67 us -> 0.48 us  [experts_sum(): lax.ppermute(mine.astype(bf16), 'seq', shift(seq_count, seq_count - k))]
    ppermute x4, waiting for transfers between devices: 18.8 us -> 16.4 us  [experts_sum(): lax.ppermute(leaving, 'exp', shift(exp_count, exp_count - 2 * j))]
    ppermute x3, waiting for transfers between devices: 12.9 us -> 15.2 us  [experts_sum(): lax.ppermute(mine.astype(bf16), 'seq', shift(seq_count, seq_count - k))]
    unnamed x45 -> x46, local copies, waits for them, and re-layouts: 16.5 us -> 14.8 us
    ppermute x9 -> x10, starting transfers between devices: 13.2 us -> 13.9 us  [the longest x3 3.83 us: experts_sum(): planes[k] = lax.ppermute(planes[source], 'seq', shift(seq_count, step_size))]
  transfers between devices with their start and end apart: 35 -> 36, of which waited for: 16 -> 16; matrix products, arithmetic and copies ran while one was open for 3% -> 1% of each run, Pallas kernels for 19% -> 24%
where the time goes in v3:
time: 180 us; the launch traced here: 179 us
  waiting for transfers between devices  80.2 us (45%)
  Pallas kernels  43.7 us (24%)
  starting transfers between devices  35 us (19%)
  local copies, waits for them, and re-layouts  17.9 us (10%)
  other arithmetic  2.19 us (1%)
    pallas_call x4, Pallas kernels, expert_part(): pl.pallas_call(functools.partial(expert_kernel, capacity, block_rows, exp...  25.6 us
    ppermute x4, waiting for transfers between devices, experts_sum(): row.append(lax.ppermute(planes[k], 'exp', shift(exp_count, 2 * j)))  23.9 us
    ppermute x4, waiting for transfers between devices, experts_sum(): lax.ppermute(leaving, 'exp', shift(exp_count, exp_count - 2 * j))  16.4 us
    ppermute x3, waiting for transfers between devices, experts_sum(): lax.ppermute(mine.astype(bf16), 'seq', shift(seq_count, seq_count - k))  15.2 us
    unnamed x46, local copies, waits for them, and re-layouts  14.8 us
    ppermute x2, waiting for transfers between devices, mix(): direct[k] = lax.ppermute(direct[source], 'seq', shift(seq_count, step_size))  11.2 us
    pallas_call x1, Pallas kernels, mix(): pl.pallas_call(functools.partial(scan_kernel, seq_count), out_shape=shape...  7.49 us
    ppermute x1, waiting for transfers between devices, mix(): direct_more = lax.ppermute(extra, 'seq', shift(seq_count, last))  6.73 us
  transfers between devices with their start and end apart: 36, of which 16 were waited for; matrix products, arithmetic and copies ran while one was open for 1% of the time, Pallas kernels for 24%

profile of v3, /device:TPU:0, one launch (start us, length us, event | category | flops | bytes accessed | tf_op | source)
XLA Modules:
  0.0 179.5 jit_solution(587195685222614366)
XLA Ops:
  0.0 1.9 %constant_dynamic-slice_fusion.1 = bf16[512,512]{1,0:T(8,128)(2,1)} fusion(bf16[1024,512]{1,0:T(8,128)(2,1)} %refs_0_.1, s32[]{:T(128)S(6)} %select_n.6), kind=kLoop, calls=%fused_computation.30 | loop fusion | bytes 1048580 | tf_op jit(solution)/shard_map/dynamic_slice | solution.py:162
  1.9 3.1 %collective-permute-start.3 = (bf16[512,512]{1,0:T(8,128)(2,1)}, bf16[512,512]{1,0:T(8,128)(2,1)}, u32[]{:S(2)}, u32[]{:S(2)}) collective-permute-start(bf16[512,512]{1,0:T(8,128)(2,1)} %constant_dynamic-slice_fusion.1), channel_id=1, source_target_pairs={{0,4},{4,8},{8,12},{12,0},{1,5},{5,9},{9,13},{13,1},{2,6},{6,10},{... | collective-permute-start | bytes 1572872 | tf_op jit(solution)/shard_map/ppermute | solution.py:164
  5.6 1.2 copy-done
  6.9 1.0 copy-done.7
  8.7 5.7 %ends.1 = (bf16[2,144,128]{2,1,0:T(8,128)(2,1)S(1)}, f32[2048,128]{1,0:T(8,128)S(1)}, f32[2048,128]{1,0:T(8,128)S(1)}) custom-call(f32[32,256]{1,0:T(8,128)S(1)} %bitcast_convert_fusion.maps_ref, bf16[256,1024]{1,0:T(8,128)(2,1)S(1)} %copy-done.7, bf16[2,256,1024]{2,1,0:T(8,128)(2,1)S(1)} %copy-done, f32[16,1024]{1,0:T(8,128)S(1)} %copy-done.8), custom_call_target="tpu_custom_call" | custom-call | tf_op jit(solution)/shard_map/ends/pallas_call | solution.py:168
  14.5 1.0 copy-done.3
  15.5 1.0 copy-done.5
  16.5 1.6 collective-permute-start
  18.1 1.3 collective-permute-start.1
  19.3 2.7 %collective-permute-start.2 = (bf16[2,144,128]{2,1,0:T(8,128)(2,1)S(1)}, bf16[2,144,128]{2,1,0:T(8,128)(2,1)S(1)}, u32[]{:S(2)}, u32[]{:S(2)}) collective-permute-start(bf16[2,144,128]{2,1,0:T(8,128)(2,1)S(1)} %get-tuple-element.30.rest_0_), channel_id=1, source_target_pairs={{0,12},{4,0},{8,4},{12,8},{1,13},{5,1},{9,5},{13,9},{2,14},{6,2},{... | collective-permute-start | bytes 221192 | tf_op jit(solution)/shard_map/ppermute | solution.py:183
  23.5 2.4 %collective-permute-done.1.rest_2_ = bf16[2,144,128]{2,1,0:T(8,128)(2,1)S(1)} collective-permute-done((bf16[2,144,128]{2,1,0:T(8,128)(2,1)S(1)}, bf16[2,144,128]{2,1,0:T(8,128)(2,1)S(1)}, u32[]{:S(2)}, u32[]{:S(2)}) %collective-permute-start.1) | collective-permute-done | bytes 73760 | tf_op jit(solution)/shard_map/ppermute | solution.py:183
  25.9 1.4 collective-permute-start.5
  27.3 1.5 collective-permute-start.4
  28.9 11.2 %collective-permute-done.5.refs_3_ = bf16[512,512]{1,0:T(8,128)(2,1)S(1)} collective-permute-done((bf16[512,512]{1,0:T(8,128)(2,1)}, bf16[512,512]{1,0:T(8,128)(2,1)S(1)}, u32[]{:S(2)}, u32[]{:S(2)}) %collective-permute-start.5) | collective-permute-done | bytes 524320 | tf_op jit(solution)/shard_map/ppermute | solution.py:189
  40.0 1.4 collective-permute-start.6
  42.1 1.2 copy-done.1
  43.4 1.2 copy-done.4
  44.6 1.2 copy-done.6
  47.3 7.5 %scan.1.mixed_ref = bf16[256,1024]{1,0:T(8,128)(2,1)S(1)} custom-call(f32[32,256]{1,0:T(8,128)S(1)} %bitcast_convert_fusion.maps_ref, f32[2048,128]{1,0:T(8,128)S(1)} %copy-done.4, f32[2048,128]{1,0:T(8,128)S(1)} %copy-done.6, f32[16,1024]{1,0:T(8,128)S(1)} %copy-done.9, bf16[2,256,1024]{2,1,0:T(8,128)(2,1)S(1)} %copy-done.1, f32[1,1024]{1,0:T(1,128)S(1)} %bitcast.15, ...), custom_call_target="tpu_custom_call" | custom-call | tf_op jit(solution)/shard_map/scan/pallas_call | solution.py:199
  54.9 1.4 copy-done.2
  56.3 2.2 %project.2 = (f32[128,1536]{1,0:T(8,128)S(1)}, f32[128,1536]{1,0:T(8,128)S(1)}) custom-call(bf16[256,1024]{1,0:T(8,128)(2,1)S(1)} %scan.1.mixed_ref, bf16[1024,512]{1,0:T(8,128)(2,1)S(1)} %copy-done.2, bf16[512,512]{1,0:T(8,128)(2,1)} %collective-permute-done.3.refs_1_, bf16[512,512]{1,0:T(8,128)(2,1)S(1)} %collective-permute-done.4.refs_2_, ...), custom_call_target="tpu_custom_call" | custom-call | flops 805306368 | bytes 3145728 | tf_op jit(solution)/shard_map/project/pallas_call | solution.py:256
  58.5 1.4 collective-permute-start.10
  60.5 6.7 %collective-permute-done.10.refs_1_ = bf16[256,512]{1,0:T(8,128)(2,1)S(1)} collective-permute-done((bf16[256,512]{1,0:T(8,128)(2,1)S(1)}, bf16[256,512]{1,0:T(8,128)(2,1)S(1)}, u32[]{:S(2)}, u32[]{:S(2)}) %collective-permute-start.10) | collective-permute-done | bytes 262176 | tf_op jit(solution)/shard_map/ppermute | solution.py:191
  67.2 1.1 collective-permute-done.11.refs_2_
  69.0 1.6 collective-permute-start.8
  70.6 1.4 collective-permute-start.13
  76.5 1.2 collective-permute-done.13.refs_5_
  79.3 3.1 %collective-permute-start.30 = (bf16[64,2176]{1,0:T(8,128)(2,1)S(1)}, bf16[64,2176]{1,0:T(8,128)(2,1)S(1)}, u32[]{:S(2)}, u32[]{:S(2)}) collective-permute-start(bf16[64,2176]{1,0:T(8,128)(2,1)S(1)} %get-tuple-element.39), channel_id=1, source_target_pairs={{0,12},{4,0},{8,4},{12,8},{1,13},{5,1},{9,5},{13,9},{2,14},{6,2},{... | collective-permute-start | bytes 835592 | tf_op jit(solution)/shard_map/ppermute | solution.py:461
  82.4 1.5 collective-permute-start.14
  83.9 6.1 %collective-permute-done.14 = bf16[64,2176]{1,0:T(8,128)(2,1)S(1)} collective-permute-done((bf16[64,2176]{1,0:T(8,128)(2,1)S(1)}, bf16[64,2176]{1,0:T(8,128)(2,1)S(1)}, u32[]{:S(2)}, u32[]{:S(2)}) %collective-permute-start.14) | collective-permute-done | bytes 278560 | tf_op jit(solution)/shard_map/ppermute | solution.py:467
  90.1 1.6 collective-permute-start.19
  91.7 1.4 collective-permute-done.30
  93.1 1.5 collective-permute-start.31
  94.6 5.1 %collective-permute-done.19 = bf16[64,2176]{1,0:T(8,128)(2,1)S(1)} collective-permute-done((bf16[64,2176]{1,0:T(8,128)(2,1)S(1)}, bf16[64,2176]{1,0:T(8,128)(2,1)S(1)}, u32[]{:S(2)}, u32[]{:S(2)}) %collective-permute-start.19) | collective-permute-done | bytes 278560 | tf_op jit(solution)/shard_map/ppermute | solution.py:467
  99.8 5.3 %collective-permute-done.31 = bf16[64,2176]{1,0:T(8,128)(2,1)S(1)} collective-permute-done((bf16[64,2176]{1,0:T(8,128)(2,1)S(1)}, bf16[64,2176]{1,0:T(8,128)(2,1)S(1)}, u32[]{:S(2)}, u32[]{:S(2)}) %collective-permute-start.31) | collective-permute-done | bytes 278560 | tf_op jit(solution)/shard_map/ppermute | solution.py:467
  105.2 1.6 collective-permute-start.25
  106.8 7.5 %collective-permute-done.25 = bf16[64,2176]{1,0:T(8,128)(2,1)S(1)} collective-permute-done((bf16[64,2176]{1,0:T(8,128)(2,1)S(1)}, bf16[64,2176]{1,0:T(8,128)(2,1)S(1)}, u32[]{:S(2)}, u32[]{:S(2)}) %collective-permute-start.25) | collective-permute-done | bytes 278560 | tf_op jit(solution)/shard_map/ppermute | solution.py:467
  114.4 6.3 %expert.4 = (f32[128,2048]{1,0:T(8,128)S(1)}, bf16[128,2048]{1,0:T(8,128)(2,1)S(1)}) custom-call(bf16[128,2176]{1,0:T(8,128)(2,1)S(1)} %constant_dynamic-update-slice_fusion.own_ref, bf16[128,2176]{1,0:T(8,128)(2,1)S(1)} %collective-permute-done.15.mate_ref, bf16[1,2048,1792]{2,1,0:T(8,128)(2,1)S(1)} %hold.3.gate_ref, ...), custom_call_target="tpu_custom_call" | custom-call | flops 3875536896 | bytes 22020096 | tf_op jit(solution)/shard_map/expert/pallas_call | solution.py:434
  121.3 6.3 %expert.5 = (f32[128,2048]{1,0:T(8,128)S(1)}, bf16[128,2048]{1,0:T(8,128)(2,1)S(1)}) custom-call(bf16[128,2176]{1,0:T(8,128)(2,1)S(1)} %constant_dynamic-update-slice_fusion.2.own_ref, bf16[128,2176]{1,0:T(8,128)(2,1)S(1)} %collective-permute-done.20.mate_ref, bf16[1,2048,1792]{2,1,0:T(8,128)(2,1)S(1)} %hold.3.gate_ref, ...), custom_call_target="tpu_custom_call" | custom-call | flops 3875536896 | bytes 22020096 | tf_op jit(solution)/shard_map/expert/pallas_call | solution.py:434
  127.8 6.6 %expert.7 = (f32[128,2048]{1,0:T(8,128)S(1)}, bf16[128,2048]{1,0:T(8,128)(2,1)S(1)}) custom-call(bf16[128,2176]{1,0:T(8,128)(2,1)S(1)} %constant_dynamic-update-slice_fusion.6.own_ref, bf16[128,2176]{1,0:T(8,128)(2,1)S(1)} %collective-permute-done.32.mate_ref, bf16[1,2048,1792]{2,1,0:T(8,128)(2,1)S(1)} %hold.3.gate_ref, ...), custom_call_target="tpu_custom_call" | custom-call | flops 3875536896 | bytes 22020096 | tf_op jit(solution)/shard_map/expert/pallas_call | solution.py:434
  135.1 1.6 collective-permute-start.17
  136.6 6.3 %expert.6 = (f32[128,2048]{1,0:T(8,128)S(1)}, bf16[128,2048]{1,0:T(8,128)(2,1)S(1)}) custom-call(bf16[128,2176]{1,0:T(8,128)(2,1)S(1)} %constant_dynamic-update-slice_fusion.4.own_ref, bf16[128,2176]{1,0:T(8,128)(2,1)S(1)} %collective-permute-done.26.mate_ref, bf16[1,2048,1792]{2,1,0:T(8,128)(2,1)S(1)} %hold.3.gate_ref, ...), custom_call_target="tpu_custom_call" | custom-call | flops 3875536896 | bytes 22020096 | tf_op jit(solution)/shard_map/expert/pallas_call | solution.py:434
  144.0 1.6 collective-permute-start.34
  145.5 6.9 %collective-permute-done.22 = bf16[64,2048]{1,0:T(8,128)(2,1)S(1)} collective-permute-done((bf16[64,2048]{1,0:T(8,128)(2,1)S(1)}, bf16[64,2048]{1,0:T(8,128)(2,1)S(1)}, u32[]{:S(2)}, u32[]{:S(2)}) %collective-permute-start.22) | collective-permute-done | bytes 262176 | tf_op jit(solution)/shard_map/ppermute | solution.py:475
  153.6 4.5 %collective-permute-done.34 = bf16[64,2048]{1,0:T(8,128)(2,1)S(1)} collective-permute-done((bf16[64,2048]{1,0:T(8,128)(2,1)S(1)}, bf16[64,2048]{1,0:T(8,128)(2,1)S(1)}, u32[]{:S(2)}, u32[]{:S(2)}) %collective-permute-start.34) | collective-permute-done | bytes 262176 | tf_op jit(solution)/shard_map/ppermute | solution.py:475
  158.2 5.0 %collective-permute-done.28 = bf16[64,2048]{1,0:T(8,128)(2,1)S(1)} collective-permute-done((bf16[64,2048]{1,0:T(8,128)(2,1)S(1)}, bf16[64,2048]{1,0:T(8,128)(2,1)S(1)}, u32[]{:S(2)}, u32[]{:S(2)}) %collective-permute-start.28) | collective-permute-done | bytes 262176 | tf_op jit(solution)/shard_map/ppermute | solution.py:475
  163.4 5.9 %collective-permute-done.35 = bf16[64,2048]{1,0:T(8,128)(2,1)S(1)} collective-permute-done((bf16[64,2048]{1,0:T(8,128)(2,1)S(1)}, bf16[64,2048]{1,0:T(8,128)(2,1)S(1)}, u32[]{:S(2)}, u32[]{:S(2)}) %collective-permute-start.35) | collective-permute-done | bytes 262176 | tf_op jit(solution)/shard_map/ppermute | solution.py:477
  169.2 9.3 %collective-permute-done.29 = bf16[64,2048]{1,0:T(8,128)(2,1)S(1)} collective-permute-done((bf16[64,2048]{1,0:T(8,128)(2,1)S(1)}, bf16[64,2048]{1,0:T(8,128)(2,1)S(1)}, u32[]{:S(2)}, u32[]{:S(2)}) %collective-permute-start.29) | collective-permute-done | bytes 262176 | tf_op jit(solution)/shard_map/ppermute | solution.py:477
  (107 shorter events, 17.6 us)
Async XLA Ops:
  1.9 70.2 %slice-start = ((s8[7340032]{0:T(1024)(128)(4,1)}), s8[3145728]{0:T(1024)(128)(4,1)S(1)}, s32[]{:S(2)}) async-start(s8[7340032]{0:T(1024)(128)(4,1)} %bitcast.7), calls=%async_computation | async-start | bytes 6291456
  1.9 24.0 %collective-permute-start.3 = (bf16[512,512]{1,0:T(8,128)(2,1)}, bf16[512,512]{1,0:T(8,128)(2,1)}, u32[]{:S(2)}, u32[]{:S(2)}) collective-permute-start(bf16[512,512]{1,0:T(8,128)(2,1)} %constant_dynamic-slice_fusion.1), channel_id=1, source_target_pairs={{0,4},{4,8},{8,12},{12,0},{1,5},{5,9},{9,13},{13,1},{2,6},{6,10},{... | collective-permute-start | bytes 1572872 | tf_op jit(solution)/shard_map/ppermute | solution.py:164
  5.6 1.2 copy-start
  16.5 7.0 %collective-permute-start = (bf16[2,144,128]{2,1,0:T(8,128)(2,1)S(1)}, bf16[2,144,128]{2,1,0:T(8,128)(2,1)S(1)}, u32[]{:S(2)}, u32[]{:S(2)}) collective-permute-start(bf16[2,144,128]{2,1,0:T(8,128)(2,1)S(1)} %get-tuple-element.30.rest_0_), channel_id=1, source_target_pairs={{0,4},{4,8},{8,12},{12,0},{1,5},{5,9},{9,13},{13,1},{2,6},{6,10},{... | collective-permute-start | bytes 221192 | tf_op jit(solution)/shard_map/ppermute | solution.py:183
  18.1 7.8 %collective-permute-start.1 = (bf16[2,144,128]{2,1,0:T(8,128)(2,1)S(1)}, bf16[2,144,128]{2,1,0:T(8,128)(2,1)S(1)}, u32[]{:S(2)}, u32[]{:S(2)}) collective-permute-start(bf16[2,144,128]{2,1,0:T(8,128)(2,1)S(1)} %get-tuple-element.30.rest_0_), channel_id=1, source_target_pairs={{0,8},{4,12},{8,0},{12,4},{1,9},{5,13},{9,1},{13,5},{2,10},{6,14},... | collective-permute-start | bytes 221192 | tf_op jit(solution)/shard_map/ppermute | solution.py:183
  19.3 6.6 %collective-permute-start.2 = (bf16[2,144,128]{2,1,0:T(8,128)(2,1)S(1)}, bf16[2,144,128]{2,1,0:T(8,128)(2,1)S(1)}, u32[]{:S(2)}, u32[]{:S(2)}) collective-permute-start(bf16[2,144,128]{2,1,0:T(8,128)(2,1)S(1)} %get-tuple-element.30.rest_0_), channel_id=1, source_target_pairs={{0,12},{4,0},{8,4},{12,8},{1,13},{5,1},{9,5},{13,9},{2,14},{6,2},{... | collective-permute-start | bytes 221192 | tf_op jit(solution)/shard_map/ppermute | solution.py:183
  25.9 14.1 %collective-permute-start.5 = (bf16[512,512]{1,0:T(8,128)(2,1)}, bf16[512,512]{1,0:T(8,128)(2,1)S(1)}, u32[]{:S(2)}, u32[]{:S(2)}) collective-permute-start(bf16[512,512]{1,0:T(8,128)(2,1)} %collective-permute-done.3.refs_1_), channel_id=1, source_target_pairs={{0,4},{4,8},{8,12},{12,0},{1,5},{5,9},{9,13},{13,1},{2,6},{6,10},{... | collective-permute-start | bytes 1572872 | tf_op jit(solution)/shard_map/ppermute | solution.py:189
  27.3 27.5 %collective-permute-start.4 = (bf16[512,512]{1,0:T(8,128)(2,1)}, bf16[512,512]{1,0:T(8,128)(2,1)S(1)}, u32[]{:S(2)}, u32[]{:S(2)}) collective-permute-start(bf16[512,512]{1,0:T(8,128)(2,1)} %collective-permute-done.3.refs_1_), channel_id=1, source_target_pairs={{0,16},{16,0},{1,17},{17,1},{2,18},{18,2},{3,19},{19,3},{4,20},{20... | collective-permute-start | bytes 1572872 | tf_op jit(solution)/shard_map/ppermute | solution.py:194
  40.0 14.8 %collective-permute-start.6 = (bf16[512,512]{1,0:T(8,128)(2,1)S(1)}, bf16[512,512]{1,0:T(8,128)(2,1)S(1)}, u32[]{:S(2)}, u32[]{:S(2)}) collective-permute-start(bf16[512,512]{1,0:T(8,128)(2,1)S(1)} %collective-permute-done.5.refs_3_), channel_id=1, source_target_pairs={{0,16},{16,0},{1,17},{17,1},{2,18},{18,2},{3,19},{19,3},{4,20},{20... | collective-permute-start | bytes 1572872 | tf_op jit(solution)/shard_map/ppermute | solution.py:194
  41.4 18.5 %collective-permute-start.9 = (bf16[512,512]{1,0:T(8,128)(2,1)}, bf16[512,512]{1,0:T(8,128)(2,1)S(1)}, u32[]{:S(2)}, u32[]{:S(2)}) collective-permute-start(bf16[512,512]{1,0:T(8,128)(2,1)} %constant_dynamic-slice_fusion.1), channel_id=1, source_target_pairs={{0,12},{4,0},{8,4},{12,8},{1,13},{5,1},{9,5},{13,9},{2,14},{6,2},{... | collective-permute-start | bytes 1572872 | tf_op jit(solution)/shard_map/ppermute | solution.py:189
  54.8 17.2 %slice-start.1 = ((s8[7340032]{0:T(1024)(128)(4,1)}), s8[4194304]{0:T(1024)(128)(4,1)S(1)}, s32[]{:S(2)}) async-start(s8[7340032]{0:T(1024)(128)(4,1)} %bitcast.7), calls=%async_computation.1 | async-start | bytes 8388608
  54.9 1.4 copy-start.2
  58.5 10.4 %collective-permute-start.7 = (f32[128,1536]{1,0:T(8,128)S(1)}, f32[128,1536]{1,0:T(8,128)S(1)}, u32[]{:S(2)}, u32[]{:S(2)}) collective-permute-start(f32[128,1536]{1,0:T(8,128)S(1)} %get-tuple-element.33), channel_id=1, source_target_pairs={{0,1},{1,0},{2,3},{3,2},{4,5},{5,4},{6,7},{7,6},{8,9},{9,8},{10,11... | collective-permute-start | bytes 2359304 | tf_op jit(solution)/shard_map/ppermute | solution.py:281
  58.5 8.7 %collective-permute-start.10 = (bf16[256,512]{1,0:T(8,128)(2,1)S(1)}, bf16[256,512]{1,0:T(8,128)(2,1)S(1)}, u32[]{:S(2)}, u32[]{:S(2)}) collective-permute-start(bf16[256,512]{1,0:T(8,128)(2,1)S(1)} %constant_dynamic-slice_fusion), channel_id=1, source_target_pairs={{0,12},{4,0},{8,4},{12,8},{1,13},{5,1},{9,5},{13,9},{2,14},{6,2},{... | collective-permute-start | bytes 786440 | tf_op jit(solution)/shard_map/ppermute | solution.py:191
  59.9 8.4 %collective-permute-start.11 = (bf16[256,512]{1,0:T(8,128)(2,1)S(1)}, bf16[256,512]{1,0:T(8,128)(2,1)S(1)}, u32[]{:S(2)}, u32[]{:S(2)}) collective-permute-start(bf16[256,512]{1,0:T(8,128)(2,1)S(1)} %slice.40), channel_id=1, source_target_pairs={{0,16},{16,0},{1,17},{17,1},{2,18},{18,2},{3,19},{19,3},{4,20},{20... | collective-permute-start | bytes 786440 | tf_op jit(solution)/shard_map/ppermute | solution.py:196
  68.8 1.7 collective-permute-start.12
  69.0 8.7 %collective-permute-start.8 = (bf16[64,1536]{1,0:T(8,128)(2,1)S(1)}, bf16[64,1536]{1,0:T(8,128)(2,1)S(1)}, u32[]{:S(2)}, u32[]{:S(2)}) collective-permute-start(bf16[64,1536]{1,0:T(8,128)(2,1)S(1)} %leave.2), channel_id=1, source_target_pairs={{0,2},{1,3},{2,0},{3,1},{4,6},{5,7},{6,4},{7,5},{8,10},{9,11},{10,... | collective-permute-start | bytes 589832 | tf_op jit(solution)/shard_map/ppermute | solution.py:293
  70.5 2.2 %slice-start.2 = ((s8[7340032]{0:T(1024)(128)(4,1)}), s8[4194304]{0:T(1024)(128)(4,1)S(1)}, s32[]{:S(2)}) async-start(s8[7340032]{0:T(1024)(128)(4,1)} %bitcast.9), calls=%async_computation.2 | async-start | bytes 8388608
  70.6 3.2 %slice-start.3 = ((s8[7340032]{0:T(1024)(128)(4,1)}), s8[3145728]{0:T(1024)(128)(4,1)S(1)}, s32[]{:S(2)}) async-start(s8[7340032]{0:T(1024)(128)(4,1)} %bitcast.9), calls=%async_computation.3 | async-start | bytes 6291456
  70.6 7.1 %collective-permute-start.13 = (bf16[64,512]{1,0:T(8,128)(2,1)S(1)}, bf16[64,512]{1,0:T(8,128)(2,1)S(1)}, u32[]{:S(2)}, u32[]{:S(2)}) collective-permute-start(bf16[64,512]{1,0:T(8,128)(2,1)S(1)} %leave.3), channel_id=1, source_target_pairs={{0,2},{1,3},{2,0},{3,1},{4,6},{5,7},{6,4},{7,5},{8,10},{9,11},{10,... | collective-permute-start | bytes 196616 | tf_op jit(solution)/shard_map/ppermute | solution.py:293
  72.0 3.1 %slice-start.4 = ((s8[7340032]{0:T(1024)(128)(4,1)}), s8[4194304]{0:T(1024)(128)(4,1)S(1)}, s32[]{:S(2)}) async-start(s8[7340032]{0:T(1024)(128)(4,1)} %bitcast.11), calls=%async_computation.4 | async-start | bytes 8388608
  73.7 2.3 %slice-start.5 = ((s8[7340032]{0:T(1024)(128)(4,1)}), s8[3145728]{0:T(1024)(128)(4,1)S(1)}, s32[]{:S(2)}) async-start(s8[7340032]{0:T(1024)(128)(4,1)} %bitcast.11), calls=%async_computation.5 | async-start | bytes 6291456
  76.0 1.7 copy-start.10
  76.0 1.7 copy-start.11
  76.0 1.7 copy-start.12
  76.0 1.8 copy-start.14
  78.5 11.6 %collective-permute-start.18 = (bf16[64,2176]{1,0:T(8,128)(2,1)S(1)}, bf16[64,2176]{1,0:T(8,128)(2,1)S(1)}, u32[]{:S(2)}, u32[]{:S(2)}) collective-permute-start(bf16[64,2176]{1,0:T(8,128)(2,1)S(1)} %get-tuple-element.39), channel_id=1, source_target_pairs={{0,4},{4,8},{8,12},{12,0},{1,5},{5,9},{9,13},{13,1},{2,6},{6,10},{... | collective-permute-start | bytes 835592 | tf_op jit(solution)/shard_map/ppermute | solution.py:461
  79.3 13.9 %collective-permute-start.30 = (bf16[64,2176]{1,0:T(8,128)(2,1)S(1)}, bf16[64,2176]{1,0:T(8,128)(2,1)S(1)}, u32[]{:S(2)}, u32[]{:S(2)}) collective-permute-start(bf16[64,2176]{1,0:T(8,128)(2,1)S(1)} %get-tuple-element.39), channel_id=1, source_target_pairs={{0,12},{4,0},{8,4},{12,8},{1,13},{5,1},{9,5},{13,9},{2,14},{6,2},{... | collective-permute-start | bytes 835592 | tf_op jit(solution)/shard_map/ppermute | solution.py:461
  82.4 7.6 %collective-permute-start.14 = (bf16[64,2176]{1,0:T(8,128)(2,1)S(1)}, bf16[64,2176]{1,0:T(8,128)(2,1)S(1)}, u32[]{:S(2)}, u32[]{:S(2)}) collective-permute-start(bf16[64,2176]{1,0:T(8,128)(2,1)S(1)} %get-tuple-element.39), channel_id=1, source_target_pairs={{0,2},{1,3},{2,0},{3,1},{4,6},{5,7},{6,4},{7,5},{8,10},{9,11},{10,... | collective-permute-start | bytes 835592 | tf_op jit(solution)/shard_map/ppermute | solution.py:467
  90.0 24.4 %collective-permute-start.15 = (bf16[128,2176]{1,0:T(8,128)(2,1)S(1)}, bf16[128,2176]{1,0:T(8,128)(2,1)S(1)}, u32[]{:S(2)}, u32[]{:S(2)}) collective-permute-start(bf16[128,2176]{1,0:T(8,128)(2,1)S(1)} %constant_dynamic-update-slice_fusion.own_ref), channel_id=1, source_target_pairs={{0,1},{1,0},{2,3},{3,2},{4,5},{5,4},{6,7},{7,6},{8,9},{9,8},{10,11... | collective-permute-start | bytes 1671176 | tf_op jit(solution)/shard_map/ppermute | solution.py:469
  90.1 9.6 %collective-permute-start.19 = (bf16[64,2176]{1,0:T(8,128)(2,1)S(1)}, bf16[64,2176]{1,0:T(8,128)(2,1)S(1)}, u32[]{:S(2)}, u32[]{:S(2)}) collective-permute-start(bf16[64,2176]{1,0:T(8,128)(2,1)S(1)} %collective-permute-done.18), channel_id=1, source_target_pairs={{0,2},{1,3},{2,0},{3,1},{4,6},{5,7},{6,4},{7,5},{8,10},{9,11},{10,... | collective-permute-start | bytes 835592 | tf_op jit(solution)/shard_map/ppermute | solution.py:467
  91.7 13.6 %collective-permute-start.24 = (bf16[64,2176]{1,0:T(8,128)(2,1)S(1)}, bf16[64,2176]{1,0:T(8,128)(2,1)S(1)}, u32[]{:S(2)}, u32[]{:S(2)}) collective-permute-start(bf16[64,2176]{1,0:T(8,128)(2,1)S(1)} %collective-permute-done.18), channel_id=1, source_target_pairs={{0,4},{4,8},{8,12},{12,0},{1,5},{5,9},{9,13},{13,1},{2,6},{6,10},{... | collective-permute-start | bytes 835592 | tf_op jit(solution)/shard_map/ppermute | solution.py:461
  93.1 12.0 %collective-permute-start.31 = (bf16[64,2176]{1,0:T(8,128)(2,1)S(1)}, bf16[64,2176]{1,0:T(8,128)(2,1)S(1)}, u32[]{:S(2)}, u32[]{:S(2)}) collective-permute-start(bf16[64,2176]{1,0:T(8,128)(2,1)S(1)} %collective-permute-done.30), channel_id=1, source_target_pairs={{0,2},{1,3},{2,0},{3,1},{4,6},{5,7},{6,4},{7,5},{8,10},{9,11},{10,... | collective-permute-start | bytes 835592 | tf_op jit(solution)/shard_map/ppermute | solution.py:467
  99.7 21.6 %collective-permute-start.20 = (bf16[128,2176]{1,0:T(8,128)(2,1)S(1)}, bf16[128,2176]{1,0:T(8,128)(2,1)S(1)}, u32[]{:S(2)}, u32[]{:S(2)}) collective-permute-start(bf16[128,2176]{1,0:T(8,128)(2,1)S(1)} %constant_dynamic-update-slice_fusion.2.own_ref), channel_id=1, source_target_pairs={{0,1},{1,0},{2,3},{3,2},{4,5},{5,4},{6,7},{7,6},{8,9},{9,8},{10,11... | collective-permute-start | bytes 1671176 | tf_op jit(solution)/shard_map/ppermute | solution.py:469
  105.2 22.6 %collective-permute-start.32 = (bf16[128,2176]{1,0:T(8,128)(2,1)S(1)}, bf16[128,2176]{1,0:T(8,128)(2,1)S(1)}, u32[]{:S(2)}, u32[]{:S(2)}) collective-permute-start(bf16[128,2176]{1,0:T(8,128)(2,1)S(1)} %constant_dynamic-update-slice_fusion.6.own_ref), channel_id=1, source_target_pairs={{0,1},{1,0},{2,3},{3,2},{4,5},{5,4},{6,7},{7,6},{8,9},{9,8},{10,11... | collective-permute-start | bytes 1671176 | tf_op jit(solution)/shard_map/ppermute | solution.py:469
  105.2 9.1 %collective-permute-start.25 = (bf16[64,2176]{1,0:T(8,128)(2,1)S(1)}, bf16[64,2176]{1,0:T(8,128)(2,1)S(1)}, u32[]{:S(2)}, u32[]{:S(2)}) collective-permute-start(bf16[64,2176]{1,0:T(8,128)(2,1)S(1)} %collective-permute-done.24), channel_id=1, source_target_pairs={{0,2},{1,3},{2,0},{3,1},{4,6},{5,7},{6,4},{7,5},{8,10},{9,11},{10,... | collective-permute-start | bytes 835592 | tf_op jit(solution)/shard_map/ppermute | solution.py:467
  114.3 22.3 %collective-permute-start.26 = (bf16[128,2176]{1,0:T(8,128)(2,1)S(1)}, bf16[128,2176]{1,0:T(8,128)(2,1)S(1)}, u32[]{:S(2)}, u32[]{:S(2)}) collective-permute-start(bf16[128,2176]{1,0:T(8,128)(2,1)S(1)} %constant_dynamic-update-slice_fusion.4.own_ref), channel_id=1, source_target_pairs={{0,1},{1,0},{2,3},{3,2},{4,5},{5,4},{6,7},{7,6},{8,9},{9,8},{10,11... | collective-permute-start | bytes 1671176 | tf_op jit(solution)/shard_map/ppermute | solution.py:469
  120.8 14.1 %collective-permute-start.16 = (bf16[128,2048]{1,0:T(8,128)(2,1)S(1)}, bf16[128,2048]{1,0:T(8,128)(2,1)S(1)}, u32[]{:S(2)}, u32[]{:S(2)}) collective-permute-start(bf16[128,2048]{1,0:T(8,128)(2,1)S(1)} %get-tuple-element.44), channel_id=1, source_target_pairs={{0,1},{1,0},{2,3},{3,2},{4,5},{5,4},{6,7},{7,6},{8,9},{9,8},{10,11... | collective-permute-start | bytes 1572872 | tf_op jit(solution)/shard_map/ppermute | solution.py:471
  127.7 15.4 %collective-permute-start.21 = (bf16[128,2048]{1,0:T(8,128)(2,1)S(1)}, bf16[128,2048]{1,0:T(8,128)(2,1)S(1)}, u32[]{:S(2)}, u32[]{:S(2)}) collective-permute-start(bf16[128,2048]{1,0:T(8,128)(2,1)S(1)} %get-tuple-element.46), channel_id=1, source_target_pairs={{0,1},{1,0},{2,3},{3,2},{4,5},{5,4},{6,7},{7,6},{8,9},{9,8},{10,11... | collective-permute-start | bytes 1572872 | tf_op jit(solution)/shard_map/ppermute | solution.py:471
  134.3 9.5 %collective-permute-start.33 = (bf16[128,2048]{1,0:T(8,128)(2,1)S(1)}, bf16[128,2048]{1,0:T(8,128)(2,1)S(1)}, u32[]{:S(2)}, u32[]{:S(2)}) collective-permute-start(bf16[128,2048]{1,0:T(8,128)(2,1)S(1)} %get-tuple-element.50), channel_id=1, source_target_pairs={{0,1},{1,0},{2,3},{3,2},{4,5},{5,4},{6,7},{7,6},{8,9},{9,8},{10,11... | collective-permute-start | bytes 1572872 | tf_op jit(solution)/shard_map/ppermute | solution.py:471
  135.1 28.3 %collective-permute-start.17 = (bf16[64,2048]{1,0:T(8,128)(2,1)S(1)}, bf16[64,2048]{1,0:T(8,128)(2,1)S(1)}, u32[]{:S(2)}, u32[]{:S(2)}) collective-permute-start(bf16[64,2048]{1,0:T(8,128)(2,1)S(1)} %slice.76), channel_id=1, source_target_pairs={{0,2},{1,3},{2,0},{3,1},{4,6},{5,7},{6,4},{7,5},{8,10},{9,11},{10,... | collective-permute-start | bytes 786440 | tf_op jit(solution)/shard_map/ppermute | solution.py:475
  143.0 9.9 %collective-permute-start.27 = (bf16[128,2048]{1,0:T(8,128)(2,1)S(1)}, bf16[128,2048]{1,0:T(8,128)(2,1)S(1)}, u32[]{:S(2)}, u32[]{:S(2)}) collective-permute-start(bf16[128,2048]{1,0:T(8,128)(2,1)S(1)} %get-tuple-element.48), channel_id=1, source_target_pairs={{0,1},{1,0},{2,3},{3,2},{4,5},{5,4},{6,7},{7,6},{8,9},{9,8},{10,11... | collective-permute-start | bytes 1572872 | tf_op jit(solution)/shard_map/ppermute | solution.py:471
  143.2 9.2 %collective-permute-start.22 = (bf16[64,2048]{1,0:T(8,128)(2,1)S(1)}, bf16[64,2048]{1,0:T(8,128)(2,1)S(1)}, u32[]{:S(2)}, u32[]{:S(2)}) collective-permute-start(bf16[64,2048]{1,0:T(8,128)(2,1)S(1)} %slice.75), channel_id=1, source_target_pairs={{0,2},{1,3},{2,0},{3,1},{4,6},{5,7},{6,4},{7,5},{8,10},{9,11},{10,... | collective-permute-start | bytes 786440 | tf_op jit(solution)/shard_map/ppermute | solution.py:475
  144.0 14.1 %collective-permute-start.34 = (bf16[64,2048]{1,0:T(8,128)(2,1)S(1)}, bf16[64,2048]{1,0:T(8,128)(2,1)S(1)}, u32[]{:S(2)}, u32[]{:S(2)}) collective-permute-start(bf16[64,2048]{1,0:T(8,128)(2,1)S(1)} %slice.73), channel_id=1, source_target_pairs={{0,2},{1,3},{2,0},{3,1},{4,6},{5,7},{6,4},{7,5},{8,10},{9,11},{10,... | collective-permute-start | bytes 786440 | tf_op jit(solution)/shard_map/ppermute | solution.py:475
  152.5 10.8 %collective-permute-start.23 = (bf16[64,2048]{1,0:T(8,128)(2,1)S(1)}, bf16[64,2048]{1,0:T(8,128)(2,1)S(1)}, u32[]{:S(2)}, u32[]{:S(2)}) collective-permute-start(bf16[64,2048]{1,0:T(8,128)(2,1)S(1)} %fusion.2), channel_id=1, source_target_pairs={{0,12},{4,0},{8,4},{12,8},{1,13},{5,1},{9,5},{13,9},{2,14},{6,2},{... | collective-permute-start | bytes 786440 | tf_op jit(solution)/shard_map/ppermute | solution.py:477
  153.0 10.2 %collective-permute-start.28 = (bf16[64,2048]{1,0:T(8,128)(2,1)S(1)}, bf16[64,2048]{1,0:T(8,128)(2,1)S(1)}, u32[]{:S(2)}, u32[]{:S(2)}) collective-permute-start(bf16[64,2048]{1,0:T(8,128)(2,1)S(1)} %slice.74), channel_id=1, source_target_pairs={{0,2},{1,3},{2,0},{3,1},{4,6},{5,7},{6,4},{7,5},{8,10},{9,11},{10,... | collective-permute-start | bytes 786440 | tf_op jit(solution)/shard_map/ppermute | solution.py:475
  158.1 11.1 %collective-permute-start.35 = (bf16[64,2048]{1,0:T(8,128)(2,1)S(1)}, bf16[64,2048]{1,0:T(8,128)(2,1)S(1)}, u32[]{:S(2)}, u32[]{:S(2)}) collective-permute-start(bf16[64,2048]{1,0:T(8,128)(2,1)S(1)} %fusion), channel_id=1, source_target_pairs={{0,4},{4,8},{8,12},{12,0},{1,5},{5,9},{9,13},{13,1},{2,6},{6,10},{... | collective-permute-start | bytes 786440 | tf_op jit(solution)/shard_map/ppermute | solution.py:477
  163.3 15.3 %collective-permute-start.29 = (bf16[64,2048]{1,0:T(8,128)(2,1)S(1)}, bf16[64,2048]{1,0:T(8,128)(2,1)S(1)}, u32[]{:S(2)}, u32[]{:S(2)}) collective-permute-start(bf16[64,2048]{1,0:T(8,128)(2,1)S(1)} %fusion.1), channel_id=1, source_target_pairs={{0,8},{4,12},{8,0},{12,4},{1,9},{5,13},{9,1},{13,5},{2,10},{6,14},... | collective-permute-start | bytes 786440 | tf_op jit(solution)/shard_map/ppermute | solution.py:477
  (9 other events, 9.1 us)

commit v4 on v3

--- a/solution.py
+++ b/solution.py
@@ -150,6 +150,35 @@
     return (k - 1, 1) if k <= count // 2 else ((k + 1) % count, count - 1)
 
 
+def pick_kernel(from_ref, mine_ref, extra_ref, sems):
+    half, more = mine_ref.shape[0], extra_ref.shape[0]
+    group = lax.axis_index("groups")
+    own = pl.ds(pl.multiple_of(group * half, 16), half)
+    next_rows = pl.ds(pl.multiple_of((1 - group) * half, 16), more)
+    copies = [
+        pltpu.make_async_copy(from_ref.at[own, :], mine_ref, sems.at[0]),
+        pltpu.make_async_copy(from_ref.at[next_rows, :], extra_ref, sems.at[1]),
+    ]
+    for copy in copies:
+        copy.start()
+    for copy in copies:
+        copy.wait()
+
+
+def pick_rows(out_weight):
+    rows, width = out_weight.shape
+    shape = jax.ShapeDtypeStruct
+    return pl.pallas_call(
+        pick_kernel,
+        out_shape=(shape((rows // 2, width), bf16), shape((rows // 4, width), bf16)),
+        in_specs=[pl.BlockSpec(memory_space=pl.ANY)],
+        out_specs=(VMEM, VMEM),
+        scratch_shapes=[pltpu.SemaphoreType.DMA((2,))],
+        compiler_params=pltpu.CompilerParams(vmem_limit_bytes=4 << 20),
+        name="pick",
+    )(out_weight)
+
+
 def mix(mixer_input, step_raw, state_maps, decay_rate, skip_gain, out_weight):
     rows, channels = step_raw.shape
     groups = channels // 128
@@ -158,9 +187,7 @@
     order = ring_order(seq_count)
     swap = [(0, 1), (1, 0)]
     half = out_weight.shape[0] // 2
-    group = lax.axis_index("groups")
-    mine = lax.dynamic_slice_in_dim(out_weight, group * half, half, 0)
-    extra = lax.dynamic_slice_in_dim(out_weight, (1 - group) * half, half // 2, 0)
+    mine, extra = pick_rows(out_weight)
     direct = {1: lax.ppermute(mine, "seq", shift(seq_count, 1))}
 
     maps = state_maps.reshape(2 * states, rows).astype(f32)

time: 180 us -> 175 us (0.972)
  local copies, waits for them, and re-layouts: 17.9 us -> 11.9 us
    unnamed x46 -> x40, local copies, waits for them, and re-layouts: 14.8 us -> 11.7 us
    dynamic_slice x2 -> x0, local copies, waits for them, and re-layouts: 2.83 us -> none  [the longest x1 1.87 us: mix(): mine = lax.dynamic_slice_in_dim(out_weight, group * half, half, 0)]
  transfers between devices with their start and end apart: 36 -> 36, of which waited for: 16 -> 17; matrix products, arithmetic and copies ran while one was open for 1% -> 1% of each run, Pallas kernels for 24% -> 24%
where the time goes in v4:
time: 175 us; the launch traced here: 174 us
  waiting for transfers between devices  81.7 us (47%)
  Pallas kernels  42.6 us (24%)
  starting transfers between devices  35.3 us (20%)
  local copies, waits for them, and re-layouts  11.9 us (7%)
  other arithmetic  2.19 us (1%)
    pallas_call x4, Pallas kernels, expert_part(): pl.pallas_call(functools.partial(expert_kernel, capacity, block_rows, exp...  25.6 us
    ppermute x4, waiting for transfers between devices, experts_sum(): row.append(lax.ppermute(planes[k], 'exp', shift(exp_count, 2 * j)))  23.3 us
    ppermute x4, waiting for transfers between devices, experts_sum(): lax.ppermute(leaving, 'exp', shift(exp_count, exp_count - 2 * j))  16.4 us
    ppermute x3, waiting for transfers between devices, experts_sum(): lax.ppermute(mine.astype(bf16), 'seq', shift(seq_count, seq_count - k))  15.1 us
    ppermute x2, waiting for transfers between devices, mix(): direct[k] = lax.ppermute(direct[source], 'seq', shift(seq_count, step_size))  11.9 us
    unnamed x40, local copies, waits for them, and re-layouts  11.7 us
    pallas_call x1, Pallas kernels, mix(): pl.pallas_call(functools.partial(scan_kernel, seq_count), out_shape=shape...  7.49 us
    ppermute x1, waiting for transfers between devices, mix(): direct_more = lax.ppermute(extra, 'seq', shift(seq_count, last))  6.6 us
  transfers between devices with their start and end apart: 36, of which 17 were waited for; matrix products, arithmetic and copies ran while one was open for 1% of the time, Pallas kernels for 24%

profile of v4, /device:TPU:0, one launch (start us, length us, event | category | flops | bytes accessed | tf_op | source)
XLA Modules:
  0.0 174.2 jit_solution(14401525389047969959)
XLA Ops:
  0.0 1.4 copy-done.2
  1.5 3.1 %collective-permute-start.3 = (bf16[512,512]{1,0:T(8,128)(2,1)S(1)}, bf16[512,512]{1,0:T(8,128)(2,1)S(1)}, u32[]{:S(2)}, u32[]{:S(2)}) collective-permute-start(bf16[512,512]{1,0:T(8,128)(2,1)S(1)} %get-tuple-element.38), channel_id=1, source_target_pairs={{0,4},{4,8},{8,12},{12,0},{1,5},{5,9},{9,13},{13,1},{2,6},{6,10},{... | collective-permute-start | bytes 1572872 | tf_op jit(solution)/shard_map/ppermute | solution.py:191
  5.3 1.2 copy-done
  6.5 1.0 copy-done.4
  8.4 5.7 %ends.1 = (bf16[2,144,128]{2,1,0:T(8,128)(2,1)S(1)}, f32[2048,128]{1,0:T(8,128)S(1)}, f32[2048,128]{1,0:T(8,128)S(1)}) custom-call(f32[32,256]{1,0:T(8,128)S(1)} %bitcast_convert_fusion.maps_ref, bf16[256,1024]{1,0:T(8,128)(2,1)S(1)} %copy-done.4, bf16[2,256,1024]{2,1,0:T(8,128)(2,1)S(1)} %copy-done, f32[16,1024]{1,0:T(8,128)S(1)} %copy-done.5), custom_call_target="tpu_custom_call" | custom-call | tf_op jit(solution)/shard_map/ends/pallas_call | solution.py:195
  14.1 1.6 collective-permute-start
  15.7 1.1 collective-permute-start.1
  16.8 2.8 %collective-permute-start.2 = (bf16[2,144,128]{2,1,0:T(8,128)(2,1)S(1)}, bf16[2,144,128]{2,1,0:T(8,128)(2,1)S(1)}, u32[]{:S(2)}, u32[]{:S(2)}) collective-permute-start(bf16[2,144,128]{2,1,0:T(8,128)(2,1)S(1)} %get-tuple-element.32.rest_0_), channel_id=1, source_target_pairs={{0,12},{4,0},{8,4},{12,8},{1,13},{5,1},{9,5},{13,9},{2,14},{6,2},{... | collective-permute-start | bytes 221192 | tf_op jit(solution)/shard_map/ppermute | solution.py:210
  19.7 1.4 collective-permute-done.rest_1_
  21.1 2.4 %collective-permute-done.1.rest_2_ = bf16[2,144,128]{2,1,0:T(8,128)(2,1)S(1)} collective-permute-done((bf16[2,144,128]{2,1,0:T(8,128)(2,1)S(1)}, bf16[2,144,128]{2,1,0:T(8,128)(2,1)S(1)}, u32[]{:S(2)}, u32[]{:S(2)}) %collective-permute-start.1) | collective-permute-done | bytes 73760 | tf_op jit(solution)/shard_map/ppermute | solution.py:210
  23.5 1.9 %collective-permute-start.5 = (bf16[512,512]{1,0:T(8,128)(2,1)S(1)}, bf16[512,512]{1,0:T(8,128)(2,1)S(1)}, u32[]{:S(2)}, u32[]{:S(2)}) collective-permute-start(bf16[512,512]{1,0:T(8,128)(2,1)S(1)} %collective-permute-done.3.refs_1_), channel_id=1, source_target_pairs={{0,4},{4,8},{8,12},{12,0},{1,5},{5,9},{9,13},{13,1},{2,6},{6,10},{... | collective-permute-start | bytes 1572872 | tf_op jit(solution)/shard_map/ppermute | solution.py:216
  25.4 1.5 collective-permute-start.4
  26.9 11.9 %collective-permute-done.5.refs_3_ = bf16[512,512]{1,0:T(8,128)(2,1)S(1)} collective-permute-done((bf16[512,512]{1,0:T(8,128)(2,1)S(1)}, bf16[512,512]{1,0:T(8,128)(2,1)S(1)}, u32[]{:S(2)}, u32[]{:S(2)}) %collective-permute-start.5) | collective-permute-done | bytes 524320 | tf_op jit(solution)/shard_map/ppermute | solution.py:216
  38.8 1.5 collective-permute-start.6
  40.4 1.2 copy-done.1
  43.1 7.5 %scan.1.mixed_ref = bf16[256,1024]{1,0:T(8,128)(2,1)S(1)} custom-call(f32[32,256]{1,0:T(8,128)S(1)} %bitcast_convert_fusion.maps_ref, f32[2048,128]{1,0:T(8,128)S(1)} %get-tuple-element.30.step_ref, f32[2048,128]{1,0:T(8,128)S(1)} %get-tuple-element.31.drive_ref, f32[16,1024]{1,0:T(8,128)S(1)} %copy-done.6, bf16[2,256,1024]{2,1,0:T(8,128)(2,1)S(1)} %copy-done.1, ...), custom_call_target="tpu_custom_call" | custom-call | tf_op jit(solution)/shard_map/scan/pallas_call | solution.py:226
  51.4 1.4 copy-done.3
  52.8 1.0 project.2
  54.6 1.3 collective-permute-start.11
  56.0 6.6 %collective-permute-done.10.refs_1_ = bf16[256,512]{1,0:T(8,128)(2,1)S(1)} collective-permute-done((bf16[256,512]{1,0:T(8,128)(2,1)S(1)}, bf16[256,512]{1,0:T(8,128)(2,1)S(1)}, u32[]{:S(2)}, u32[]{:S(2)}) %collective-permute-start.10) | collective-permute-done | bytes 262176 | tf_op jit(solution)/shard_map/ppermute | solution.py:218
  63.7 1.6 collective-permute-start.8
  65.3 1.4 collective-permute-start.13
  67.4 1.0 slice-done.3
  68.9 0.9 slice-done.4
  71.2 1.2 collective-permute-done.13.refs_5_
  73.2 1.3 collective-permute-start.18
  74.6 2.5 %collective-permute-start.30 = (bf16[64,2176]{1,0:T(8,128)(2,1)S(1)}, bf16[64,2176]{1,0:T(8,128)(2,1)S(1)}, u32[]{:S(2)}, u32[]{:S(2)}) collective-permute-start(bf16[64,2176]{1,0:T(8,128)(2,1)S(1)} %get-tuple-element.43), channel_id=1, source_target_pairs={{0,12},{4,0},{8,4},{12,8},{1,13},{5,1},{9,5},{13,9},{2,14},{6,2},{... | collective-permute-start | bytes 835592 | tf_op jit(solution)/shard_map/ppermute | solution.py:488
  77.1 1.5 collective-permute-start.14
  78.6 6.1 %collective-permute-done.14 = bf16[64,2176]{1,0:T(8,128)(2,1)S(1)} collective-permute-done((bf16[64,2176]{1,0:T(8,128)(2,1)S(1)}, bf16[64,2176]{1,0:T(8,128)(2,1)S(1)}, u32[]{:S(2)}, u32[]{:S(2)}) %collective-permute-start.14) | collective-permute-done | bytes 278560 | tf_op jit(solution)/shard_map/ppermute | solution.py:494
  84.8 1.6 collective-permute-start.19
  86.4 2.1 %collective-permute-done.30 = bf16[64,2176]{1,0:T(8,128)(2,1)S(1)} collective-permute-done((bf16[64,2176]{1,0:T(8,128)(2,1)S(1)}, bf16[64,2176]{1,0:T(8,128)(2,1)S(1)}, u32[]{:S(2)}, u32[]{:S(2)}) %collective-permute-start.30) | collective-permute-done | bytes 278560 | tf_op jit(solution)/shard_map/ppermute | solution.py:488
  88.4 1.5 collective-permute-start.31
  90.0 4.4 %collective-permute-done.19 = bf16[64,2176]{1,0:T(8,128)(2,1)S(1)} collective-permute-done((bf16[64,2176]{1,0:T(8,128)(2,1)S(1)}, bf16[64,2176]{1,0:T(8,128)(2,1)S(1)}, u32[]{:S(2)}, u32[]{:S(2)}) %collective-permute-start.19) | collective-permute-done | bytes 278560 | tf_op jit(solution)/shard_map/ppermute | solution.py:494
  94.5 5.3 %collective-permute-done.31 = bf16[64,2176]{1,0:T(8,128)(2,1)S(1)} collective-permute-done((bf16[64,2176]{1,0:T(8,128)(2,1)S(1)}, bf16[64,2176]{1,0:T(8,128)(2,1)S(1)}, u32[]{:S(2)}, u32[]{:S(2)}) %collective-permute-start.31) | collective-permute-done | bytes 278560 | tf_op jit(solution)/shard_map/ppermute | solution.py:494
  99.9 1.6 collective-permute-start.25
  101.5 7.5 %collective-permute-done.25 = bf16[64,2176]{1,0:T(8,128)(2,1)S(1)} collective-permute-done((bf16[64,2176]{1,0:T(8,128)(2,1)S(1)}, bf16[64,2176]{1,0:T(8,128)(2,1)S(1)}, u32[]{:S(2)}, u32[]{:S(2)}) %collective-permute-start.25) | collective-permute-done | bytes 278560 | tf_op jit(solution)/shard_map/ppermute | solution.py:494
  109.1 6.4 %expert.4 = (f32[128,2048]{1,0:T(8,128)S(1)}, bf16[128,2048]{1,0:T(8,128)(2,1)S(1)}) custom-call(bf16[128,2176]{1,0:T(8,128)(2,1)S(1)} %constant_dynamic-update-slice_fusion.own_ref, bf16[128,2176]{1,0:T(8,128)(2,1)S(1)} %collective-permute-done.15.mate_ref, bf16[1,2048,1792]{2,1,0:T(8,128)(2,1)S(1)} %hold.3.gate_ref, ...), custom_call_target="tpu_custom_call" | custom-call | flops 3875536896 | bytes 22020096 | tf_op jit(solution)/shard_map/expert/pallas_call | solution.py:461
  116.0 6.3 %expert.5 = (f32[128,2048]{1,0:T(8,128)S(1)}, bf16[128,2048]{1,0:T(8,128)(2,1)S(1)}) custom-call(bf16[128,2176]{1,0:T(8,128)(2,1)S(1)} %constant_dynamic-update-slice_fusion.2.own_ref, bf16[128,2176]{1,0:T(8,128)(2,1)S(1)} %collective-permute-done.20.mate_ref, bf16[1,2048,1792]{2,1,0:T(8,128)(2,1)S(1)} %hold.3.gate_ref, ...), custom_call_target="tpu_custom_call" | custom-call | flops 3875536896 | bytes 22020096 | tf_op jit(solution)/shard_map/expert/pallas_call | solution.py:461
  122.5 6.6 %expert.7 = (f32[128,2048]{1,0:T(8,128)S(1)}, bf16[128,2048]{1,0:T(8,128)(2,1)S(1)}) custom-call(bf16[128,2176]{1,0:T(8,128)(2,1)S(1)} %constant_dynamic-update-slice_fusion.6.own_ref, bf16[128,2176]{1,0:T(8,128)(2,1)S(1)} %collective-permute-done.32.mate_ref, bf16[1,2048,1792]{2,1,0:T(8,128)(2,1)S(1)} %hold.3.gate_ref, ...), custom_call_target="tpu_custom_call" | custom-call | flops 3875536896 | bytes 22020096 | tf_op jit(solution)/shard_map/expert/pallas_call | solution.py:461
  129.8 1.6 collective-permute-start.17
  131.3 6.3 %expert.6 = (f32[128,2048]{1,0:T(8,128)S(1)}, bf16[128,2048]{1,0:T(8,128)(2,1)S(1)}) custom-call(bf16[128,2176]{1,0:T(8,128)(2,1)S(1)} %constant_dynamic-update-slice_fusion.4.own_ref, bf16[128,2176]{1,0:T(8,128)(2,1)S(1)} %collective-permute-done.26.mate_ref, bf16[1,2048,1792]{2,1,0:T(8,128)(2,1)S(1)} %hold.3.gate_ref, ...), custom_call_target="tpu_custom_call" | custom-call | flops 3875536896 | bytes 22020096 | tf_op jit(solution)/shard_map/expert/pallas_call | solution.py:461
  138.7 1.6 collective-permute-start.34
  140.2 6.9 %collective-permute-done.22 = bf16[64,2048]{1,0:T(8,128)(2,1)S(1)} collective-permute-done((bf16[64,2048]{1,0:T(8,128)(2,1)S(1)}, bf16[64,2048]{1,0:T(8,128)(2,1)S(1)}, u32[]{:S(2)}, u32[]{:S(2)}) %collective-permute-start.22) | collective-permute-done | bytes 262176 | tf_op jit(solution)/shard_map/ppermute | solution.py:502
  148.3 4.5 %collective-permute-done.34 = bf16[64,2048]{1,0:T(8,128)(2,1)S(1)} collective-permute-done((bf16[64,2048]{1,0:T(8,128)(2,1)S(1)}, bf16[64,2048]{1,0:T(8,128)(2,1)S(1)}, u32[]{:S(2)}, u32[]{:S(2)}) %collective-permute-start.34) | collective-permute-done | bytes 262176 | tf_op jit(solution)/shard_map/ppermute | solution.py:502
  152.9 5.0 %collective-permute-done.28 = bf16[64,2048]{1,0:T(8,128)(2,1)S(1)} collective-permute-done((bf16[64,2048]{1,0:T(8,128)(2,1)S(1)}, bf16[64,2048]{1,0:T(8,128)(2,1)S(1)}, u32[]{:S(2)}, u32[]{:S(2)}) %collective-permute-start.28) | collective-permute-done | bytes 262176 | tf_op jit(solution)/shard_map/ppermute | solution.py:502
  158.2 5.7 %collective-permute-done.35 = bf16[64,2048]{1,0:T(8,128)(2,1)S(1)} collective-permute-done((bf16[64,2048]{1,0:T(8,128)(2,1)S(1)}, bf16[64,2048]{1,0:T(8,128)(2,1)S(1)}, u32[]{:S(2)}, u32[]{:S(2)}) %collective-permute-start.35) | collective-permute-done | bytes 262176 | tf_op jit(solution)/shard_map/ppermute | solution.py:504
  163.9 9.3 %collective-permute-done.29 = bf16[64,2048]{1,0:T(8,128)(2,1)S(1)} collective-permute-done((bf16[64,2048]{1,0:T(8,128)(2,1)S(1)}, bf16[64,2048]{1,0:T(8,128)(2,1)S(1)}, u32[]{:S(2)}, u32[]{:S(2)}) %collective-permute-start.29) | collective-permute-done | bytes 262176 | tf_op jit(solution)/shard_map/ppermute | solution.py:504
  173.3 0.9 fusion.7
  (100 shorter events, 13.6 us)
Async XLA Ops:
  0.0 66.7 %slice-start = ((s8[7340032]{0:T(1024)(128)(4,1)}), s8[4194304]{0:T(1024)(128)(4,1)S(1)}, s32[]{:S(2)}) async-start(s8[7340032]{0:T(1024)(128)(4,1)} %bitcast.7), calls=%async_computation | async-start | bytes 8388608
  0.0 1.4 copy-start.2
  1.5 22.0 %collective-permute-start.3 = (bf16[512,512]{1,0:T(8,128)(2,1)S(1)}, bf16[512,512]{1,0:T(8,128)(2,1)S(1)}, u32[]{:S(2)}, u32[]{:S(2)}) collective-permute-start(bf16[512,512]{1,0:T(8,128)(2,1)S(1)} %get-tuple-element.38), channel_id=1, source_target_pairs={{0,4},{4,8},{8,12},{12,0},{1,5},{5,9},{9,13},{13,1},{2,6},{6,10},{... | collective-permute-start | bytes 1572872 | tf_op jit(solution)/shard_map/ppermute | solution.py:191
  14.1 7.0 %collective-permute-start = (bf16[2,144,128]{2,1,0:T(8,128)(2,1)S(1)}, bf16[2,144,128]{2,1,0:T(8,128)(2,1)S(1)}, u32[]{:S(2)}, u32[]{:S(2)}) collective-permute-start(bf16[2,144,128]{2,1,0:T(8,128)(2,1)S(1)} %get-tuple-element.32.rest_0_), channel_id=1, source_target_pairs={{0,4},{4,8},{8,12},{12,0},{1,5},{5,9},{9,13},{13,1},{2,6},{6,10},{... | collective-permute-start | bytes 221192 | tf_op jit(solution)/shard_map/ppermute | solution.py:210
  15.7 7.7 %collective-permute-start.1 = (bf16[2,144,128]{2,1,0:T(8,128)(2,1)S(1)}, bf16[2,144,128]{2,1,0:T(8,128)(2,1)S(1)}, u32[]{:S(2)}, u32[]{:S(2)}) collective-permute-start(bf16[2,144,128]{2,1,0:T(8,128)(2,1)S(1)} %get-tuple-element.32.rest_0_), channel_id=1, source_target_pairs={{0,8},{4,12},{8,0},{12,4},{1,9},{5,13},{9,1},{13,5},{2,10},{6,14},... | collective-permute-start | bytes 221192 | tf_op jit(solution)/shard_map/ppermute | solution.py:210
  16.8 6.6 %collective-permute-start.2 = (bf16[2,144,128]{2,1,0:T(8,128)(2,1)S(1)}, bf16[2,144,128]{2,1,0:T(8,128)(2,1)S(1)}, u32[]{:S(2)}, u32[]{:S(2)}) collective-permute-start(bf16[2,144,128]{2,1,0:T(8,128)(2,1)S(1)} %get-tuple-element.32.rest_0_), channel_id=1, source_target_pairs={{0,12},{4,0},{8,4},{12,8},{1,13},{5,1},{9,5},{13,9},{2,14},{6,2},{... | collective-permute-start | bytes 221192 | tf_op jit(solution)/shard_map/ppermute | solution.py:210
  23.5 15.3 %collective-permute-start.5 = (bf16[512,512]{1,0:T(8,128)(2,1)S(1)}, bf16[512,512]{1,0:T(8,128)(2,1)S(1)}, u32[]{:S(2)}, u32[]{:S(2)}) collective-permute-start(bf16[512,512]{1,0:T(8,128)(2,1)S(1)} %collective-permute-done.3.refs_1_), channel_id=1, source_target_pairs={{0,4},{4,8},{8,12},{12,0},{1,5},{5,9},{9,13},{13,1},{2,6},{6,10},{... | collective-permute-start | bytes 1572872 | tf_op jit(solution)/shard_map/ppermute | solution.py:216
  25.4 25.2 %collective-permute-start.4 = (bf16[512,512]{1,0:T(8,128)(2,1)S(1)}, bf16[512,512]{1,0:T(8,128)(2,1)S(1)}, u32[]{:S(2)}, u32[]{:S(2)}) collective-permute-start(bf16[512,512]{1,0:T(8,128)(2,1)S(1)} %collective-permute-done.3.refs_1_), channel_id=1, source_target_pairs={{0,16},{16,0},{1,17},{17,1},{2,18},{18,2},{3,19},{19,3},{4,20},{20... | collective-permute-start | bytes 1572872 | tf_op jit(solution)/shard_map/ppermute | solution.py:221
  38.8 12.6 %collective-permute-start.6 = (bf16[512,512]{1,0:T(8,128)(2,1)S(1)}, bf16[512,512]{1,0:T(8,128)(2,1)S(1)}, u32[]{:S(2)}, u32[]{:S(2)}) collective-permute-start(bf16[512,512]{1,0:T(8,128)(2,1)S(1)} %collective-permute-done.5.refs_3_), channel_id=1, source_target_pairs={{0,16},{16,0},{1,17},{17,1},{2,18},{18,2},{3,19},{19,3},{4,20},{20... | collective-permute-start | bytes 1572872 | tf_op jit(solution)/shard_map/ppermute | solution.py:221
  40.3 14.3 %collective-permute-start.9 = (bf16[512,512]{1,0:T(8,128)(2,1)S(1)}, bf16[512,512]{1,0:T(8,128)(2,1)S(1)}, u32[]{:S(2)}, u32[]{:S(2)}) collective-permute-start(bf16[512,512]{1,0:T(8,128)(2,1)S(1)} %get-tuple-element.38), channel_id=1, source_target_pairs={{0,12},{4,0},{8,4},{12,8},{1,13},{5,1},{9,5},{13,9},{2,14},{6,2},{... | collective-permute-start | bytes 1572872 | tf_op jit(solution)/shard_map/ppermute | solution.py:216
  50.6 16.1 %slice-start.1 = ((s8[7340032]{0:T(1024)(128)(4,1)}), s8[3145728]{0:T(1024)(128)(4,1)S(1)}, s32[]{:S(2)}) async-start(s8[7340032]{0:T(1024)(128)(4,1)} %bitcast.7), calls=%async_computation.1 | async-start | bytes 6291456
  51.4 1.4 copy-start.3
  53.8 9.8 %collective-permute-start.7 = (f32[128,1536]{1,0:T(8,128)S(1)}, f32[128,1536]{1,0:T(8,128)S(1)}, u32[]{:S(2)}, u32[]{:S(2)}) collective-permute-start(f32[128,1536]{1,0:T(8,128)S(1)} %get-tuple-element.37), channel_id=1, source_target_pairs={{0,1},{1,0},{2,3},{3,2},{4,5},{5,4},{6,7},{7,6},{8,9},{9,8},{10,11... | collective-permute-start | bytes 2359304 | tf_op jit(solution)/shard_map/ppermute | solution.py:308
  53.9 8.7 %collective-permute-start.10 = (bf16[256,512]{1,0:T(8,128)(2,1)S(1)}, bf16[256,512]{1,0:T(8,128)(2,1)S(1)}, u32[]{:S(2)}, u32[]{:S(2)}) collective-permute-start(bf16[256,512]{1,0:T(8,128)(2,1)S(1)} %get-tuple-element.39), channel_id=1, source_target_pairs={{0,12},{4,0},{8,4},{12,8},{1,13},{5,1},{9,5},{13,9},{2,14},{6,2},{... | collective-permute-start | bytes 786440 | tf_op jit(solution)/shard_map/ppermute | solution.py:218
  54.6 8.4 %collective-permute-start.11 = (bf16[256,512]{1,0:T(8,128)(2,1)S(1)}, bf16[256,512]{1,0:T(8,128)(2,1)S(1)}, u32[]{:S(2)}, u32[]{:S(2)}) collective-permute-start(bf16[256,512]{1,0:T(8,128)(2,1)S(1)} %slice.40), channel_id=1, source_target_pairs={{0,16},{16,0},{1,17},{17,1},{2,18},{18,2},{3,19},{19,3},{4,20},{20... | collective-permute-start | bytes 786440 | tf_op jit(solution)/shard_map/ppermute | solution.py:223
  63.5 1.7 collective-permute-start.12
  63.7 8.7 %collective-permute-start.8 = (bf16[64,1536]{1,0:T(8,128)(2,1)S(1)}, bf16[64,1536]{1,0:T(8,128)(2,1)S(1)}, u32[]{:S(2)}, u32[]{:S(2)}) collective-permute-start(bf16[64,1536]{1,0:T(8,128)(2,1)S(1)} %leave.2), channel_id=1, source_target_pairs={{0,2},{1,3},{2,0},{3,1},{4,6},{5,7},{6,4},{7,5},{8,10},{9,11},{10,... | collective-permute-start | bytes 589832 | tf_op jit(solution)/shard_map/ppermute | solution.py:320
  65.2 2.2 %slice-start.2 = ((s8[7340032]{0:T(1024)(128)(4,1)}), s8[4194304]{0:T(1024)(128)(4,1)S(1)}, s32[]{:S(2)}) async-start(s8[7340032]{0:T(1024)(128)(4,1)} %bitcast.9), calls=%async_computation.2 | async-start | bytes 8388608
  65.3 3.2 %slice-start.3 = ((s8[7340032]{0:T(1024)(128)(4,1)}), s8[3145728]{0:T(1024)(128)(4,1)S(1)}, s32[]{:S(2)}) async-start(s8[7340032]{0:T(1024)(128)(4,1)} %bitcast.9), calls=%async_computation.3 | async-start | bytes 6291456
  65.3 7.2 %collective-permute-start.13 = (bf16[64,512]{1,0:T(8,128)(2,1)S(1)}, bf16[64,512]{1,0:T(8,128)(2,1)S(1)}, u32[]{:S(2)}, u32[]{:S(2)}) collective-permute-start(bf16[64,512]{1,0:T(8,128)(2,1)S(1)} %leave.3), channel_id=1, source_target_pairs={{0,2},{1,3},{2,0},{3,1},{4,6},{5,7},{6,4},{7,5},{8,10},{9,11},{10,... | collective-permute-start | bytes 196616 | tf_op jit(solution)/shard_map/ppermute | solution.py:320
  66.7 3.1 %slice-start.4 = ((s8[7340032]{0:T(1024)(128)(4,1)}), s8[4194304]{0:T(1024)(128)(4,1)S(1)}, s32[]{:S(2)}) async-start(s8[7340032]{0:T(1024)(128)(4,1)} %bitcast.11), calls=%async_computation.4 | async-start | bytes 8388608
  68.4 2.3 %slice-start.5 = ((s8[7340032]{0:T(1024)(128)(4,1)}), s8[3145728]{0:T(1024)(128)(4,1)S(1)}, s32[]{:S(2)}) async-start(s8[7340032]{0:T(1024)(128)(4,1)} %bitcast.11), calls=%async_computation.5 | async-start | bytes 6291456
  70.7 1.8 %copy-start.7 = (bf16[64,2048]{1,0:T(8,128)(2,1)S(1)}, bf16[64,2048]{1,0:T(8,128)(2,1)}, u32[]{:S(2)}) copy-start(bf16[64,2048]{1,0:T(8,128)(2,1)} %refs_6_.1) | copy-start | bytes 786436
  70.7 1.8 %copy-start.8 = (bf16[2048,4]{0,1:T(4,128)(2,1)S(1)}, bf16[2048,4]{0,1:T(4,128)(2,1)}, u32[]{:S(2)}) copy-start(bf16[2048,4]{0,1:T(4,128)(2,1)} %param.21) | copy-start | bytes 49156
  70.7 1.8 %copy-start.9 = (f32[2048]{0:T(1024)S(1)}, f32[2048]{0:T(1024)}, u32[]{:S(2)}) copy-start(f32[2048]{0:T(1024)} %param.20) | copy-start | bytes 24580
  70.7 1.8 %copy-start.11 = (s32[64,2]{0,1:T(2,128)S(1)}, s32[64,2]{0,1:T(2,128)}, u32[]{:S(2)}) copy-start(s32[64,2]{0,1:T(2,128)} %param.22) | copy-start | bytes 1540
  73.2 11.6 %collective-permute-start.18 = (bf16[64,2176]{1,0:T(8,128)(2,1)S(1)}, bf16[64,2176]{1,0:T(8,128)(2,1)S(1)}, u32[]{:S(2)}, u32[]{:S(2)}) collective-permute-start(bf16[64,2176]{1,0:T(8,128)(2,1)S(1)} %get-tuple-element.43), channel_id=1, source_target_pairs={{0,4},{4,8},{8,12},{12,0},{1,5},{5,9},{9,13},{13,1},{2,6},{6,10},{... | collective-permute-start | bytes 835592 | tf_op jit(solution)/shard_map/ppermute | solution.py:488
  74.6 13.9 %collective-permute-start.30 = (bf16[64,2176]{1,0:T(8,128)(2,1)S(1)}, bf16[64,2176]{1,0:T(8,128)(2,1)S(1)}, u32[]{:S(2)}, u32[]{:S(2)}) collective-permute-start(bf16[64,2176]{1,0:T(8,128)(2,1)S(1)} %get-tuple-element.43), channel_id=1, source_target_pairs={{0,12},{4,0},{8,4},{12,8},{1,13},{5,1},{9,5},{13,9},{2,14},{6,2},{... | collective-permute-start | bytes 835592 | tf_op jit(solution)/shard_map/ppermute | solution.py:488
  77.1 7.6 %collective-permute-start.14 = (bf16[64,2176]{1,0:T(8,128)(2,1)S(1)}, bf16[64,2176]{1,0:T(8,128)(2,1)S(1)}, u32[]{:S(2)}, u32[]{:S(2)}) collective-permute-start(bf16[64,2176]{1,0:T(8,128)(2,1)S(1)} %get-tuple-element.43), channel_id=1, source_target_pairs={{0,2},{1,3},{2,0},{3,1},{4,6},{5,7},{6,4},{7,5},{8,10},{9,11},{10,... | collective-permute-start | bytes 835592 | tf_op jit(solution)/shard_map/ppermute | solution.py:494
  84.7 24.4 %collective-permute-start.15 = (bf16[128,2176]{1,0:T(8,128)(2,1)S(1)}, bf16[128,2176]{1,0:T(8,128)(2,1)S(1)}, u32[]{:S(2)}, u32[]{:S(2)}) collective-permute-start(bf16[128,2176]{1,0:T(8,128)(2,1)S(1)} %constant_dynamic-update-slice_fusion.own_ref), channel_id=1, source_target_pairs={{0,1},{1,0},{2,3},{3,2},{4,5},{5,4},{6,7},{7,6},{8,9},{9,8},{10,11... | collective-permute-start | bytes 1671176 | tf_op jit(solution)/shard_map/ppermute | solution.py:496
  84.8 9.6 %collective-permute-start.19 = (bf16[64,2176]{1,0:T(8,128)(2,1)S(1)}, bf16[64,2176]{1,0:T(8,128)(2,1)S(1)}, u32[]{:S(2)}, u32[]{:S(2)}) collective-permute-start(bf16[64,2176]{1,0:T(8,128)(2,1)S(1)} %collective-permute-done.18), channel_id=1, source_target_pairs={{0,2},{1,3},{2,0},{3,1},{4,6},{5,7},{6,4},{7,5},{8,10},{9,11},{10,... | collective-permute-start | bytes 835592 | tf_op jit(solution)/shard_map/ppermute | solution.py:494
  86.4 13.6 %collective-permute-start.24 = (bf16[64,2176]{1,0:T(8,128)(2,1)S(1)}, bf16[64,2176]{1,0:T(8,128)(2,1)S(1)}, u32[]{:S(2)}, u32[]{:S(2)}) collective-permute-start(bf16[64,2176]{1,0:T(8,128)(2,1)S(1)} %collective-permute-done.18), channel_id=1, source_target_pairs={{0,4},{4,8},{8,12},{12,0},{1,5},{5,9},{9,13},{13,1},{2,6},{6,10},{... | collective-permute-start | bytes 835592 | tf_op jit(solution)/shard_map/ppermute | solution.py:488
  88.4 11.4 %collective-permute-start.31 = (bf16[64,2176]{1,0:T(8,128)(2,1)S(1)}, bf16[64,2176]{1,0:T(8,128)(2,1)S(1)}, u32[]{:S(2)}, u32[]{:S(2)}) collective-permute-start(bf16[64,2176]{1,0:T(8,128)(2,1)S(1)} %collective-permute-done.30), channel_id=1, source_target_pairs={{0,2},{1,3},{2,0},{3,1},{4,6},{5,7},{6,4},{7,5},{8,10},{9,11},{10,... | collective-permute-start | bytes 835592 | tf_op jit(solution)/shard_map/ppermute | solution.py:494
  94.4 21.6 %collective-permute-start.20 = (bf16[128,2176]{1,0:T(8,128)(2,1)S(1)}, bf16[128,2176]{1,0:T(8,128)(2,1)S(1)}, u32[]{:S(2)}, u32[]{:S(2)}) collective-permute-start(bf16[128,2176]{1,0:T(8,128)(2,1)S(1)} %constant_dynamic-update-slice_fusion.2.own_ref), channel_id=1, source_target_pairs={{0,1},{1,0},{2,3},{3,2},{4,5},{5,4},{6,7},{7,6},{8,9},{9,8},{10,11... | collective-permute-start | bytes 1671176 | tf_op jit(solution)/shard_map/ppermute | solution.py:496
  99.9 22.6 %collective-permute-start.32 = (bf16[128,2176]{1,0:T(8,128)(2,1)S(1)}, bf16[128,2176]{1,0:T(8,128)(2,1)S(1)}, u32[]{:S(2)}, u32[]{:S(2)}) collective-permute-start(bf16[128,2176]{1,0:T(8,128)(2,1)S(1)} %constant_dynamic-update-slice_fusion.6.own_ref), channel_id=1, source_target_pairs={{0,1},{1,0},{2,3},{3,2},{4,5},{5,4},{6,7},{7,6},{8,9},{9,8},{10,11... | collective-permute-start | bytes 1671176 | tf_op jit(solution)/shard_map/ppermute | solution.py:496
  99.9 9.1 %collective-permute-start.25 = (bf16[64,2176]{1,0:T(8,128)(2,1)S(1)}, bf16[64,2176]{1,0:T(8,128)(2,1)S(1)}, u32[]{:S(2)}, u32[]{:S(2)}) collective-permute-start(bf16[64,2176]{1,0:T(8,128)(2,1)S(1)} %collective-permute-done.24), channel_id=1, source_target_pairs={{0,2},{1,3},{2,0},{3,1},{4,6},{5,7},{6,4},{7,5},{8,10},{9,11},{10,... | collective-permute-start | bytes 835592 | tf_op jit(solution)/shard_map/ppermute | solution.py:494
  109.0 22.3 %collective-permute-start.26 = (bf16[128,2176]{1,0:T(8,128)(2,1)S(1)}, bf16[128,2176]{1,0:T(8,128)(2,1)S(1)}, u32[]{:S(2)}, u32[]{:S(2)}) collective-permute-start(bf16[128,2176]{1,0:T(8,128)(2,1)S(1)} %constant_dynamic-update-slice_fusion.4.own_ref), channel_id=1, source_target_pairs={{0,1},{1,0},{2,3},{3,2},{4,5},{5,4},{6,7},{7,6},{8,9},{9,8},{10,11... | collective-permute-start | bytes 1671176 | tf_op jit(solution)/shard_map/ppermute | solution.py:496
  115.5 14.1 %collective-permute-start.16 = (bf16[128,2048]{1,0:T(8,128)(2,1)S(1)}, bf16[128,2048]{1,0:T(8,128)(2,1)S(1)}, u32[]{:S(2)}, u32[]{:S(2)}) collective-permute-start(bf16[128,2048]{1,0:T(8,128)(2,1)S(1)} %get-tuple-element.48), channel_id=1, source_target_pairs={{0,1},{1,0},{2,3},{3,2},{4,5},{5,4},{6,7},{7,6},{8,9},{9,8},{10,11... | collective-permute-start | bytes 1572872 | tf_op jit(solution)/shard_map/ppermute | solution.py:498
  122.4 15.4 %collective-permute-start.21 = (bf16[128,2048]{1,0:T(8,128)(2,1)S(1)}, bf16[128,2048]{1,0:T(8,128)(2,1)S(1)}, u32[]{:S(2)}, u32[]{:S(2)}) collective-permute-start(bf16[128,2048]{1,0:T(8,128)(2,1)S(1)} %get-tuple-element.50), channel_id=1, source_target_pairs={{0,1},{1,0},{2,3},{3,2},{4,5},{5,4},{6,7},{7,6},{8,9},{9,8},{10,11... | collective-permute-start | bytes 1572872 | tf_op jit(solution)/shard_map/ppermute | solution.py:498
  129.0 9.5 %collective-permute-start.33 = (bf16[128,2048]{1,0:T(8,128)(2,1)S(1)}, bf16[128,2048]{1,0:T(8,128)(2,1)S(1)}, u32[]{:S(2)}, u32[]{:S(2)}) collective-permute-start(bf16[128,2048]{1,0:T(8,128)(2,1)S(1)} %get-tuple-element.54), channel_id=1, source_target_pairs={{0,1},{1,0},{2,3},{3,2},{4,5},{5,4},{6,7},{7,6},{8,9},{9,8},{10,11... | collective-permute-start | bytes 1572872 | tf_op jit(solution)/shard_map/ppermute | solution.py:498
  129.8 28.4 %collective-permute-start.17 = (bf16[64,2048]{1,0:T(8,128)(2,1)S(1)}, bf16[64,2048]{1,0:T(8,128)(2,1)S(1)}, u32[]{:S(2)}, u32[]{:S(2)}) collective-permute-start(bf16[64,2048]{1,0:T(8,128)(2,1)S(1)} %slice.76), channel_id=1, source_target_pairs={{0,2},{1,3},{2,0},{3,1},{4,6},{5,7},{6,4},{7,5},{8,10},{9,11},{10,... | collective-permute-start | bytes 786440 | tf_op jit(solution)/shard_map/ppermute | solution.py:502
  137.7 9.9 %collective-permute-start.27 = (bf16[128,2048]{1,0:T(8,128)(2,1)S(1)}, bf16[128,2048]{1,0:T(8,128)(2,1)S(1)}, u32[]{:S(2)}, u32[]{:S(2)}) collective-permute-start(bf16[128,2048]{1,0:T(8,128)(2,1)S(1)} %get-tuple-element.52), channel_id=1, source_target_pairs={{0,1},{1,0},{2,3},{3,2},{4,5},{5,4},{6,7},{7,6},{8,9},{9,8},{10,11... | collective-permute-start | bytes 1572872 | tf_op jit(solution)/shard_map/ppermute | solution.py:498
  137.9 9.2 %collective-permute-start.22 = (bf16[64,2048]{1,0:T(8,128)(2,1)S(1)}, bf16[64,2048]{1,0:T(8,128)(2,1)S(1)}, u32[]{:S(2)}, u32[]{:S(2)}) collective-permute-start(bf16[64,2048]{1,0:T(8,128)(2,1)S(1)} %slice.75), channel_id=1, source_target_pairs={{0,2},{1,3},{2,0},{3,1},{4,6},{5,7},{6,4},{7,5},{8,10},{9,11},{10,... | collective-permute-start | bytes 786440 | tf_op jit(solution)/shard_map/ppermute | solution.py:502
  138.7 14.1 %collective-permute-start.34 = (bf16[64,2048]{1,0:T(8,128)(2,1)S(1)}, bf16[64,2048]{1,0:T(8,128)(2,1)S(1)}, u32[]{:S(2)}, u32[]{:S(2)}) collective-permute-start(bf16[64,2048]{1,0:T(8,128)(2,1)S(1)} %slice.73), channel_id=1, source_target_pairs={{0,2},{1,3},{2,0},{3,1},{4,6},{5,7},{6,4},{7,5},{8,10},{9,11},{10,... | collective-permute-start | bytes 786440 | tf_op jit(solution)/shard_map/ppermute | solution.py:502
  147.2 11.0 %collective-permute-start.23 = (bf16[64,2048]{1,0:T(8,128)(2,1)S(1)}, bf16[64,2048]{1,0:T(8,128)(2,1)S(1)}, u32[]{:S(2)}, u32[]{:S(2)}) collective-permute-start(bf16[64,2048]{1,0:T(8,128)(2,1)S(1)} %fusion.2), channel_id=1, source_target_pairs={{0,12},{4,0},{8,4},{12,8},{1,13},{5,1},{9,5},{13,9},{2,14},{6,2},{... | collective-permute-start | bytes 786440 | tf_op jit(solution)/shard_map/ppermute | solution.py:504
  147.7 10.2 %collective-permute-start.28 = (bf16[64,2048]{1,0:T(8,128)(2,1)S(1)}, bf16[64,2048]{1,0:T(8,128)(2,1)S(1)}, u32[]{:S(2)}, u32[]{:S(2)}) collective-permute-start(bf16[64,2048]{1,0:T(8,128)(2,1)S(1)} %slice.74), channel_id=1, source_target_pairs={{0,2},{1,3},{2,0},{3,1},{4,6},{5,7},{6,4},{7,5},{8,10},{9,11},{10,... | collective-permute-start | bytes 786440 | tf_op jit(solution)/shard_map/ppermute | solution.py:502
  152.8 11.1 %collective-permute-start.35 = (bf16[64,2048]{1,0:T(8,128)(2,1)S(1)}, bf16[64,2048]{1,0:T(8,128)(2,1)S(1)}, u32[]{:S(2)}, u32[]{:S(2)}) collective-permute-start(bf16[64,2048]{1,0:T(8,128)(2,1)S(1)} %fusion), channel_id=1, source_target_pairs={{0,4},{4,8},{8,12},{12,0},{1,5},{5,9},{9,13},{13,1},{2,6},{6,10},{... | collective-permute-start | bytes 786440 | tf_op jit(solution)/shard_map/ppermute | solution.py:504
  158.0 15.3 %collective-permute-start.29 = (bf16[64,2048]{1,0:T(8,128)(2,1)S(1)}, bf16[64,2048]{1,0:T(8,128)(2,1)S(1)}, u32[]{:S(2)}, u32[]{:S(2)}) collective-permute-start(bf16[64,2048]{1,0:T(8,128)(2,1)S(1)} %fusion.1), channel_id=1, source_target_pairs={{0,8},{4,12},{8,0},{12,4},{1,9},{5,13},{9,1},{13,5},{2,10},{6,14},... | collective-permute-start | bytes 786440 | tf_op jit(solution)/shard_map/ppermute | solution.py:504
  (6 other events, 5.9 us)
